TPU v7x, 128 devices: a whole 4x4x4 slice. The times are simulated.
128 devices in a mesh: seq: 8 (over y, x_lo), ch: 16 (over x_hi, z, core).
Axes of the slice: x: 4 (x_hi: 2, x_lo: 2; x = x_hi * 2 + x_lo), y: 4, z: 4, core: 2. Of those that a mesh axis runs over, the one named last changes fastest.
Arguments:
- token_ids: int32 [4096], P('seq'), may hold values from 0 to 511
- embedding: bfloat16 [512, 4096], P(None, 'ch'), may hold values from -6 to 6
- gain_first: bfloat16 [4096], P('ch'), may hold values from 0.5 to 1.5
- gain_second: bfloat16 [4096], P('ch'), may hold values from 0.5 to 1.5
- weights_first: bfloat16 [4096, 3, 4096], P(None, None, 'ch'), may hold values from -0.09375 to 0.09375
- weights_second: bfloat16 [4096, 3, 4096], P(None, None, 'ch'), may hold values from -0.09375 to 0.09375
- short_first: float32 [7, 3, 4096], P(None, None, 'ch'), may hold values from -2.5 to 2.5
- short_second: float32 [7, 3, 4096], P(None, None, 'ch'), may hold values from -2.5 to 2.5
- medium: bfloat16 [128, 4096], P(None, 'ch'), may hold values from -0.5 to 0.5
- residues: float32 [16, 4096], P(None, 'ch'), as said below
- decay_rates: float32 [16, 4096], P(None, 'ch'), as said below
- cotangent: bfloat16 [4096, 4096], P('seq', 'ch'), may hold values from -6 to 6
Outputs:
- output: bfloat16 [4096, 4096], P('seq', 'ch')
- grad_embedding: float32 [512, 4096], P(None, 'ch')
- grad_gain_first: float32 [4096], P('ch')
- grad_gain_second: float32 [4096], P('ch')
- grad_weights_first: float32 [4096, 3, 4096], P('seq', None, 'ch')
- grad_weights_second: float32 [4096, 3, 4096], P('seq', None, 'ch')
Inputs may be any that keep to these rules, and one draw needn't show every extreme that they name: `decay_rates`: positive, at most 0.06 and at least 0.05 / 4096. `residues`: magnitude at most 4 sqrt((0.12 + 1 / 4096) / 16).
All inputs are finite; a program needn't handle non-finite values.
Results may differ from a plain program's by a relative error of at most 0.028.
Values may be sent and summed in bfloat16 or wider, within the bound.
A program may use at most 128 MiB of HBM per device.

v0:
```python
import jax
import jax.numpy as jnp
from jax import lax
from jax.sharding import PartitionSpec as P

epsilon = 1e-06
highest = lax.Precision.HIGHEST


def from_behind(shard, axis, by):
    devices = lax.axis_size(axis)
    pairs = [(i, i + by) for i in range(devices) if 0 <= i + by < devices]
    return lax.ppermute(shard, axis, pairs)


def short_forward(projected, short_filter):
    tap_count = short_filter.shape[0]
    row_count = projected.shape[0]
    earlier = from_behind(projected[row_count - (tap_count - 1) :], "seq", 1)
    widened = jnp.concatenate([earlier, projected], axis=0).astype(jnp.float32)
    running = jnp.zeros(projected.shape, jnp.float32)
    for offset in range(tap_count):
        first_row = tap_count - 1 - offset
        running = running + short_filter[offset] * widened[first_row : first_row + row_count]
    return running


def short_backward(gradient, short_filter):
    tap_count = short_filter.shape[0]
    row_count = gradient.shape[0]
    following = from_behind(gradient[: tap_count - 1], "seq", -1)
    widened = jnp.concatenate([gradient, following], axis=0).astype(jnp.float32)
    running = jnp.zeros(gradient.shape, jnp.float32)
    for offset in range(tap_count):
        running = running + short_filter[offset] * widened[offset : offset + row_count]
    return running


def medium_tables(medium):
    tap_count = medium.shape[0]
    lag_grid = (
        jnp.arange(tap_count, dtype=jnp.int32)[:, None]
        - jnp.arange(tap_count, dtype=jnp.int32)[None, :]
    )
    zero_value = jnp.zeros((), jnp.bfloat16)
    near_part = jnp.where(
        (lag_grid >= 0)[:, :, None],
        jnp.take(medium, jnp.clip(lag_grid, 0, tap_count - 1), axis=0),
        zero_value,
    )
    far_part = jnp.where(
        (lag_grid < 0)[:, :, None],
        jnp.take(medium, jnp.clip(lag_grid + tap_count, 0, tap_count - 1), axis=0),
        zero_value,
    )
    return (near_part, far_part)


def medium_forward(gated, near_part, far_part):
    tap_count = near_part.shape[0]
    row_count, width_local = gated.shape
    earlier = from_behind(gated[row_count - tap_count :], "seq", 1)
    blocks = gated.reshape(row_count // tap_count, tap_count, width_local)
    previous = jnp.concatenate([earlier[None], blocks[:-1]], axis=0)
    result = jnp.einsum("abc,jbc->jac", near_part, blocks, preferred_element_type=jnp.float32)
    result = result + jnp.einsum(
        "abc,jbc->jac", far_part, previous, preferred_element_type=jnp.float32
    )
    return result.reshape(row_count, width_local)


def medium_backward(gradient, near_part, far_part):
    tap_count = near_part.shape[0]
    row_count, width_local = gradient.shape
    following = from_behind(gradient[:tap_count], "seq", -1)
    blocks = gradient.reshape(row_count // tap_count, tap_count, width_local)
    later_blocks = jnp.concatenate([blocks[1:], following[None]], axis=0)
    result = jnp.einsum("abc,jac->jbc", near_part, blocks, preferred_element_type=jnp.float32)
    result = result + jnp.einsum(
        "abc,jac->jbc", far_part, later_blocks, preferred_element_type=jnp.float32
    )
    return result.reshape(row_count, width_local)


def mode_tables(decay_rates, residues, block_rows):
    lag_index = jnp.arange(block_rows + 1, dtype=jnp.float32)
    powers = jnp.exp(-decay_rates[:, None, :] * lag_index[None, :, None])
    response = jnp.sum(residues[:, None, :] * powers[:, :block_rows, :], axis=0)
    lag_grid = (
        jnp.arange(block_rows, dtype=jnp.int32)[:, None]
        - jnp.arange(block_rows, dtype=jnp.int32)[None, :]
    )
    picked = jnp.take(response, jnp.clip(lag_grid, 0, block_rows - 1), axis=0)
    toeplitz = jnp.where((lag_grid >= 0)[:, :, None], picked, jnp.zeros((), jnp.float32))
    closing_weights = powers[:, block_rows - 1 :: -1, :]
    lift_table = residues[:, None, :] * powers[:, 1:, :]
    stride = powers[:, block_rows, :]
    return (toeplitz, closing_weights, lift_table, stride)


def mode_blocks(values, tables):
    toeplitz, closing_weights, lift_table, stride = tables
    block_rows = toeplitz.shape[0]
    row_count, width_local = values.shape
    blocks = values.reshape(row_count // block_rows, block_rows, width_local)
    in_block = jnp.einsum("abc,jbc->jac", toeplitz, blocks, precision=highest)
    closing = jnp.einsum("mbc,jbc->jmc", closing_weights, blocks, precision=highest)
    return (in_block, closing)


def mode_chain(closing, stride, start_state):

    def advance(state, close_term):
        return (stride * state + close_term, state)

    last_state, entering = lax.scan(advance, start_state, closing)
    return (entering, last_state)


def mode_finish(in_block, entering, lift_table):
    added = in_block + jnp.einsum("mac,jmc->jac", lift_table, entering, precision=highest)
    return added.reshape(-1, added.shape[2])


def long_filter(signal, decay_rates, residues, backward):
    group_count = lax.axis_size("seq")
    group_width = signal.shape[1] // group_count
    offset = lax.axis_index("seq") * group_width
    rate_part = lax.dynamic_slice_in_dim(decay_rates, offset, group_width, 1)
    residue_part = lax.dynamic_slice_in_dim(residues, offset, group_width, 1)
    gathered = lax.all_to_all(signal, "seq", split_axis=1, concat_axis=0, tiled=True).astype(
        jnp.float32
    )
    if backward:
        gathered = gathered[::-1]
    tables = mode_tables(rate_part, residue_part, min(64, gathered.shape[0]))
    in_block, closing = mode_blocks(gathered, tables)
    entering, last_state = mode_chain(closing, tables[3], jnp.zeros(rate_part.shape, jnp.float32))
    result = mode_finish(in_block, entering, tables[2])
    if backward:
        result = result[::-1]
    return lax.all_to_all(
        result.astype(jnp.bfloat16), "seq", split_axis=0, concat_axis=1, tiled=True
    ).astype(result.dtype)


def mixer_input(inputs, gain, weights, short_filter):
    whole_rows, whole_gain = (
        lax.all_gather(inputs, "ch", axis=1, tiled=True),
        lax.all_gather(gain, "ch", axis=0, tiled=True),
    )
    as_float = whole_rows.astype(jnp.float32)
    row_scale = lax.rsqrt(jnp.mean(as_float * as_float, axis=1) + epsilon)
    normed = (as_float * row_scale[:, None] * whole_gain.astype(jnp.float32)).astype(jnp.bfloat16)
    features = weights.shape[0]
    width_local = weights.shape[2]
    projected = jnp.dot(
        normed, weights.reshape(features, 3 * width_local), preferred_element_type=jnp.float32
    )
    projected = projected.astype(jnp.bfloat16).reshape(-1, 3, width_local)
    featured = short_forward(projected, short_filter)
    gated = (featured[:, 1, :] * featured[:, 2, :]).astype(jnp.bfloat16)
    return (normed, row_scale, featured, gated)


def weight_grad(normed, flat_grad):
    return lax.psum_scatter(
        lax.dot_general(
            normed, flat_grad, (((0,), (0,)), ((), ())), preferred_element_type=jnp.float32
        ).astype(jnp.bfloat16),
        "seq",
        scatter_dimension=0,
        tiled=True,
    ).astype(jnp.float32)


def project_back(grad_featured, inputs, gain, weights, short_filter, normed, row_scale, grad_above):
    row_count, width_local = inputs.shape
    features = weights.shape[0]
    grad_projected = short_backward(grad_featured, short_filter).astype(jnp.bfloat16)
    flat_grad = grad_projected.reshape(row_count, 3 * width_local)
    partial_sum = lax.dot_general(
        flat_grad,
        weights.reshape(features, 3 * width_local),
        (((1,), (1,)), ((), ())),
        preferred_element_type=jnp.float32,
    )
    grad_normed = lax.psum_scatter(
        partial_sum.astype(jnp.bfloat16), "ch", scatter_dimension=1, tiled=True
    ).astype(jnp.float32)
    as_float = inputs.astype(jnp.float32)
    scaled = grad_normed * gain.astype(jnp.float32)
    row_terms = lax.psum(jnp.sum(scaled * as_float, axis=1), "ch")
    grad_inputs = (
        grad_above
        + row_scale[:, None] * scaled
        - as_float * (row_scale**3)[:, None] * row_terms[:, None] / features
    )
    grad_gain = jnp.sum(grad_normed * as_float * row_scale[:, None], axis=0)
    grad_weights = weight_grad(normed, flat_grad).reshape(-1, 3, width_local)
    return (grad_inputs.astype(jnp.bfloat16), grad_gain, grad_weights)


def per_device(
    token_ids,
    embedding,
    gain_first,
    gain_second,
    weights_first,
    weights_second,
    short_first,
    short_second,
    medium,
    residues,
    decay_rates,
    cotangent,
):
    vocab_size = embedding.shape[0]
    onehot = (token_ids[:, None] == jnp.arange(vocab_size, dtype=jnp.int32)[None, :]).astype(
        jnp.bfloat16
    )
    embedded = jnp.dot(onehot, embedding, preferred_element_type=jnp.float32).astype(jnp.bfloat16)
    normed_first, scale_first, featured_first, gated_first = mixer_input(
        embedded, gain_first, weights_first, short_first
    )
    near_part, far_part = medium_tables(medium)
    filtered_first = medium_forward(gated_first, near_part, far_part)
    middle = (embedded.astype(jnp.float32) + featured_first[:, 0, :] * filtered_first).astype(
        jnp.bfloat16
    )
    normed_second, scale_second, featured_second, gated_second = mixer_input(
        middle, gain_second, weights_second, short_second
    )
    filtered_second = long_filter(gated_second, decay_rates, residues, False)
    output = (middle.astype(jnp.float32) + featured_second[:, 0, :] * filtered_second).astype(
        jnp.bfloat16
    )
    above_second = cotangent.astype(jnp.float32)
    grad_filtered = (above_second * featured_second[:, 0, :]).astype(jnp.bfloat16)
    grad_gated = long_filter(grad_filtered, decay_rates, residues, True)
    grad_featured = jnp.stack(
        [
            above_second * filtered_second,
            grad_gated * featured_second[:, 2, :],
            grad_gated * featured_second[:, 1, :],
        ],
        axis=1,
    ).astype(jnp.bfloat16)
    grad_middle, gain_grad_second, weight_grad_second = project_back(
        grad_featured,
        middle,
        gain_second,
        weights_second,
        short_second,
        normed_second,
        scale_second,
        above_second,
    )
    above_first = grad_middle.astype(jnp.float32)
    grad_filtered = (above_first * featured_first[:, 0, :]).astype(jnp.bfloat16)
    grad_gated = medium_backward(grad_filtered, near_part, far_part)
    grad_featured = jnp.stack(
        [
            above_first * filtered_first,
            grad_gated * featured_first[:, 2, :],
            grad_gated * featured_first[:, 1, :],
        ],
        axis=1,
    ).astype(jnp.bfloat16)
    grad_embedded, gain_grad_first, weight_grad_first = project_back(
        grad_featured,
        embedded,
        gain_first,
        weights_first,
        short_first,
        normed_first,
        scale_first,
        above_first,
    )
    embed_part = lax.dot_general(
        onehot, grad_embedded, (((0,), (0,)), ((), ())), preferred_element_type=jnp.float32
    )
    gain_total_first, gain_total_second, embed_total = (
        lax.psum(gain_grad_first.astype(jnp.bfloat16), "seq").astype(jnp.float32),
        lax.psum(gain_grad_second.astype(jnp.bfloat16), "seq").astype(jnp.float32),
        lax.psum(embed_part.astype(jnp.bfloat16), "seq").astype(jnp.float32),
    )
    return (
        output,
        embed_total,
        gain_total_first,
        gain_total_second,
        weight_grad_first,
        weight_grad_second,
    )


def solution(mesh):
    placed = (
        P("seq"),
        P(None, "ch"),
        P("ch"),
        P("ch"),
        P(None, None, "ch"),
        P(None, None, "ch"),
        P(None, None, "ch"),
        P(None, None, "ch"),
        P(None, "ch"),
        P(None, "ch"),
        P(None, "ch"),
        P("seq", "ch"),
    )
    return jax.shard_map(
        per_device,
        mesh=mesh,
        in_specs=placed,
        out_specs=(
            P("seq", "ch"),
            P(None, "ch"),
            P("ch"),
            P("ch"),
            P("seq", None, "ch"),
            P("seq", None, "ch"),
        ),
        check_vma=False,
    )
```

profile of v0, /device:TPU:1, one launch (start us, length us, event | category | flops | bytes accessed | tf_op | source)
XLA Modules:
  0.0 1239.2 jit_solution(2467422524469405294)
XLA Ops:
  10.6 26.8 %all-gather = bf16[16,1,256]{2,1,0:T(2,128)(2,1)S(1)} all-gather(bf16[1,1,256]{2,1,0:T(2,128)(2,1)S(1)} %reshape.242), channel_id=1, replica_groups=mesh['seq'=8,'ch'=16] {'ch'}, dimensions={0}, use_global_device_ids=true | all-gather | bytes 8704 | tf_op jit(solution)/shard_map/all_gather | solution.py:150
  37.4 8.7 copy.197
  46.3 24.2 %all-gather.5.cloned.1.call-done = bf16[512,4096]{1,0:T(8,128)(2,1)} async-done(((bf16[512,256]{1,0:T(8,128)(2,1)}), bf16[512,4096]{1,0:T(8,128)(2,1)}) %all-gather.5.cloned.1.call-update) | async-done | bytes 4194320 | tf_op jit(solution)/shard_map/all_gather | solution.py:149
  70.5 3.2 fusion
  74.3 6.2 convolution_convert_fusion.3
  82.9 65.3 %gather_fusion = bf16[16384,256]{1,0:T(8,128)(2,1)} fusion(bf16[128,256]{1,0:T(8,128)(2,1)S(1)} %copy-done.2, s32[16384]{0:T(1024)S(1)} %bitcast_clamp_fusion.1), kind=kCustom, calls=%fused_computation.clone | custom fusion | bytes 16842752 | tf_op jit(solution)/shard_map/jit(_take)/gather | solution.py:48
  148.2 12.4 %copy.200 = bf16[128,128,256]{1,0,2:T(8,128)(2,1)} copy(bf16[128,128,256]{2,1,0:T(8,128)(2,1)} %bitcast.158) | data formatting | bytes 16777216 | tf_op jit(solution)/shard_map/jit(_take)/gather | solution.py:48
  160.6 65.2 %gather_fusion.1 = bf16[16384,256]{1,0:T(8,128)(2,1)} fusion(bf16[128,256]{1,0:T(8,128)(2,1)S(1)} %copy-done.2, s32[16384]{0:T(1024)S(1)} %bitcast_clamp_fusion), kind=kCustom, calls=%fused_computation.2.clone | custom fusion | bytes 16842752 | tf_op jit(solution)/shard_map/jit(_take)/gather | solution.py:53
  225.7 12.4 %copy.204 = bf16[128,128,256]{1,0,2:T(8,128)(2,1)} copy(bf16[128,128,256]{2,1,0:T(8,128)(2,1)} %bitcast.159) | data formatting | bytes 16777216 | tf_op jit(solution)/shard_map/jit(_take)/gather | solution.py:53
  240.4 4.2 collective-permute-start.1
  244.7 7.8 fusion.7
  252.8 7.8 fusion.48
  261.8 20.4 %all-gather.1 = bf16[16,1,256]{2,1,0:T(2,128)(2,1)S(1)} all-gather(bf16[1,1,256]{2,1,0:T(2,128)(2,1)S(1)} %reshape.244), channel_id=1, replica_groups=mesh['seq'=8,'ch'=16] {'ch'}, dimensions={0}, use_global_device_ids=true | all-gather | bytes 8704 | tf_op jit(solution)/shard_map/all_gather | solution.py:150
  282.8 8.7 copy.206
  293.3 23.1 %all-gather.7.cloned.1.call-done = bf16[512,4096]{1,0:T(8,128)(2,1)} async-done(((bf16[512,256]{1,0:T(8,128)(2,1)}), bf16[512,4096]{1,0:T(8,128)(2,1)}) %all-gather.7.cloned.1.call-update) | async-done | bytes 4194320 | tf_op jit(solution)/shard_map/all_gather | solution.py:149
  316.4 3.2 fusion.3
  320.2 6.3 convolution_convert_fusion.2
  330.1 14.2 %gather_fusion.2 = f32[4096,32]{1,0:T(8,128)} fusion(f32[64,32]{1,0:T(8,128)S(1)} %copy.211, s32[4096]{0:T(1024)S(1)} %broadcast_clamp_fusion), kind=kCustom, calls=%fused_computation.1.clone | custom fusion | bytes 1064960 | tf_op jit(solution)/shard_map/jit(_take)/gather | solution.py:93
  357.7 5.5 all-to-all-start.2
  363.5 6.1 all-to-all-done.2
  371.4 15.5 %rev.11 = f32[4096,32]{0,1:T(8,128)} reverse(f32[4096,32]{0,1:T(8,128)} %bitcast.175), dimensions={0} | reverse | bytes 1048576 | tf_op jit(solution)/shard_map/rev | solution.py:135
  389.4 3.7 convolution_bitcast_fusion.1
  396.0 83.5 %while.27 = (s32[]{:T(128)}, f32[16,32]{1,0:T(8,128)S(1)}, f32[64,16,32]{2,1,0:T(8,128)}, f32[16,32]{1,0:T(8,128)S(1)}, f32[64,16,32]{2,1,0:T(8,128)}, /*index=5*/s32[]{:T(128)}, s32[]{:T(128)}) while((s32[]{:T(128)}, f32[16,32]{1,0:T(8,128)S(1)}, f32[64,16,32]{2,1,0:T(8,128)}, f32[16,32]{1,0:T(8,128)S(1)}, ...), condition=%wide.region_6.9_spmd.clone, body=%wide.region_5.8_spmd.clone.sunk | while | flops 2051 | bytes 19036 | solution.py:116
  481.5 2.9 fusion.102
  484.4 2.7 fusion.44
  489.3 15.3 %rev.12 = bf16[4096,32]{0,1:T(8,128)(2,1)} reverse(bf16[4096,32]{0,1:T(8,128)(2,1)} %reshape.196), dimensions={0} | reverse | bytes 524288 | tf_op jit(solution)/shard_map/rev | solution.py:141
  505.5 8.7 all_to_all.49
  521.3 4.1 all-to-all-start
  525.6 5.9 all-to-all-done
  540.9 83.5 %while.26 = (s32[]{:T(128)}, f32[16,32]{1,0:T(8,128)S(1)}, f32[64,16,32]{2,1,0:T(8,128)}, f32[16,32]{1,0:T(8,128)S(1)}, f32[64,16,32]{2,1,0:T(8,128)}, /*index=5*/s32[]{:T(128)}, s32[]{:T(128)}) while((s32[]{:T(128)}, f32[16,32]{1,0:T(8,128)S(1)}, f32[64,16,32]{2,1,0:T(8,128)}, f32[16,32]{1,0:T(8,128)S(1)}, ...), condition=%wide.region_4.7_spmd.clone, body=%wide.region_3.6_spmd.clone.sunk | while | flops 2051 | bytes 19036 | solution.py:116
  626.4 2.8 fusion.104
  632.6 8.7 all_to_all.50
  647.7 3.1 collective-permute-done.3
  652.6 5.1 bitcast_convert_fusion.1
  658.3 80.5 %reduce-scatter.5.cloned.1.call-done = bf16[512,256]{1,0:T(8,128)(2,1)} async-done(((bf16[512,4096]{1,0:T(8,128)(2,1)}), bf16[512,256]{1,0:T(8,128)(2,1)}) %reduce-scatter.5.cloned.1.call-update) | async-done | bytes 262160 | tf_op jit(solution)/shard_map/reduce_scatter | solution.py:188
  740.0 34.7 %psum.35 = f32[512]{0:T(512)S(1)} all-reduce(f32[512]{0:T(512)S(1)} %get-tuple-element.177), channel_id=1, replica_groups=mesh['seq'=8,'ch'=16] {'ch'}, use_global_device_ids=true, to_apply=%region_9.12 | all-reduce | flops 512 | bytes 4096 | tf_op jit(solution)/shard_map/psum | solution.py:193
  778.8 6.5 fusion.6
  785.6 6.5 fusion.50
  795.1 3.8 collective-permute-done.5
  800.6 5.1 bitcast_convert_fusion
  806.4 8.7 convolution_convert_fusion
  816.0 70.9 %reduce-scatter.7.cloned.1.call-done = bf16[512,256]{1,0:T(8,128)(2,1)} async-done(((bf16[512,4096]{1,0:T(8,128)(2,1)}), bf16[512,256]{1,0:T(8,128)(2,1)}) %reduce-scatter.7.cloned.1.call-update) | async-done | bytes 262160 | tf_op jit(solution)/shard_map/reduce_scatter | solution.py:188
  888.2 36.1 %psum.36 = f32[512]{0:T(512)S(1)} all-reduce(f32[512]{0:T(512)S(1)} %get-tuple-element.179), channel_id=1, replica_groups=mesh['seq'=8,'ch'=16] {'ch'}, use_global_device_ids=true, to_apply=%region_12.15 | all-reduce | flops 512 | bytes 4096 | tf_op jit(solution)/shard_map/psum | solution.py:193
  926.7 8.8 convolution_convert_fusion.1
  935.5 83.9 %reduce-scatter.11.cloned.1.call-done = bf16[512,768]{1,0:T(8,128)(2,1)} async-done(((bf16[4096,768]{1,0:T(8,128)(2,1)}), bf16[512,768]{1,0:T(8,128)(2,1)}) %reduce-scatter.11.cloned.1.call-update) | async-done | bytes 786448 | tf_op jit(solution)/shard_map/reduce_scatter | solution.py:167
  1022.5 14.5 %all-reduce = (bf16[256]{0:T(256)(128)(2,1)S(1)}, bf16[256]{0:T(256)(128)(2,1)S(1)}) all-reduce(bf16[256]{0:T(256)(128)(2,1)S(1)} %get-tuple-element.178, bf16[256]{0:T(256)(128)(2,1)S(1)} %get-tuple-element.176), channel_id=1, replica_groups=mesh['seq'=8,'ch'=16] {'seq'}, use_global_device_ids=true, to_apply=%region_15.18 | all-reduce | flops 512 | bytes 2048 | tf_op jit(solution)/shard_map/psum | solution.py:284
  1038.1 54.1 %all-reduce.3.cloned.1.call-done = bf16[512,256]{1,0:T(8,128)(2,1)} async-done(((bf16[512,256]{1,0:T(8,128)(2,1)}), bf16[512,256]{1,0:T(8,128)(2,1)}) %all-reduce.3.cloned.1.call-update) | async-done | bytes 262160 | tf_op jit(solution)/shard_map/psum | solution.py:286
  1094.0 134.8 %reduce-scatter.9.cloned.1.call-done = bf16[512,768]{1,0:T(8,128)(2,1)} async-done(((bf16[4096,768]{1,0:T(8,128)(2,1)}), bf16[512,768]{1,0:T(8,128)(2,1)}) %reduce-scatter.9.cloned.1.call-update) | async-done | bytes 786448 | tf_op jit(solution)/shard_map/reduce_scatter | solution.py:167
  (482 shorter events, 264.6 us)
Async XLA Ops:
  7.2 63.3 %all-gather.5.cloned.1.call-start = ((), (), s32[]{:S(2)}) async-start(), calls=%async_computation.8 | async-start | bytes 4456448 | tf_op jit(solution)/shard_map/all_gather | solution.py:149
  9.9 306.5 %all-gather.7.cloned.1.call-start = ((), (), s32[]{:S(2)}) async-start(), calls=%async_computation.9 | async-start | bytes 4456448 | tf_op jit(solution)/shard_map/all_gather | solution.py:149
  37.4 8.7 copy-start.22
  46.1 198.6 %copy-start.24 = (pred[128,128]{1,0:T(8,128)(4,1)}, pred[128,128]{1,0:T(8,128)(4,1)S(1)}, u32[]{:S(2)}) copy-start(pred[128,128]{1,0:T(8,128)(4,1)S(1)} %get-tuple-element.241) | copy-start | bytes 49156
  70.5 3.8 copy-start.7
  74.3 6.3 copy-start.33
  80.6 158.1 %collective-permute-start = (bf16[6,3,256]{2,0,1:T(8,128)(2,1)S(1)}, bf16[6,3,256]{2,0,1:T(8,128)(2,1)S(1)}, u32[]{:S(2)}, u32[]{:S(2)}) collective-permute-start(bf16[6,3,256]{2,0,1:T(8,128)(2,1)S(1)} %bitcast.197), channel_id=1, source_target_pairs={{0,16},{16,32},{32,48},{48,64},{64,80},{80,96},{96,112},{1,17},{17... | collective-permute-start | bytes 27656 | tf_op jit(solution)/shard_map/ppermute | solution.py:13
  82.9 170.0 %copy-start.26 = (pred[128,128]{1,0:T(8,128)(4,1)}, pred[128,128]{1,0:T(8,128)(4,1)S(1)}, u32[]{:S(2)}) copy-start(pred[128,128]{1,0:T(8,128)(4,1)S(1)} %get-tuple-element.242) | copy-start | bytes 49156
  82.9 170.0 %copy-start.28 = (pred[128,128]{1,0:T(8,128)(4,1)}, pred[128,128]{1,0:T(8,128)(4,1)S(1)}, u32[]{:S(2)}) copy-start(pred[128,128]{1,0:T(8,128)(4,1)S(1)} %get-tuple-element.243) | copy-start | bytes 49156
  240.4 12.3 collective-permute-start.1
  252.8 8.1 copy-start.13
  282.8 8.8 copy-start.36
  282.8 8.8 copy-start.37
  282.8 8.8 copy-start.23
  292.4 27.3 %copy-start.9 = (f32[16,65,32]{1,2,0:T(8,128)}, f32[16,65,32]{1,2,0:T(8,128)S(1)}, u32[]{:S(2)}) copy-start(f32[16,65,32]{1,2,0:T(8,128)S(1)} %multiply_exponential_fusion) | copy-start | bytes 399364
  292.4 27.9 %copy-start.30 = (f32[16,1,256]{2,1,0:T(1,128)S(1)}, f32[16,1,256]{2,1,0:T(1,128)}, u32[]{:S(2)}) copy-start(f32[16,1,256]{2,1,0:T(1,128)} %convert_element_type.251) | copy-start | bytes 49156
  316.4 3.8 copy-start.8
  320.2 8.9 copy-start.32
  326.5 17.8 %copy-start.21 = (bf16[512,768]{1,0:T(8,128)(2,1)}, bf16[512,768]{1,0:T(8,128)(2,1)S(1)}, u32[]{:S(2)}) copy-start(bf16[512,768]{1,0:T(8,128)(2,1)S(1)} %convolution_convert_fusion.2) | copy-start | bytes 2359300
  326.5 24.9 %collective-permute-start.2 = (bf16[6,3,256]{2,0,1:T(8,128)(2,1)S(1)}, bf16[6,3,256]{2,0,1:T(8,128)(2,1)S(1)}, u32[]{:S(2)}, u32[]{:S(2)}) collective-permute-start(bf16[6,3,256]{2,0,1:T(8,128)(2,1)S(1)} %bitcast.196), channel_id=1, source_target_pairs={{0,16},{16,32},{32,48},{48,64},{64,80},{80,96},{96,112},{1,17},{17... | collective-permute-start | bytes 27656 | tf_op jit(solution)/shard_map/ppermute | solution.py:13
  355.2 8.1 copy-start.10
  357.7 11.9 all-to-all-start.2
  370.6 18.8 %copy-start.15 = (f32[16,64,32]{1,2,0:T(8,128)S(1)}, f32[16,64,32]{1,2,0:T(8,128)}, u32[]{:S(2)}) copy-start(f32[16,64,32]{1,2,0:T(8,128)} %rev.10) | copy-start | bytes 393220
  521.3 10.2 all-to-all-start
  525.3 213.4 %reduce-scatter.5.cloned.1.call-start = ((), (), s32[]{:S(2)}) async-start(), calls=%async_computation.10 | async-start | bytes 4456448 | tf_op jit(solution)/shard_map/reduce_scatter | solution.py:188
  538.0 88.4 %copy-start.16 = (f32[16,64,32]{1,2,0:T(8,128)S(1)}, f32[16,64,32]{1,2,0:T(8,128)}, u32[]{:S(2)}) copy-start(f32[16,64,32]{1,2,0:T(8,128)} %get-tuple-element.212) | copy-start | bytes 393220
  632.5 11.7 copy-start.5
  632.5 11.7 copy-start.18
  642.1 4.3 copy-start.11
  642.1 4.3 copy-start.12
  644.2 8.1 slice-start
  646.4 4.4 collective-permute-start.3
  657.6 117.1 %copy-start.35 = (f32[512]{0:T(512)S(1)}, f32[512]{0:T(512)}, u32[]{:S(2)}) copy-start(f32[512]{0:T(512)} %get-tuple-element.230) | copy-start | bytes 6148
  657.7 229.2 %reduce-scatter.7.cloned.1.call-start = ((), (), s32[]{:S(2)}) async-start(), calls=%async_computation.11 | async-start | bytes 4456448 | tf_op jit(solution)/shard_map/reduce_scatter | solution.py:188
  774.8 4.0 copy-start.25
  777.1 8.5 copy-start.27
  777.1 8.5 copy-start.29
  777.1 8.3 collective-permute-start.4
  793.4 6.9 slice-start.2
  793.5 5.3 collective-permute-start.5
  805.7 213.7 %reduce-scatter.11.cloned.1.call-start = ((), (), s32[]{:S(2)}) async-start(), calls=%async_computation.14 | async-start | bytes 7077888 | tf_op jit(solution)/shard_map/reduce_scatter | solution.py:167
  815.1 71.9 %copy-start.34 = (f32[512]{0:T(512)S(1)}, f32[512]{0:T(512)}, u32[]{:S(2)}) copy-start(f32[512]{0:T(512)} %copy-done.33) | copy-start | bytes 6148
  815.1 71.8 %copy-start.14 = (bf16[512,256]{1,0:T(8,128)(2,1)S(1)}, bf16[512,256]{1,0:T(8,128)(2,1)}, u32[]{:S(2)}) copy-start(bf16[512,256]{1,0:T(8,128)(2,1)} %convolution_convert_fusion.5) | copy-start | bytes 786436
  815.1 109.1 %copy-start.20 = (bf16[512,256]{1,0:T(8,128)(2,1)S(1)}, bf16[512,256]{1,0:T(8,128)(2,1)}, u32[]{:S(2)}) copy-start(bf16[512,256]{1,0:T(8,128)(2,1)} %copy-done.19) | copy-start | bytes 786436
  815.1 109.1 %copy-start.38 = (f32[512]{0:T(512)S(1)}, f32[512]{0:T(512)}, u32[]{:S(2)}) copy-start(f32[512]{0:T(512)} %get-tuple-element.228) | copy-start | bytes 6148
  815.1 109.1 %copy-start.39 = (s32[512]{0:T(512)S(1)}, s32[512]{0:T(512)}, u32[]{:S(2)}) copy-start(s32[512]{0:T(512)} %param.20) | copy-start | bytes 6148
  815.1 277.1 %all-reduce.3.cloned.1.call-start = ((), (), s32[]{:S(2)}) async-start(), calls=%async_computation.12 | async-start | bytes 524288 | tf_op jit(solution)/shard_map/psum | solution.py:286
  926.7 302.2 %reduce-scatter.9.cloned.1.call-start = ((), (), s32[]{:S(2)}) async-start(), calls=%async_computation.13 | async-start | bytes 7077888 | tf_op jit(solution)/shard_map/reduce_scatter | solution.py:167
  (14 other events, 22.7 us)
Sparse Core Ops, SparseCore 0:
  10.3 60.1 all-gather.4
  261.9 54.4 all-gather.6
  657.8 80.9 reduce-scatter.4
  805.8 81.0 reduce-scatter.6
  889.2 130.2 reduce-scatter.10
  1022.3 69.8 all-reduce.2
  1094.6 134.1 reduce-scatter.8
where the time goes:
time: 1260 us; the launch traced here: 1240 us
  waiting for transfers between devices  491 us (39%)
  local copies, waits for them, and re-layouts  271 us (22%)
  other arithmetic  199 us (16%)
  blocking collectives  150 us (12%)
  matrix products  89.6 us (7%)
  starting transfers between devices  23.5 us (2%)
  between operations  15.4 us (1%)
    reduce_scatter x2, waiting for transfers between devices, weight_grad(): lax.psum_scatter(lax.dot_general(normed, flat_grad, (((0,), (0,)), ((), (...  219 us
    reduce_scatter x2, waiting for transfers between devices, project_back(): lax.psum_scatter(partial_sum.astype(jnp.bfloat16), 'ch', scatter_dimensio...  151 us
    add x128, other arithmetic, advance(): return (stride * state + close_term, state)  89.8 us
    gather x2, local copies, waits for them, and re-layouts, medium_tables(): jnp.take(medium, jnp.clip(lag_grid, 0, tap_count - 1), axis=0)  77.7 us
    gather x2, local copies, waits for them, and re-layouts, medium_tables(): jnp.take(medium, jnp.clip(lag_grid + tap_count, 0, tap_count - 1), axis=0)  77.6 us
    dynamic_update_slice x128, other arithmetic, mode_chain(): last_state, entering = lax.scan(advance, start_state, closing)  77.1 us
    psum x2, blocking collectives, project_back(): row_terms = lax.psum(jnp.sum(scaled * as_float, axis=1), 'ch')  70.8 us
    psum x1, waiting for transfers between devices, per_device(): lax.psum(embed_part.astype(jnp.bfloat16), 'seq').astype(jnp.float32)  54.1 us
  transfers between devices with their start and end apart: 15, of which 11 were waited for; matrix products, arithmetic and copies ran while one was open for 19% of the time, Pallas kernels for 0%

commit v1 on v0

v1 whole, which is shorter than its diff:
```python
import functools

import jax
import jax.numpy as jnp
from jax import lax
from jax.experimental import pallas as pl
from jax.experimental.pallas import tpu as pltpu
from jax.sharding import PartitionSpec as P

epsilon = 1e-06
MESH = pl.DeviceIdType.MESH
f32 = jnp.float32
bf16 = jnp.bfloat16
LANES = 128
SUB = 8
HALO = 144
LEAD = 8


class Item:
    def __init__(self, array, axis, window=None, reduce=False):
        self.array, self.axis, self.window, self.reduce = array, axis, window, reduce

    def block(self):
        shape = list(self.array.shape)
        if self.window is not None:
            shape[self.window] //= lax.axis_size(self.axis)
        return tuple(shape)


def exchange(cid, items):
    count = len(items)
    sizes = [lax.axis_size(it.axis) for it in items]
    blocks = [it.block() for it in items]
    axes = []
    for it in items:
        if it.axis not in axes:
            axes.append(it.axis)
    most = max(sizes)
    reduced = [k for k in range(count) if items[k].reduce]

    def body(*refs):
        srcs, outs = refs[:count], refs[count : 2 * count]
        bufs = list(outs)
        rest = refs[2 * count :]
        for slot, k in enumerate(reduced):
            bufs[k] = rest[slot]
        send_sem, recv_sem, own_sem = rest[len(reduced) :]

        def part(k, peer):
            if items[k].window is None:
                return srcs[k]
            width = blocks[k][items[k].window]
            start = pl.multiple_of(peer * width, width)
            index = [slice(None)] * len(blocks[k])
            index[items[k].window] = pl.ds(start, width)
            return srcs[k].at[tuple(index)]

        barrier = pltpu.get_barrier_semaphore()
        total = 0
        for axis in axes:
            n = lax.axis_size(axis)
            total += n - 1
            me = lax.axis_index(axis)

            def greet(step, carry, axis=axis, n=n, me=me):
                peer = lax.rem(me + step, n)
                pl.semaphore_signal(barrier, inc=1, device_id={axis: peer}, device_id_type=MESH)
                return carry

            lax.fori_loop(1, n, greet, 0)
        pl.semaphore_wait(barrier, total)

        def copy(k, peer, slot):
            me = lax.axis_index(items[k].axis)
            return pltpu.make_async_remote_copy(
                src_ref=part(k, peer),
                dst_ref=bufs[k].at[me],
                send_sem=send_sem.at[k, slot],
                recv_sem=recv_sem.at[k, me],
                device_id={items[k].axis: peer},
                device_id_type=MESH,
            )

        for k in range(count):
            n = sizes[k]
            me = lax.axis_index(items[k].axis)

            def push(step, carry, k=k, n=n, me=me):
                copy(k, lax.rem(me + step, n), step).start()
                return carry

            lax.fori_loop(1, n, push, 0)
        for k in range(count):
            me = lax.axis_index(items[k].axis)
            pltpu.make_async_copy(part(k, me), bufs[k].at[me], own_sem.at[k]).start()
        for k in range(count):
            n = sizes[k]
            me = lax.axis_index(items[k].axis)
            pltpu.make_async_copy(part(k, me), bufs[k].at[me], own_sem.at[k]).wait()

            def finish(step, carry, k=k, n=n, me=me):
                peer = lax.rem(me + step, n)
                copy(k, peer, step).wait_send()
                pltpu.make_async_remote_copy(
                    src_ref=part(k, peer),
                    dst_ref=bufs[k].at[peer],
                    send_sem=send_sem.at[k, step],
                    recv_sem=recv_sem.at[k, peer],
                    device_id={items[k].axis: peer},
                    device_id_type=MESH,
                ).wait_recv()
                return carry

            lax.fori_loop(1, n, finish, 0)
            if items[k].reduce:
                running = bufs[k][0].astype(f32)
                for j in range(1, n):
                    running = running + bufs[k][j].astype(f32)
                outs[k][...] = running

    shapes = []
    scratch = []
    for k in range(count):
        full = (sizes[k],) + blocks[k]
        if items[k].reduce:
            shapes.append(jax.ShapeDtypeStruct(blocks[k], f32))
            scratch.append(pltpu.VMEM(full, items[k].array.dtype))
        else:
            shapes.append(jax.ShapeDtypeStruct(full, items[k].array.dtype))
    scratch += [
        pltpu.SemaphoreType.DMA((count, most)),
        pltpu.SemaphoreType.DMA((count, most)),
        pltpu.SemaphoreType.DMA((count,)),
    ]
    vmem = pl.BlockSpec(memory_space=pltpu.VMEM)
    return pl.pallas_call(
        body,
        out_shape=shapes,
        in_specs=[vmem] * count,
        out_specs=[vmem] * count,
        scratch_shapes=scratch,
        compiler_params=pltpu.CompilerParams(collective_id=cid, has_side_effects=True),
        name=f"exchange_{cid}",
    )(*[it.array for it in items])


def lag_sum(x, taps):
    tap_count, width = taps.shape
    rows = x.shape[0] - tap_count
    length = rows // SUB
    span = length + tap_count - 1
    group = 11
    tap_group = 8

    def body(x_ref, taps_ref, y_ref, spread, wide):
        for lane in range(width // LANES):
            lanes = slice(lane * LANES, (lane + 1) * LANES)

            def arrange(q, carry):
                spread[q] = x_ref[lane, pl.ds(q, SUB, stride=length), :]
                return carry

            lax.fori_loop(0, span, arrange, 0)

            def widen(k, carry):
                eight = taps_ref[pl.ds(pl.multiple_of(k * SUB, SUB), SUB), lanes]
                for i in range(SUB):
                    wide[k * SUB + i] = jnp.broadcast_to(eight[i : i + 1], (SUB, LANES))
                return carry

            lax.fori_loop(0, tap_count // SUB, widen, 0)

            def block(b, carry):
                first = b * group

                def add(kb, sums):
                    base = first + (tap_count - tap_group) - kb * tap_group
                    window = [spread[base + w] for w in range(group + tap_group - 1)]
                    out = list(sums)
                    for kk in range(tap_group):
                        tap = wide[kb * tap_group + kk]
                        for r in range(group):
                            out[r] = out[r] + tap * window[r + tap_group - 1 - kk]
                    return tuple(out)

                zero = tuple(jnp.zeros((SUB, LANES), f32) for _ in range(group))
                sums = lax.fori_loop(0, tap_count // tap_group, add, zero)
                for r in range(group):
                    y_ref[lane, pl.ds(first + r, SUB, stride=length), :] = sums[r]
                return carry

            lax.fori_loop(0, length // group, block, 0)

    vmem = pl.BlockSpec(memory_space=pltpu.VMEM)
    lanes_first = jnp.stack([x[:, i : i + LANES] for i in range(0, width, LANES)], axis=0)
    y = pl.pallas_call(
        body,
        out_shape=jax.ShapeDtypeStruct((width // LANES, rows, LANES), f32),
        in_specs=[vmem, vmem],
        out_specs=vmem,
        scratch_shapes=[
            pltpu.VMEM((span, SUB, LANES), f32),
            pltpu.VMEM((tap_count, SUB, LANES), f32),
        ],
        name="lag_sum",
    )(lanes_first, taps)
    return jnp.concatenate([y[i] for i in range(width // LANES)], axis=1)


def split_lanes(x):
    return jnp.stack([x[:, i : i + LANES] for i in range(0, x.shape[1], LANES)], axis=0)


def join_lanes(x):
    return jnp.concatenate([x[i] for i in range(x.shape[0])], axis=1)


def mode_close(ahead, behind, rates):
    groups, rows, _ = ahead.shape
    modes, width = rates.shape
    length = rows // SUB
    unroll = 4

    def body(a_ref, b_ref, rate_ref, chunk_ref, shard_ref):
        order = lax.broadcasted_iota(jnp.int32, (SUB, LANES), 0).astype(f32)
        for way, src in enumerate((a_ref, b_ref)):
            for lane in range(groups):
                lanes = slice(lane * LANES, (lane + 1) * LANES)
                rate = [jnp.broadcast_to(rate_ref[m : m + 1, lanes], (SUB, LANES)) for m in range(modes)]
                decay = [jnp.exp(-r) for r in rate]

                def step(i, states):
                    states = list(states)
                    for u in range(unroll):
                        r = i * unroll + u
                        if way == 1:
                            r = length - 1 - r
                        x = src[lane, pl.ds(r, SUB, stride=length), :]
                        states = [decay[m] * states[m] + x for m in range(modes)]
                    return tuple(states)

                zero = tuple(jnp.zeros((SUB, LANES), f32) for _ in range(modes))
                states = lax.fori_loop(0, length // unroll, step, zero)
                after = (SUB - 1) - order if way == 0 else order
                for m in range(modes):
                    chunk_ref[way, m, :, lanes] = states[m]
                    weighted = states[m] * jnp.exp(-(rate[m] * (after * float(length))))
                    shard_ref[way, m : m + 1, lanes] = jnp.sum(weighted, axis=0, keepdims=True)

    vmem = pl.BlockSpec(memory_space=pltpu.VMEM)
    return pl.pallas_call(
        body,
        out_shape=[
            jax.ShapeDtypeStruct((2, modes, SUB, width), f32),
            jax.ShapeDtypeStruct((2, modes, width), f32),
        ],
        in_specs=[vmem] * 3,
        out_specs=[vmem] * 2,
        name="mode_close",
    )(ahead, behind, rates)


def mode_apply(ahead, behind, rates, residues, chunks, entering):
    groups, rows, _ = ahead.shape
    modes, width = rates.shape
    length = rows // SUB
    unroll = 2

    def body(a_ref, b_ref, rate_ref, res_ref, chunk_ref, enter_ref, ya_ref, yb_ref):
        order = lax.broadcasted_iota(jnp.int32, (SUB, LANES), 0)
        for way, (src, dst) in enumerate(((a_ref, ya_ref), (b_ref, yb_ref))):
            place = order if way == 0 else (SUB - 1) - order
            for lane in range(groups):
                lanes = slice(lane * LANES, (lane + 1) * LANES)
                decay = []
                residue = []
                start = []
                for m in range(modes):
                    rate = jnp.broadcast_to(rate_ref[m : m + 1, lanes], (SUB, LANES))
                    decay.append(jnp.exp(-rate))
                    residue.append(jnp.broadcast_to(res_ref[m : m + 1, lanes], (SUB, LANES)))
                    first = jnp.broadcast_to(enter_ref[way, m : m + 1, lanes], (SUB, LANES))

                    def back(v, by):
                        moved = pltpu.roll(v, by if way == 0 else SUB - by, 0)
                        return moved

                    state = jnp.where(place == 0, first, back(chunk_ref[way, m, :, lanes], 1))
                    for by in (1, 2, 4):
                        factor = jnp.exp(-(rate * float(by * length)))
                        state = state + jnp.where(place >= by, factor * back(state, by), 0.0)
                    start.append(state)

                def step(i, states):
                    states = list(states)
                    for u in range(unroll):
                        r = i * unroll + u
                        if way == 1:
                            r = length - 1 - r
                        x = src[lane, pl.ds(r, SUB, stride=length), :]
                        states = [decay[m] * states[m] + x for m in range(modes)]
                        terms = [residue[m] * states[m] for m in range(modes)]
                        while len(terms) > 1:
                            terms = [a + b for a, b in zip(terms[::2], terms[1::2])]
                        dst[lane, pl.ds(r, SUB, stride=length), :] = terms[0]
                    return tuple(states)

                lax.fori_loop(0, length // unroll, step, tuple(start))

    vmem = pl.BlockSpec(memory_space=pltpu.VMEM)
    return pl.pallas_call(
        body,
        out_shape=[jax.ShapeDtypeStruct(ahead.shape, f32)] * 2,
        in_specs=[vmem] * 6,
        out_specs=[vmem] * 2,
        name="mode_apply",
    )(ahead, behind, rates, residues, chunks, entering)


def shift_axis(shard, axis, by):
    n = lax.axis_size(axis)
    pairs = [(i, i + by) for i in range(n) if 0 <= i + by < n]
    return lax.ppermute(shard, axis, pairs)


def taps_ahead(projected, short_filter, first, rows):
    tap_count = short_filter.shape[0]
    running = None
    for i in range(tap_count):
        term = short_filter[i] * projected[first - i : first - i + rows].astype(f32)
        running = term if running is None else running + term
    return running


def taps_behind(gradient, short_filter, rows):
    running = None
    for i in range(short_filter.shape[0]):
        term = short_filter[i] * gradient[i : i + rows].astype(f32)
        running = term if running is None else running + term
    return running


def normalise(whole, gain):
    as_float = whole.astype(f32)
    scale = lax.rsqrt(jnp.mean(as_float * as_float, axis=1) + epsilon)
    return (as_float * scale[:, None] * gain[None, :].astype(f32)).astype(bf16), scale


def small(vector, lanes=LANES):
    rows = vector.reshape(-1, lanes)
    pad = -rows.shape[0] % SUB
    return jnp.pad(rows, ((0, pad), (0, 0)))


def per_device(
    token_ids,
    embedding,
    gain_first,
    gain_second,
    weights_first,
    weights_second,
    short_first,
    short_second,
    medium,
    residues,
    decay_rates,
    cotangent,
):
    n_seq, n_ch = lax.axis_size("seq"), lax.axis_size("ch")
    seq_at = lax.axis_index("seq")
    rows = token_ids.shape[0]
    vocab, width = embedding.shape
    features = weights_first.shape[0]
    wide = 3 * width
    vocab_part = vocab // n_seq
    flat_first = weights_first.reshape(features, wide)
    flat_second = weights_second.reshape(features, wide)
    taps_first = short_first.reshape(-1, wide)
    taps_second = short_second.reshape(-1, wide)

    shifted = token_ids + 1
    ids = jnp.concatenate(
        [
            shift_axis(shifted[rows - HALO :], "seq", 1),
            shifted,
            shift_axis(shifted[:HALO], "seq", -1),
        ]
    ) - 1

    table_rows = lax.dynamic_slice_in_dim(embedding, seq_at * vocab_part, vocab_part, 0)
    packed = jnp.concatenate(
        [table_rows, gain_first[None], gain_second[None], jnp.zeros((14, width), bf16)], axis=0
    )
    (gathered,) = exchange(0, [Item(packed, "ch")])
    joined = jnp.concatenate([gathered[i] for i in range(n_ch)], axis=1)
    whole_gain_first, whole_gain_second = joined[vocab_part], joined[vocab_part + 1]
    table_normed, table_scale = normalise(joined[:vocab_part], whole_gain_first)
    table_projected = jnp.dot(table_normed, flat_first, preferred_element_type=f32).astype(bf16)
    projected_parts, normed_parts = exchange(
        1, [Item(table_projected, "seq"), Item(table_normed, "seq", window=1)]
    )
    table = jnp.concatenate([projected_parts.reshape(vocab, wide), embedding], axis=1)

    onehot = (ids[:, None] == jnp.arange(vocab, dtype=jnp.int32)[None, :]).astype(bf16)
    looked_up = jnp.dot(onehot, table, preferred_element_type=f32).astype(bf16)
    ahead = HALO - SUB
    featured_first = taps_ahead(looked_up[:, :wide], taps_first, SUB, looked_up.shape[0] - SUB)
    gated_first = (
        (featured_first[:, width : 2 * width] * featured_first[:, 2 * width :]).astype(bf16).astype(f32)
    )
    medium_float = medium.astype(f32)
    tap_count = medium.shape[0]
    out_rows = rows + 2 * LEAD
    begin = ahead - LEAD - (tap_count - 1)
    filtered_first = lag_sum(gated_first[begin : begin + out_rows + tap_count], medium_float)
    near = slice(ahead - LEAD, ahead - LEAD + out_rows)
    embedded = looked_up[HALO - LEAD : HALO - LEAD + out_rows, wide:].astype(f32)
    middle_near = (embedded + featured_first[near, :width] * filtered_first).astype(bf16)
    middle = middle_near[LEAD : LEAD + rows]

    whole_rows = lax.all_gather(middle_near, "ch", axis=1, tiled=True)
    normed_near, scale_near = normalise(whole_rows, whole_gain_second)
    normed_second, scale_second = normed_near[LEAD : LEAD + rows], scale_near[LEAD : LEAD + rows]
    projected_near = jnp.dot(normed_near, flat_second, preferred_element_type=f32).astype(bf16)
    featured_second = taps_ahead(projected_near, taps_second, LEAD, rows)
    pick = [featured_second[:, j * width : (j + 1) * width] for j in range(3)]
    gated_second = (pick[1] * pick[2]).astype(bf16).astype(f32)
    above_second = cotangent.astype(f32)
    grad_filtered = (above_second * pick[0]).astype(bf16).astype(f32)
    gated_lanes, grad_lanes = split_lanes(gated_second), split_lanes(grad_filtered)
    chunks, shard_states = mode_close(gated_lanes, grad_lanes, decay_rates)
    (all_states,) = exchange(2, [Item(shard_states, "seq")])
    other = jnp.arange(n_seq, dtype=jnp.int32)
    gaps = jnp.stack([seq_at - 1 - other, other - 1 - seq_at], axis=1)
    weights_of = jnp.where(
        (gaps >= 0)[:, :, None, None],
        jnp.exp(-decay_rates[None, None] * (jnp.maximum(gaps, 0) * rows).astype(f32)[:, :, None, None]),
        0.0,
    )
    entering = jnp.sum(weights_of * all_states, axis=0)
    filtered_lanes, gated_grad_lanes = mode_apply(
        gated_lanes, grad_lanes, decay_rates, residues, chunks, entering
    )
    filtered_second, grad_gated = join_lanes(filtered_lanes), join_lanes(gated_grad_lanes)
    output = (middle.astype(f32) + pick[0] * filtered_second).astype(bf16)

    grad_featured = jnp.concatenate(
        [above_second * filtered_second, grad_gated * pick[2], grad_gated * pick[1]], axis=1
    ).astype(bf16)
    following = shift_axis(grad_featured[:SUB], "seq", -1)
    grad_projected = taps_behind(
        jnp.concatenate([grad_featured, following], axis=0), taps_second, rows
    ).astype(bf16)
    row_part = jnp.sum(
        grad_projected.astype(f32) * projected_near[LEAD : LEAD + rows].astype(f32), axis=1
    )
    (row_total,) = exchange(3, [Item(small(row_part), "ch", reduce=True)])
    row_total = row_total.reshape(-1)[:rows]
    partial_sum = lax.dot_general(
        grad_projected, flat_second, (((1,), (1,)), ((), ())), preferred_element_type=f32
    ).astype(bf16)
    grad_normed = lax.psum_scatter(partial_sum, "ch", scatter_dimension=1, tiled=True).astype(f32)
    weight_grad_second = lax.psum_scatter(
        lax.dot_general(
            normed_second, grad_projected, (((0,), (0,)), ((), ())), preferred_element_type=f32
        ).astype(bf16),
        "seq",
        scatter_dimension=0,
        tiled=True,
    ).astype(f32)
    middle_float = middle.astype(f32)
    scale = scale_second[:, None]
    grad_middle = (
        above_second
        + scale * grad_normed * gain_second.astype(f32)
        - middle_float * (scale * scale) * row_total[:, None] / features
    ).astype(bf16)
    gain_part_second = jnp.sum(grad_normed * middle_float * scale, axis=0)

    grad_near = jnp.concatenate([grad_middle, shift_axis(grad_middle[:HALO], "seq", -1)], axis=0)
    from_here = slice(ahead, ahead + rows + HALO)
    grad_filtered = (
        (grad_near.astype(f32) * featured_first[from_here, :width]).astype(bf16).astype(f32)
    )
    grad_gated = lag_sum(grad_filtered, medium_float[::-1])[: rows + SUB]
    here = slice(ahead, ahead + rows + SUB)
    grad_featured = jnp.concatenate(
        [
            grad_near[: rows + SUB].astype(f32) * filtered_first[LEAD:],
            grad_gated * featured_first[here, 2 * width :],
            grad_gated * featured_first[here, width : 2 * width],
        ],
        axis=1,
    ).astype(bf16)
    grad_projected = taps_behind(grad_featured, taps_first, rows).astype(bf16)
    by_token = lax.dot_general(
        onehot[HALO : HALO + rows],
        jnp.concatenate([grad_projected, grad_middle], axis=1),
        (((0,), (0,)), ((), ())),
        preferred_element_type=f32,
    ).astype(bf16)
    (token_sums,) = exchange(4, [Item(by_token, "seq", window=0, reduce=True)])
    token_grad = token_sums[:, :wide].astype(bf16)
    token_above = token_sums[:, wide:]
    token_part = jnp.sum(token_grad.astype(f32) * table_projected.astype(f32), axis=1)
    token_partial = lax.dot_general(
        token_grad, flat_first, (((1,), (1,)), ((), ())), preferred_element_type=f32
    ).astype(bf16)
    spread = jnp.broadcast_to(token_part[:, None], (vocab_part, LANES))
    token_normed, token_total, token_grads = exchange(
        5,
        [
            Item(token_partial, "ch", window=1, reduce=True),
            Item(spread, "ch", reduce=True),
            Item(token_grad, "seq"),
        ],
    )
    table_float = table_rows.astype(f32)
    scale = table_scale[:, None]
    grad_table = (
        token_above
        + scale * token_normed * gain_first.astype(f32)
        - table_float * (scale * scale) * token_total[:, :1] / features
    )
    gain_part_first = jnp.sum(token_normed * table_float * scale, axis=0)
    gain_parts = jnp.concatenate(
        [gain_part_first[None], gain_part_second[None], jnp.zeros((6, width), f32)], axis=0
    )
    table_parts, gain_total = exchange(
        6, [Item(grad_table.astype(bf16), "seq"), Item(gain_parts, "seq", reduce=True)]
    )
    weight_grad_first = lax.dot_general(
        normed_parts.reshape(vocab, features // n_seq),
        token_grads.reshape(vocab, wide),
        (((0,), (0,)), ((), ())),
        preferred_element_type=f32,
    )
    return (
        output,
        table_parts.reshape(vocab, width).astype(f32),
        gain_total[0],
        gain_total[1],
        weight_grad_first.reshape(-1, 3, width),
        weight_grad_second.reshape(-1, 3, width),
    )


def solution(mesh):
    placed = (
        P("seq"),
        P(None, "ch"),
        P("ch"),
        P("ch"),
        P(None, None, "ch"),
        P(None, None, "ch"),
        P(None, None, "ch"),
        P(None, None, "ch"),
        P(None, "ch"),
        P(None, "ch"),
        P(None, "ch"),
        P("seq", "ch"),
    )
    return jax.shard_map(
        per_device,
        mesh=mesh,
        in_specs=placed,
        out_specs=(
            P("seq", "ch"),
            P(None, "ch"),
            P("ch"),
            P("ch"),
            P("seq", None, "ch"),
            P("seq", None, "ch"),
        ),
        check_vma=False,
    )
```

time: 1260 us -> 473 us (0.38); the launches traced: 1240 us -> 471 us
  waiting for transfers between devices: 491 us -> 148 us
  local copies, waits for them, and re-layouts: 271 us -> 50.4 us
  Pallas kernels: 0 us -> 185 us
  other arithmetic: 199 us -> 30.9 us
  blocking collectives: 150 us -> 0 us
  matrix products: 89.6 us -> 33.1 us
  starting transfers between devices: 23.5 us -> 9.21 us
    reduce_scatter x4 -> x2, waiting for transfers between devices: 370 us -> 91.6 us  [the longest x1 56.7 us: per_device(): lax.psum_scatter(partial_sum, 'ch', scatter_dimension=1, tiled=True)]
    pallas_call x0 -> x11, Pallas kernels: none -> 185 us  [the longest x7 154 us: exchange(): pl.pallas_call(body, out_shape=shapes, in_specs=[vmem] * count, out_specs...]
    gather x6 -> x0, local copies, waits for them, and re-layouts: 172 us -> none  [the longest x2 77.7 us: medium_tables(): jnp.take(medium, jnp.clip(lag_grid, 0, tap_count - 1), axis=0)]
    add x130 -> x3, other arithmetic: 92.3 us -> 4.19 us  [the longest x2 3.5 us: taps_ahead(): running = term if running is None else running + term]
    psum x3 -> x0, blocking collectives: 85.4 us -> none  [the longest x2 70.8 us: project_back(): row_terms = lax.psum(jnp.sum(scaled * as_float, axis=1), 'ch')]
    dynamic_update_slice x128 -> x0, other arithmetic: 77.1 us -> none  [mode_chain(): last_state, entering = lax.scan(advance, start_state, closing)]
    dot_general x18 -> x8, matrix products: 89.6 us -> 33.1 us  [the longest x1 8.35 us: per_device(): lax.dot_general(normed_second, grad_projected, (((0,), (0,)), ((), ())),...]
    psum x1 -> x0, waiting for transfers between devices: 54.1 us -> none  [per_device(): lax.psum(embed_part.astype(jnp.bfloat16), 'seq').astype(jnp.float32)]
  transfers between devices with their start and end apart: 15 -> 7, of which waited for: 11 -> 5; matrix products, arithmetic and copies ran while one was open for 19% -> 16% of each run, Pallas kernels for 0% -> 33%
where the time goes in v1:
time: 473 us; the launch traced here: 471 us
  Pallas kernels  185 us (39%)
  waiting for transfers between devices  148 us (31%)
  local copies, waits for them, and re-layouts  50.4 us (11%)
  matrix products  33.1 us (7%)
  other arithmetic  30.9 us (7%)
  between operations  14.5 us (3%)
  starting transfers between devices  9.21 us (2%)
    pallas_call x7, Pallas kernels, exchange(): pl.pallas_call(body, out_shape=shapes, in_specs=[vmem] * count, out_specs...  154 us
    reduce_scatter x1, waiting for transfers between devices, per_device(): lax.psum_scatter(partial_sum, 'ch', scatter_dimension=1, tiled=True)  56.7 us
    all_gather x1, waiting for transfers between devices, per_device(): whole_rows = lax.all_gather(middle_near, 'ch', axis=1, tiled=True)  50.5 us
    unnamed x100, local copies, waits for them, and re-layouts  35.4 us
    reduce_scatter x1, waiting for transfers between devices, per_device(): lax.psum_scatter(lax.dot_general(normed_second, grad_projected, (((0,), (...  34.9 us
    pallas_call x2, Pallas kernels, lag_sum(): pl.pallas_call(body, out_shape=jax.ShapeDtypeStruct((width // LANES, rows...  20 us
  transfers between devices with their start and end apart: 7, of which 5 were waited for; matrix products, arithmetic and copies ran while one was open for 16% of the time, Pallas kernels for 33%

profile of v1, /device:TPU:1, one launch (start us, length us, event | category | flops | bytes accessed | tf_op | source)
XLA Modules:
  0.0 470.8 jit_solution(10474004675267765795)
XLA Ops:
  8.0 1.3 collective-permute-start.1
  9.3 4.6 collective-permute-start
  16.7 17.8 %exchange_0.1 = bf16[16,80,256]{2,1,0:T(8,128)(2,1)} custom-call(bf16[80,256]{1,0:T(8,128)(2,1)} %maximum_maximum_fusion.refs_0_), custom_call_target="tpu_custom_call" | custom-call | tf_op jit(solution)/shard_map/exchange_0/pallas_call | solution.py:137
  47.8 8.7 %copy.27 = bf16[4096,3,256]{0,2,1:T(8,128)(2,1)} copy(bf16[4096,3,256]{2,0,1:T(8,128)(2,1)} %param.16) | data formatting | bytes 12582912 | tf_op args[4]
  56.8 5.7 %convolution_convert_fusion.6.refs_0_ = bf16[64,768]{1,0:T(8,128)(2,1)} fusion(bf16[64,4096]{1,0:T(8,128)(2,1)S(1)} %fusion.13.refs_1_, bf16[4096,768]{0,1:T(8,128)(2,1)} %bitcast.98), kind=kOutput, calls=%fused_computation.27 | convolution fusion | flops 402702336 | bytes 6914048 | tf_op jit(solution)/shard_map/dot_general | solution.py:399
  62.4 22.3 %exchange_1.1 = (bf16[8,64,768]{2,1,0:T(8,128)(2,1)}, bf16[8,64,512]{2,1,0:T(8,128)(2,1)}) custom-call(bf16[64,768]{1,0:T(8,128)(2,1)} %convolution_convert_fusion.6.refs_0_, bf16[64,4096]{1,0:T(8,128)(2,1)} %copy-done.4), custom_call_target="tpu_custom_call" | custom-call | tf_op jit(solution)/shard_map/exchange_1/pallas_call | solution.py:137
  85.8 2.2 convolution_convert_fusion.3
  88.0 2.2 multiply_add_fusion
  90.4 1.3 copy-done.1
  92.6 10.0 %lag_sum.2 = f32[2,528,128]{2,1,0:T(8,128)} custom-call(f32[2,656,128]{2,1,0:T(8,128)} %pad_maximum_fusion.3.x_ref, f32[128,256]{1,0:T(8,128)} %convert_element_type.236.taps_ref), custom_call_target="tpu_custom_call" | custom-call | tf_op jit(solution)/shard_map/lag_sum/pallas_call | solution.py:197
  103.7 1.9 fusion.25
  105.8 8.7 %copy.28 = bf16[4096,3,256]{0,2,1:T(8,128)(2,1)} copy(bf16[4096,3,256]{2,0,1:T(8,128)(2,1)} %param.17) | data formatting | bytes 12582912 | tf_op args[5]
  114.9 50.5 %all-gather.2.cloned.1.call-done = bf16[528,4096]{1,0:T(8,128)(2,1)} async-done(((bf16[528,256]{1,0:T(8,128)(2,1)}), bf16[528,4096]{1,0:T(8,128)(2,1)}) %all-gather.2.cloned.1.call-update) | async-done | bytes 4325392 | tf_op jit(solution)/shard_map/all_gather | solution.py:422
  165.4 3.3 fusion
  169.0 1.6 fusion.2
  170.6 1.6 copy-done.3
  172.2 3.6 convolution_convert_fusion.5
  175.8 1.3 fusion.9
  179.1 4.0 mode_close.1
  183.1 8.9 %exchange_2.1 = f32[8,2,16,256]{3,2,1,0:T(8,128)} custom-call(f32[2,16,256]{2,1,0:T(8,128)} %get-tuple-element.19.refs_0_), custom_call_target="tpu_custom_call" | custom-call | tf_op jit(solution)/shard_map/exchange_2/pallas_call | solution.py:137
  191.9 1.7 multiply_reduce_fusion.enter_ref
  193.6 6.6 %mode_apply.1 = (f32[2,512,128]{2,1,0:T(8,128)}, f32[2,512,128]{2,1,0:T(8,128)}) custom-call(f32[2,512,128]{2,1,0:T(8,128)} %pad_maximum_fusion.7.a_ref, f32[2,512,128]{2,1,0:T(8,128)} %pad_maximum_fusion.8.b_ref, f32[16,256]{1,0:T(8,128)} %rate_ref.3, f32[16,256]{1,0:T(8,128)} %res_ref.1, f32[2,16,8,256]{3,2,1,0:T(8,128)} %get-tuple-element.18.chunk_ref, ...), custom_call_target="tpu_custom_call" | custom-call | tf_op jit(solution)/shard_map/mode_apply/pallas_call | solution.py:312
  203.5 1.6 collective-permute-start.2
  205.0 3.1 collective-permute-done.2
  208.2 1.8 fusion.10
  210.0 5.0 %convolution_convert_fusion.1 = bf16[512,4096]{1,0:T(8,128)(2,1)} fusion(bf16[512,768]{1,0:T(8,128)(2,1)S(1)} %get-tuple-element.63, bf16[4096,768]{0,1:T(8,128)(2,1)S(1)} %bitcast.103), kind=kOutput, calls=%fused_computation.6 | convolution fusion | flops 3223322624 | bytes 11272192 | tf_op jit(solution)/shard_map/dot_general | solution.py:460
  215.3 8.3 %convolution_convert_fusion = bf16[4096,768]{1,0:T(8,128)(2,1)} fusion(bf16[512,768]{1,0:T(8,128)(2,1)S(1)} %get-tuple-element.63, bf16[528,4096]{1,0:T(8,128)(2,1)} %copy-done.5), kind=kOutput, calls=%fused_computation.5 | convolution fusion | flops 3224371200 | bytes 11272192 | tf_op jit(solution)/shard_map/dot_general | solution.py:465
  226.0 11.0 %exchange_3.1 = f32[8,128]{1,0:T(8,128)} custom-call(f32[8,128]{1,0:T(8,128)} %pad.4.refs_0_), custom_call_target="tpu_custom_call" | custom-call | tf_op jit(solution)/shard_map/exchange_3/pallas_call | solution.py:137
  237.7 56.7 %reduce-scatter.3.cloned.1.call-done = bf16[512,256]{1,0:T(8,128)(2,1)} async-done(((bf16[512,4096]{1,0:T(8,128)(2,1)}), bf16[512,256]{1,0:T(8,128)(2,1)}) %reduce-scatter.3.cloned.1.call-update) | async-done | bytes 262160 | tf_op jit(solution)/shard_map/reduce_scatter | solution.py:463
  294.3 1.4 fusion.38
  295.8 1.3 collective-permute-start.3
  298.1 2.7 collective-permute-done.3
  301.9 10.0 %lag_sum.3 = f32[2,528,128]{2,1,0:T(8,128)} custom-call(f32[2,656,128]{2,1,0:T(8,128)} %pad_maximum_fusion.4.x_ref, f32[128,256]{1,0:T(8,128)} %rev.3.taps_ref), custom_call_target="tpu_custom_call" | custom-call | tf_op jit(solution)/shard_map/lag_sum/pallas_call | solution.py:197
  311.9 1.1 slice_bitcast_fusion.5
  313.7 1.4 add_convert_fusion
  315.1 1.7 convolution_convert_fusion.4.refs_0_
  316.8 28.8 %exchange_4.1 = f32[64,1024]{1,0:T(8,128)} custom-call(bf16[512,1024]{1,0:T(8,128)(2,1)} %convolution_convert_fusion.4.refs_0_), custom_call_target="tpu_custom_call" | custom-call | tf_op jit(solution)/shard_map/exchange_4/pallas_call | solution.py:137
  346.7 4.8 %convolution_convert_fusion.2.refs_0_ = bf16[64,4096]{1,0:T(8,128)(2,1)} fusion(bf16[64,768]{1,0:T(8,128)(2,1)S(1)} %get-tuple-element.61.refs_2_, bf16[4096,768]{0,1:T(8,128)(2,1)} %bitcast.99), kind=kOutput, calls=%fused_computation.7 | convolution fusion | flops 402915328 | bytes 6914048 | tf_op jit(solution)/shard_map/dot_general | solution.py:507
  352.3 51.1 %exchange_5.1 = (f32[64,256]{1,0:T(8,128)}, f32[64,128]{1,0:T(8,128)}, bf16[8,64,768]{2,1,0:T(8,128)(2,1)}) custom-call(bf16[64,4096]{1,0:T(8,128)(2,1)} %convolution_convert_fusion.2.refs_0_, f32[64,128]{1,0:T(8,128)} %broadcast_in_dim.53.refs_1_, bf16[64,768]{1,0:T(8,128)(2,1)} %copy-done.9), custom_call_target="tpu_custom_call" | custom-call | tf_op jit(solution)/shard_map/exchange_5/pallas_call | solution.py:137
  403.4 1.5 copy.31
  405.0 1.6 fusion.51
  407.3 14.1 %exchange_6.1 = (bf16[8,64,256]{2,1,0:T(8,128)(2,1)}, f32[8,256]{1,0:T(8,128)}) custom-call(bf16[64,256]{1,0:T(8,128)(2,1)} %get-tuple-element.93.refs_0_, f32[8,256]{1,0:T(8,128)} %maximum_maximum_fusion.1.refs_1_), custom_call_target="tpu_custom_call" | custom-call | tf_op jit(solution)/shard_map/exchange_6/pallas_call | solution.py:137
  421.4 1.3 fusion.55
  422.7 1.8 bitcast_convert_fusion
  424.5 1.8 fusion.58
  426.3 34.9 %reduce-scatter.5.cloned.1.call-done = bf16[512,768]{1,0:T(8,128)(2,1)} async-done(((bf16[4096,768]{1,0:T(8,128)(2,1)}), bf16[512,768]{1,0:T(8,128)(2,1)}) %reduce-scatter.5.cloned.1.call-update) | async-done | bytes 786448 | tf_op jit(solution)/shard_map/reduce_scatter | solution.py:464
  461.2 1.4 copy.33
  462.6 1.6 copy.34
  (176 shorter events, 34.7 us)
Async XLA Ops:
  7.2 158.3 %all-gather.2.cloned.1.call-start = ((), (), s32[]{:S(2)}) async-start(), calls=%async_computation.2 | async-start | bytes 4595712 | tf_op jit(solution)/shard_map/all_gather | solution.py:422
  8.0 77.7 %collective-permute-start.1 = (s32[144]{0:T(256)S(1)}, s32[144]{0:T(256)S(1)}, u32[]{:S(2)}, u32[]{:S(2)}) collective-permute-start(s32[144]{0:T(256)S(1)} %get-tuple-element.99), channel_id=1, source_target_pairs={{16,0},{32,16},{48,32},{64,48},{80,64},{96,80},{112,96},{17,1},{33... | collective-permute-start | bytes 1736 | tf_op jit(solution)/shard_map/ppermute | solution.py:324
  9.3 76.4 %collective-permute-start = (s32[144]{0:T(256)S(1)}, s32[144]{0:T(256)S(1)}, u32[]{:S(2)}, u32[]{:S(2)}) collective-permute-start(s32[144]{0:T(256)S(1)} %get-tuple-element.98), channel_id=1, source_target_pairs={{0,16},{16,32},{32,48},{48,64},{64,80},{80,96},{96,112},{1,17},{17... | collective-permute-start | bytes 1736 | tf_op jit(solution)/shard_map/ppermute | solution.py:324
  47.8 8.7 %copy-start.34 = (f32[64]{0:T(128)}, f32[64]{0:T(128)S(1)}, u32[]{:S(2)}) copy-start(f32[64]{0:T(128)S(1)} %get-tuple-element.101) | copy-start | bytes 772
  56.7 5.7 %copy-start.4 = (bf16[64,4096]{1,0:T(8,128)(2,1)}, bf16[64,4096]{1,0:T(8,128)(2,1)S(1)}, u32[]{:S(2)}) copy-start(bf16[64,4096]{1,0:T(8,128)(2,1)S(1)} %fusion.13.refs_1_) | copy-start | bytes 1572868
  56.7 28.1 %copy-start.29 = (f32[7,3,256]{2,0,1:T(8,128)S(1)}, f32[7,3,256]{2,0,1:T(8,128)}, u32[]{:S(2)}) copy-start(f32[7,3,256]{2,0,1:T(8,128)} %param.18) | copy-start | bytes 64516
  56.7 28.3 %copy-start.12 = (bf16[128,256]{1,0:T(8,128)(2,1)S(1)}, bf16[128,256]{1,0:T(8,128)(2,1)}, u32[]{:S(2)}) copy-start(bf16[128,256]{1,0:T(8,128)(2,1)} %param.20) | copy-start | bytes 196612
  56.8 29.0 %copy-start.33 = (bf16[512,256]{1,0:T(8,128)(2,1)S(1)}, bf16[512,256]{1,0:T(8,128)(2,1)}, u32[]{:S(2)}) copy-start(bf16[512,256]{1,0:T(8,128)(2,1)} %param.13) | copy-start | bytes 786436
  84.9 3.1 copy-start.16
  84.9 3.1 copy-start.18
  84.9 3.1 copy-start.20
  85.0 3.1 copy-start.22
  85.0 3.0 copy-start.24
  85.0 3.0 copy-start.26
  85.8 2.3 copy-start.31
  90.2 1.5 copy-start.1
  105.6 9.0 %copy-start.30 = (f32[7,3,256]{2,0,1:T(8,128)S(1)}, f32[7,3,256]{2,0,1:T(8,128)}, u32[]{:S(2)}) copy-start(f32[7,3,256]{2,0,1:T(8,128)} %param.19) | copy-start | bytes 64516
  105.6 9.2 %copy-start.14 = (f32[16,256]{1,0:T(8,128)S(1)}, f32[16,256]{1,0:T(8,128)}, u32[]{:S(2)}) copy-start(f32[16,256]{1,0:T(8,128)} %rate_ref.3) | copy-start | bytes 49156
  105.6 188.8 %reduce-scatter.3.cloned.1.call-start = ((), (), s32[]{:S(2)}) async-start(), calls=%async_computation.3 | async-start | bytes 4456448 | tf_op jit(solution)/shard_map/reduce_scatter | solution.py:463
  165.4 3.5 copy-start
  169.0 3.3 copy-start.3
  170.6 5.2 %copy-start.5 = (bf16[528,4096]{1,0:T(8,128)(2,1)}, bf16[528,4096]{1,0:T(8,128)(2,1)S(1)}, u32[]{:S(2)}) copy-start(bf16[528,4096]{1,0:T(8,128)(2,1)S(1)} %fusion.2) | copy-start | bytes 12976132
  175.8 1.3 copy-start.7
  193.6 8.7 %copy-start.6 = (bf16[528,256]{1,0:T(8,128)(2,1)S(1)}, bf16[528,256]{1,0:T(8,128)(2,1)}, u32[]{:S(2)}) copy-start(bf16[528,256]{1,0:T(8,128)(2,1)} %fusion.25) | copy-start | bytes 811012
  202.3 7.6 %slice-start = ((s8[6291456]{0:T(1024)(128)(4,1)}), s8[4194304]{0:T(1024)(128)(4,1)S(1)}, s32[]{:S(2)}) async-start(s8[6291456]{0:T(1024)(128)(4,1)} %bitcast.101), calls=%async_computation.5 | async-start | bytes 8388608
  203.5 6.6 %slice-start.1 = ((s8[6291456]{0:T(1024)(128)(4,1)}), s8[2097152]{0:T(1024)(128)(4,1)S(1)}, s32[]{:S(2)}) async-start(s8[6291456]{0:T(1024)(128)(4,1)} %bitcast.101), calls=%async_computation.6 | async-start | bytes 4194304
  203.5 4.7 collective-permute-start.2
  215.0 246.2 %reduce-scatter.5.cloned.1.call-start = ((), (), s32[]{:S(2)}) async-start(), calls=%async_computation.4 | async-start | bytes 7077888 | tf_op jit(solution)/shard_map/reduce_scatter | solution.py:464
  223.7 0.7 copy-start.37
  223.7 0.9 copy-start.13
  223.7 1.5 copy-start.38
  223.7 73.4 %copy-start.32 = (s32[800]{0:T(1024)S(1)}, s32[800]{0:T(1024)}, u32[]{:S(2)}) copy-start(s32[800]{0:T(1024)} %copy-done.31) | copy-start | bytes 9604
  223.7 77.2 %copy-start.2 = (f32[792,768]{1,0:T(8,128)S(1)}, f32[792,768]{1,0:T(8,128)}, u32[]{:S(2)}) copy-start(f32[792,768]{1,0:T(8,128)} %copy-done.1) | copy-start | bytes 7299076
  295.8 5.1 %collective-permute-start.3 = (bf16[144,256]{1,0:T(8,128)(2,1)S(1)}, bf16[144,256]{1,0:T(8,128)(2,1)S(1)}, u32[]{:S(2)}, u32[]{:S(2)}) collective-permute-start(bf16[144,256]{1,0:T(8,128)(2,1)S(1)} %slice.495), channel_id=1, source_target_pairs={{16,0},{32,16},{48,32},{64,48},{80,64},{96,80},{112,96},{17,1},{33... | collective-permute-start | bytes 221192 | tf_op jit(solution)/shard_map/ppermute | solution.py:324
  313.0 0.7 copy-start.17
  313.0 0.7 copy-start.19
  313.0 0.7 copy-start.21
  313.0 0.7 copy-start.23
  313.1 0.7 copy-start.25
  313.1 0.7 copy-start.27
  313.7 1.4 copy-start.11
  315.1 30.5 %copy-start.8 = (bf16[64,768]{1,0:T(8,128)(2,1)S(1)}, bf16[64,768]{1,0:T(8,128)(2,1)}, u32[]{:S(2)}) copy-start(bf16[64,768]{1,0:T(8,128)(2,1)} %convolution_convert_fusion.6.refs_0_) | copy-start | bytes 294916
  346.7 4.8 %copy-start.9 = (bf16[64,768]{1,0:T(8,128)(2,1)}, bf16[64,768]{1,0:T(8,128)(2,1)S(1)}, u32[]{:S(2)}) copy-start(bf16[64,768]{1,0:T(8,128)(2,1)S(1)} %get-tuple-element.61.refs_2_) | copy-start | bytes 294916
  351.6 53.5 %copy-start.35 = (f32[64]{0:T(128)S(1)}, f32[64]{0:T(128)}, u32[]{:S(2)}) copy-start(f32[64]{0:T(128)} %copy-done.34) | copy-start | bytes 772
  351.6 53.5 %copy-start.36 = (f32[64]{0:T(128)S(1)}, f32[64]{0:T(128)}, u32[]{:S(2)}) copy-start(f32[64]{0:T(128)} %get-tuple-element.100) | copy-start | bytes 772
  352.3 72.2 %copy-start.10 = (bf16[8,64,512]{2,1,0:T(8,128)(2,1)S(1)}, bf16[8,64,512]{2,1,0:T(8,128)(2,1)}, u32[]{:S(2)}) copy-start(bf16[8,64,512]{2,1,0:T(8,128)(2,1)} %get-tuple-element.26) | copy-start | bytes 1572868
  403.4 1.5 copy-start.28
  403.4 1.6 copy-start.15
Sparse Core Ops, SparseCore 0:
  105.7 59.7 all-gather.1
  215.2 79.1 reduce-scatter.2
  296.8 164.4 reduce-scatter.4

commit v2 on v1

--- a/solution.py
+++ b/solution.py
@@ -143,6 +143,288 @@
         compiler_params=pltpu.CompilerParams(collective_id=cid, has_side_effects=True),
         name=f"exchange_{cid}",
     )(*[it.array for it in items])
+
+
+def place(x, z, core):
+    return x * 8 + z * 2 + core
+
+
+def spot():
+    at = lax.axis_index("ch")
+    return at // 8, lax.rem(at // 2, 4), lax.rem(at, 2)
+
+
+def ring_gather(cid, block):
+    rows, width = block.shape
+    n = lax.axis_size("ch")
+    cut = (rows // 2 + 15) // 16 * 16
+    halves = ((0, cut), (cut, rows - cut))
+
+    def body(src, out, send_sem, recv_sem, own_sem):
+        x, z, core = spot()
+        me = place(x, z, core)
+        z_up, z_down, z_far = lax.rem(z + 1, 4), lax.rem(z + 3, 4), lax.rem(z + 2, 4)
+        up, down, far = place(x, z_up, core), place(x, z_down, core), place(x, z_far, core)
+        over, twin = place(1 - x, z, core), place(x, z, 1 - core)
+        over_up, over_down = place(1 - x, z_up, core), place(1 - x, z_down, core)
+        over_far = place(1 - x, z_far, core)
+
+        barrier = pltpu.get_barrier_semaphore()
+        for peer in (up, down, over, twin):
+            pl.semaphore_signal(barrier, inc=1, device_id={"ch": peer}, device_id_type=MESH)
+        pl.semaphore_wait(barrier, 4)
+
+        def window(c, h):
+            first, size = halves[h]
+            return out.at[pl.ds(first, size), pl.ds(pl.multiple_of(c * width, width), width)]
+
+        sends = []
+
+        def send(c, h, to, ref=None):
+            copy = pltpu.make_async_remote_copy(
+                src_ref=window(c, h) if ref is None else ref,
+                dst_ref=window(c, h),
+                send_sem=send_sem.at[len(sends)],
+                recv_sem=recv_sem.at[c, h],
+                device_id={"ch": to},
+                device_id_type=MESH,
+            )
+            copy.start()
+            sends.append(copy)
+
+        def arrive(c, h):
+            pltpu.make_async_remote_copy(
+                src_ref=window(c, h),
+                dst_ref=window(c, h),
+                send_sem=send_sem.at[0],
+                recv_sem=recv_sem.at[c, h],
+                device_id={"ch": twin},
+                device_id_type=MESH,
+            ).wait_recv()
+
+        mine = [src.at[pl.ds(first, size), :] for first, size in halves]
+        for h, to in ((0, up), (1, down), (0, over), (1, over), (1, up), (0, down), (0, twin), (1, twin)):
+            send(me, h, to, mine[h])
+        own = pltpu.make_async_copy(
+            src, out.at[:, pl.ds(pl.multiple_of(me * width, width), width)], own_sem
+        )
+        own.start()
+        arrive(down, 0)
+        send(down, 0, up)
+        arrive(up, 1)
+        send(up, 1, down)
+        send(down, 0, twin)
+        send(up, 1, twin)
+        for h in (0, 1):
+            arrive(over, h)
+            send(over, h, up)
+            send(over, h, down)
+            send(over, h, twin)
+        arrive(down, 1)
+        send(down, 1, twin)
+        arrive(up, 0)
+        send(up, 0, twin)
+        arrive(over_down, 0)
+        send(over_down, 0, up)
+        arrive(over_up, 1)
+        send(over_up, 1, down)
+        for c, h in ((far, 0), (far, 1)):
+            arrive(c, h)
+            send(c, h, twin)
+        send(over_down, 0, twin)
+        send(over_up, 1, twin)
+        for c, h in ((over_down, 1), (over_up, 0), (over_far, 0), (over_far, 1)):
+            arrive(c, h)
+            send(c, h, twin)
+        for px in (0, 1):
+            for pz in range(4):
+                for h in (0, 1):
+                    arrive(place(px, pz, 1 - core), h)
+        own.wait()
+        for copy in sends:
+            copy.wait_send()
+
+    vmem = pl.BlockSpec(memory_space=pltpu.VMEM)
+    return pl.pallas_call(
+        body,
+        out_shape=jax.ShapeDtypeStruct((rows, n * width), block.dtype),
+        in_specs=[vmem],
+        out_specs=vmem,
+        scratch_shapes=[
+            pltpu.SemaphoreType.DMA((32,)),
+            pltpu.SemaphoreType.DMA((n, 2)),
+            pltpu.SemaphoreType.DMA,
+        ],
+        compiler_params=pltpu.CompilerParams(collective_id=cid, has_side_effects=True),
+        name=f"ring_gather_{cid}",
+    )(block)
+
+
+def ring_scatter(cid, partial, row_part):
+    rows, columns = partial.shape
+    n = lax.axis_size("ch")
+    width = columns // n
+    half = rows // 2
+    step_rows = 32
+
+    def body(part, row_in, out, row_out, mate, acc, fwd, blk, cross, mine, row_buf, sems, row_send, row_recv):
+        x, z, core = spot()
+        me = place(x, z, core)
+        z_up, z_down, z_far = lax.rem(z + 1, 4), lax.rem(z + 3, 4), lax.rem(z + 2, 4)
+        up, down = place(x, z_up, core), place(x, z_down, core)
+        over, twin = place(1 - x, z, core), place(x, z, 1 - core)
+        barrier = pltpu.get_barrier_semaphore()
+
+        def greet(step, carry):
+            peer = lax.rem(me + step, n)
+            pl.semaphore_signal(barrier, inc=1, device_id={"ch": peer}, device_id_type=MESH)
+            return carry
+
+        lax.fori_loop(1, n, greet, 0)
+        pl.semaphore_wait(barrier, n - 1)
+
+        def columns_of(px, pz, pk):
+            return pl.ds(pl.multiple_of(place(px, pz, pk) * width, width), width)
+
+        order = []
+        for px in (1 - x, x):
+            for pz in (z_far, z_up, z_down, z):
+                order.append((px, pz))
+
+        def remote(src, dst, k, to):
+            return pltpu.make_async_remote_copy(
+                src_ref=src,
+                dst_ref=dst,
+                send_sem=sems.at[0, k],
+                recv_sem=sems.at[1, k],
+                device_id={"ch": to},
+                device_id_type=MESH,
+            )
+
+        firsts = []
+        for i, (px, pz) in enumerate(order):
+            copy = remote(part.at[:, columns_of(px, pz, 1 - core)], mate.at[i], i, twin)
+            copy.start()
+            firsts.append(copy)
+
+        def row_copy(peer, slot):
+            return pltpu.make_async_remote_copy(
+                src_ref=row_in,
+                dst_ref=row_buf.at[me],
+                send_sem=row_send.at[slot],
+                recv_sem=row_recv.at[me],
+                device_id={"ch": peer},
+                device_id_type=MESH,
+            )
+
+        def push_row(step, carry):
+            row_copy(lax.rem(me + step, n), step).start()
+            return carry
+
+        lax.fori_loop(1, n, push_row, 0)
+
+        def add(target, sources, first, size):
+            def chunk(i, carry):
+                at = pl.ds(pl.multiple_of(first + i * step_rows, step_rows), step_rows)
+                total = None
+                for ref, base in sources:
+                    index = pl.ds(pl.multiple_of(first - base + i * step_rows, step_rows), step_rows)
+                    term = ref[index, :].astype(f32)
+                    total = term if total is None else total + term
+                target[at, :] = total.astype(target.dtype)
+                return carry
+
+            lax.fori_loop(0, size // step_rows, chunk, 0)
+
+        def meet(i):
+            px, pz = order[i]
+            firsts[i].wait_recv()
+            add(acc.at[i], ((part.at[:, columns_of(px, pz, core)], 0), (mate.at[i], 0)), 0, rows)
+
+        pending = []
+        slots = 8
+
+        def begin(p):
+            base = 4 * p
+            meet(base)
+            k = slots + 4 * p
+            a = remote(acc.at[base, pl.ds(0, half), :], fwd.at[p, 0], k, up)
+            b = remote(acc.at[base, pl.ds(half, half), :], fwd.at[p, 1], k + 1, down)
+            a.start()
+            b.start()
+            meet(base + 1)
+            meet(base + 2)
+            meet(base + 3)
+            return a, b
+
+        def middle(p, pair):
+            base, k = 4 * p, slots + 4 * p
+            a, b = pair
+            a.wait_recv()
+            add(acc.at[base + 1], ((acc.at[base + 1], 0), (fwd.at[p, 0], 0)), 0, half)
+            c = remote(acc.at[base + 1], blk.at[p, 0], k + 2, up)
+            c.start()
+            b.wait_recv()
+            add(acc.at[base + 2], ((acc.at[base + 2], 0), (fwd.at[p, 1], half)), half, half)
+            d = remote(acc.at[base + 2], blk.at[p, 1], k + 3, down)
+            d.start()
+            return c, d
+
+        pair = begin(0)
+        blocks = middle(0, pair)
+        pair_own = begin(1)
+        blocks_own = middle(1, pair_own)
+        for copy in blocks:
+            copy.wait_recv()
+        add(mine, ((acc.at[3], 0), (blk.at[0, 0], 0), (blk.at[0, 1], 0)), 0, rows)
+        crossing = remote(mine, cross, slots + 8, over)
+        crossing.start()
+        for copy in blocks_own:
+            copy.wait_recv()
+        crossing.wait_recv()
+        add(out, ((acc.at[7], 0), (blk.at[1, 0], 0), (blk.at[1, 1], 0), (cross, 0)), 0, rows)
+        for copy in [*firsts, *pair, *blocks, *pair_own, *blocks_own, crossing]:
+            copy.wait_send()
+
+        def gather_row(step, carry):
+            peer = lax.rem(me + step, n)
+            row_copy(peer, step).wait_send()
+            pltpu.make_async_remote_copy(
+                src_ref=row_in,
+                dst_ref=row_buf.at[peer],
+                send_sem=row_send.at[step],
+                recv_sem=row_recv.at[peer],
+                device_id={"ch": peer},
+                device_id_type=MESH,
+            ).wait_recv()
+            return carry + row_buf[peer]
+
+        row_out[...] = lax.fori_loop(1, n, gather_row, row_in[...])
+
+    vmem = pl.BlockSpec(memory_space=pltpu.VMEM)
+    return pl.pallas_call(
+        body,
+        out_shape=[
+            jax.ShapeDtypeStruct((rows, width), f32),
+            jax.ShapeDtypeStruct(row_part.shape, f32),
+        ],
+        in_specs=[vmem] * 2,
+        out_specs=[vmem] * 2,
+        scratch_shapes=[
+            pltpu.VMEM((8, rows, width), bf16),
+            pltpu.VMEM((8, rows, width), bf16),
+            pltpu.VMEM((2, 2, half, width), bf16),
+            pltpu.VMEM((2, 2, rows, width), bf16),
+            pltpu.VMEM((rows, width), bf16),
+            pltpu.VMEM((rows, width), bf16),
+            pltpu.VMEM((n,) + row_part.shape, f32),
+            pltpu.SemaphoreType.DMA((2, 17)),
+            pltpu.SemaphoreType.DMA((n,)),
+            pltpu.SemaphoreType.DMA((n,)),
+        ],
+        compiler_params=pltpu.CompilerParams(collective_id=cid, has_side_effects=True),
+        name=f"ring_scatter_{cid}",
+    )(partial, row_part)
 
 
 def lag_sum(x, taps):
@@ -388,19 +670,14 @@
         ]
     ) - 1
 
-    table_rows = lax.dynamic_slice_in_dim(embedding, seq_at * vocab_part, vocab_part, 0)
     packed = jnp.concatenate(
-        [table_rows, gain_first[None], gain_second[None], jnp.zeros((14, width), bf16)], axis=0
-    )
-    (gathered,) = exchange(0, [Item(packed, "ch")])
-    joined = jnp.concatenate([gathered[i] for i in range(n_ch)], axis=1)
-    whole_gain_first, whole_gain_second = joined[vocab_part], joined[vocab_part + 1]
-    table_normed, table_scale = normalise(joined[:vocab_part], whole_gain_first)
+        [embedding, gain_first[None], gain_second[None], jnp.zeros((14, width), bf16)], axis=0
+    )
+    joined = ring_gather(0, packed)
+    whole_gain_first, whole_gain_second = joined[vocab], joined[vocab + 1]
+    table_normed, table_scale = normalise(joined[:vocab], whole_gain_first)
     table_projected = jnp.dot(table_normed, flat_first, preferred_element_type=f32).astype(bf16)
-    projected_parts, normed_parts = exchange(
-        1, [Item(table_projected, "seq"), Item(table_normed, "seq", window=1)]
-    )
-    table = jnp.concatenate([projected_parts.reshape(vocab, wide), embedding], axis=1)
+    table = jnp.concatenate([table_projected, embedding], axis=1)
 
     onehot = (ids[:, None] == jnp.arange(vocab, dtype=jnp.int32)[None, :]).astype(bf16)
     looked_up = jnp.dot(onehot, table, preferred_element_type=f32).astype(bf16)
@@ -419,7 +696,7 @@
     middle_near = (embedded + featured_first[near, :width] * filtered_first).astype(bf16)
     middle = middle_near[LEAD : LEAD + rows]
 
-    whole_rows = lax.all_gather(middle_near, "ch", axis=1, tiled=True)
+    whole_rows = ring_gather(1, middle_near)
     normed_near, scale_near = normalise(whole_rows, whole_gain_second)
     normed_second, scale_second = normed_near[LEAD : LEAD + rows], scale_near[LEAD : LEAD + rows]
     projected_near = jnp.dot(normed_near, flat_second, preferred_element_type=f32).astype(bf16)
@@ -455,12 +732,11 @@
     row_part = jnp.sum(
         grad_projected.astype(f32) * projected_near[LEAD : LEAD + rows].astype(f32), axis=1
     )
-    (row_total,) = exchange(3, [Item(small(row_part), "ch", reduce=True)])
-    row_total = row_total.reshape(-1)[:rows]
     partial_sum = lax.dot_general(
         grad_projected, flat_second, (((1,), (1,)), ((), ())), preferred_element_type=f32
     ).astype(bf16)
-    grad_normed = lax.psum_scatter(partial_sum, "ch", scatter_dimension=1, tiled=True).astype(f32)
+    grad_normed, row_total = ring_scatter(3, partial_sum, small(row_part))
+    row_total = row_total.reshape(-1)[:rows]
     weight_grad_second = lax.psum_scatter(
         lax.dot_general(
             normed_second, grad_projected, (((0,), (0,)), ((), ())), preferred_element_type=f32
@@ -503,7 +779,8 @@
     (token_sums,) = exchange(4, [Item(by_token, "seq", window=0, reduce=True)])
     token_grad = token_sums[:, :wide].astype(bf16)
     token_above = token_sums[:, wide:]
-    token_part = jnp.sum(token_grad.astype(f32) * table_projected.astype(f32), axis=1)
+    own_part = lambda array: lax.dynamic_slice_in_dim(array, seq_at * vocab_part, vocab_part, 0)
+    token_part = jnp.sum(token_grad.astype(f32) * own_part(table_projected).astype(f32), axis=1)
     token_partial = lax.dot_general(
         token_grad, flat_first, (((1,), (1,)), ((), ())), preferred_element_type=f32
     ).astype(bf16)
@@ -516,8 +793,8 @@
             Item(token_grad, "seq"),
         ],
     )
-    table_float = table_rows.astype(f32)
-    scale = table_scale[:, None]
+    table_float = own_part(embedding).astype(f32)
+    scale = own_part(table_scale)[:, None]
     grad_table = (
         token_above
         + scale * token_normed * gain_first.astype(f32)
@@ -531,7 +808,7 @@
         6, [Item(grad_table.astype(bf16), "seq"), Item(gain_parts, "seq", reduce=True)]
     )
     weight_grad_first = lax.dot_general(
-        normed_parts.reshape(vocab, features // n_seq),
+        lax.dynamic_slice_in_dim(table_normed, seq_at * (features // n_seq), features // n_seq, 1),
         token_grads.reshape(vocab, wide),
         (((0,), (0,)), ((), ())),
         preferred_element_type=f32,

time: 473 us -> 373 us (0.79)
  waiting for transfers between devices: 148 us -> 8.16 us
  Pallas kernels: 185 us -> 230 us
  local copies, waits for them, and re-layouts: 50.4 us -> 35.4 us
  other arithmetic: 30.9 us -> 40.1 us
    pallas_call x0 -> x3, Pallas kernels: none -> 98 us  [the longest x2 59.3 us: ring_gather(): pl.pallas_call(body, out_shape=jax.ShapeDtypeStruct((rows, n * width), bl...]
    reduce_scatter x1 -> x0, waiting for transfers between devices: 56.7 us -> none  [per_device(): lax.psum_scatter(partial_sum, 'ch', scatter_dimension=1, tiled=True)]
    pallas_call x7 -> x4, Pallas kernels: 154 us -> 101 us  [exchange(): pl.pallas_call(body, out_shape=shapes, in_specs=[vmem] * count, out_specs...]
    all_gather x1 -> x0, waiting for transfers between devices: 50.5 us -> none  [per_device(): whole_rows = lax.all_gather(middle_near, 'ch', axis=1, tiled=True)]
    reduce_scatter x1, waiting for transfers between devices: 34.9 us -> 0.01 us  [per_device(): lax.psum_scatter(lax.dot_general(normed_second, grad_projected, (((0,), (...]
    unnamed x100 -> x75, local copies, waits for them, and re-layouts: 35.4 us -> 22 us
  transfers between devices with their start and end apart: 7 -> 5, of which waited for: 5 -> 2; matrix products, arithmetic and copies ran while one was open for 16% -> 18% of each run, Pallas kernels for 33% -> 46%
where the time goes in v2:
time: 373 us; the launch traced here: 372 us
  Pallas kernels  230 us (62%)
  other arithmetic  40.1 us (11%)
  local copies, waits for them, and re-layouts  35.4 us (9%)
  matrix products  34.7 us (9%)
  between operations  14.8 us (4%)
  starting transfers between devices  8.59 us (2%)
  waiting for transfers between devices  8.16 us (2%)
    pallas_call x4, Pallas kernels, exchange(): pl.pallas_call(body, out_shape=shapes, in_specs=[vmem] * count, out_specs...  101 us
    pallas_call x2, Pallas kernels, ring_gather(): pl.pallas_call(body, out_shape=jax.ShapeDtypeStruct((rows, n * width), bl...  59.3 us
    pallas_call x1, Pallas kernels, ring_scatter(): pl.pallas_call(body, out_shape=[jax.ShapeDtypeStruct((rows, width), f32),...  38.7 us
    unnamed x75, local copies, waits for them, and re-layouts  22 us
    pallas_call x2, Pallas kernels, lag_sum(): pl.pallas_call(body, out_shape=jax.ShapeDtypeStruct((width // LANES, rows...  20 us
    ppermute x4, starting transfers between devices, shift_axis(): return lax.ppermute(shard, axis, pairs)  8.56 us
    ppermute x4, waiting for transfers between devices, shift_axis(): return lax.ppermute(shard, axis, pairs)  8.14 us
    dot_general x1, matrix products, per_device(): lax.dot_general(grad_projected, flat_second, (((1,), (1,)), ((), ())), pr...  7.93 us
  transfers between devices with their start and end apart: 5, of which 2 were waited for; matrix products, arithmetic and copies ran while one was open for 18% of the time, Pallas kernels for 46%

profile of v2, /device:TPU:1, one launch (start us, length us, event | category | flops | bytes accessed | tf_op | source)
XLA Modules:
  0.0 371.6 jit_solution(2054348013465991092)
XLA Ops:
  8.0 1.3 collective-permute-start.1
  9.3 4.6 %collective-permute-start = (s32[144]{0:T(256)S(1)}, s32[144]{0:T(256)S(1)}, u32[]{:S(2)}, u32[]{:S(2)}) collective-permute-start(s32[144]{0:T(256)S(1)} %get-tuple-element.100), channel_id=1, source_target_pairs={{0,16},{16,32},{32,48},{48,64},{64,80},{80,96},{96,112},{1,17},{17... | collective-permute-start | bytes 1736 | tf_op jit(solution)/shard_map/ppermute | solution.py:606
  15.2 1.8 maximum_maximum_fusion.src
  17.0 30.6 %ring_gather_0.1 = bf16[528,4096]{1,0:T(8,128)(2,1)} custom-call(bf16[528,256]{1,0:T(8,128)(2,1)} %maximum_maximum_fusion.src), custom_call_target="tpu_custom_call" | custom-call | tf_op jit(solution)/shard_map/ring_gather_0/pallas_call | solution.py:248
  48.6 3.1 fusion.3
  51.8 8.8 %copy.27 = bf16[4096,3,256]{0,2,1:T(8,128)(2,1)} copy(bf16[4096,3,256]{2,0,1:T(8,128)(2,1)} %param.16) | data formatting | bytes 12582912 | tf_op args[4]
  61.5 8.7 %copy.28 = bf16[4096,3,256]{0,2,1:T(8,128)(2,1)} copy(bf16[4096,3,256]{2,0,1:T(8,128)(2,1)} %param.17) | data formatting | bytes 12582912 | tf_op args[5]
  70.3 4.0 %fusion.5 = bf16[512,4096]{1,0:T(8,128)(2,1)S(1)} fusion(f32[4096]{0:T(1024)S(1)} %bitcast.74, f32[512]{0:T(512)S(1)} %add_rsqrt_fusion.1, bf16[528,4096]{1,0:T(8,128)(2,1)} %ring_gather_0.1), kind=kLoop, calls=%fused_computation.9 | loop fusion | flops 8388608 | bytes 8407040 | tf_op jit(solution)/shard_map/convert_element_type | solution.py:629
  74.3 3.5 convolution_convert_fusion.6
  79.3 2.2 multiply_add_fusion
  81.7 1.3 copy-done.2
  83.8 10.0 %lag_sum.2 = f32[2,528,128]{2,1,0:T(8,128)} custom-call(f32[2,656,128]{2,1,0:T(8,128)} %pad_maximum_fusion.3.x_ref, f32[128,256]{1,0:T(8,128)} %convert_element_type.233.taps_ref), custom_call_target="tpu_custom_call" | custom-call | tf_op jit(solution)/shard_map/lag_sum/pallas_call | solution.py:479
  93.8 1.1 slice_bitcast_fusion.7
  94.9 1.9 fusion.25.src
  96.8 28.7 %ring_gather_1.1 = bf16[528,4096]{1,0:T(8,128)(2,1)} custom-call(bf16[528,256]{1,0:T(8,128)(2,1)} %fusion.25.src), custom_call_target="tpu_custom_call" | custom-call | tf_op jit(solution)/shard_map/ring_gather_1/pallas_call | solution.py:248
  125.5 3.3 fusion
  129.0 1.6 fusion.2
  130.6 7.5 %convolution_convert_fusion.5 = bf16[528,768]{1,0:T(8,128)(2,1)S(1)} fusion(bf16[528,4096]{1,0:T(8,128)(2,1)S(1)} %fusion.2, bf16[4096,768]{0,1:T(8,128)(2,1)} %bitcast.66), kind=kOutput, calls=%fused_computation.29 | convolution fusion | flops 3322294272 | bytes 11427840 | tf_op jit(solution)/shard_map/dot_general | solution.py:702
  138.1 1.3 fusion.12
  141.4 4.0 %mode_close.1 = (f32[2,16,8,256]{3,2,1,0:T(8,128)}, f32[2,16,256]{2,1,0:T(8,128)}) custom-call(f32[2,512,128]{2,1,0:T(8,128)} %pad_maximum_fusion.7.a_ref, f32[2,512,128]{2,1,0:T(8,128)} %pad_maximum_fusion.8.b_ref, f32[16,256]{1,0:T(8,128)} %rate_ref.3), custom_call_target="tpu_custom_call" | custom-call | tf_op jit(solution)/shard_map/mode_close/pallas_call | solution.py:534
  145.4 10.6 %exchange_2.1 = f32[8,2,16,256]{3,2,1,0:T(8,128)} custom-call(f32[2,16,256]{2,1,0:T(8,128)} %get-tuple-element.18.refs_0_), custom_call_target="tpu_custom_call" | custom-call | tf_op jit(solution)/shard_map/exchange_2/pallas_call | solution.py:137
  156.0 1.7 multiply_reduce_fusion.enter_ref
  157.6 6.6 %mode_apply.1 = (f32[2,512,128]{2,1,0:T(8,128)}, f32[2,512,128]{2,1,0:T(8,128)}) custom-call(f32[2,512,128]{2,1,0:T(8,128)} %pad_maximum_fusion.7.a_ref, f32[2,512,128]{2,1,0:T(8,128)} %pad_maximum_fusion.8.b_ref, f32[16,256]{1,0:T(8,128)} %rate_ref.3, f32[16,256]{1,0:T(8,128)} %res_ref.1, f32[2,16,8,256]{3,2,1,0:T(8,128)} %get-tuple-element.17.chunk_ref, ...), custom_call_target="tpu_custom_call" | custom-call | tf_op jit(solution)/shard_map/mode_apply/pallas_call | solution.py:594
  167.5 1.4 collective-permute-start.2
  168.9 3.1 collective-permute-done.2
  172.1 2.0 fusion.13
  174.1 5.4 %convolution_convert_fusion = bf16[4096,768]{1,0:T(8,128)(2,1)} fusion(bf16[512,768]{1,0:T(8,128)(2,1)S(1)} %get-tuple-element.65, bf16[528,4096]{1,0:T(8,128)(2,1)S(1)} %bitcast.70), kind=kOutput, calls=%fused_computation.10 | convolution fusion | flops 3224371200 | bytes 11272192 | tf_op jit(solution)/shard_map/dot_general | solution.py:741
  182.6 7.9 %convolution_convert_fusion.1.part = bf16[512,4096]{1,0:T(8,128)(2,1)} fusion(bf16[512,768]{1,0:T(8,128)(2,1)S(1)} %get-tuple-element.65, bf16[4096,768]{0,1:T(8,128)(2,1)} %bitcast.67), kind=kOutput, calls=%fused_computation.11 | convolution fusion | flops 3223322624 | bytes 11272192 | tf_op jit(solution)/shard_map/dot_general | solution.py:735
  190.5 38.7 %ring_scatter_3.1 = (f32[512,256]{1,0:T(8,128)}, f32[8,128]{1,0:T(8,128)}) custom-call(bf16[512,4096]{1,0:T(8,128)(2,1)} %convolution_convert_fusion.1.part, f32[8,128]{1,0:T(8,128)} %pad.4.row_in), custom_call_target="tpu_custom_call" | custom-call | tf_op jit(solution)/shard_map/ring_scatter_3/pallas_call | solution.py:405
  229.9 1.4 fusion.37
  231.3 1.3 collective-permute-start.3
  233.7 5.0 %collective-permute-done.3 = bf16[144,256]{1,0:T(8,128)(2,1)S(1)} collective-permute-done((bf16[144,256]{1,0:T(8,128)(2,1)S(1)}, bf16[144,256]{1,0:T(8,128)(2,1)S(1)}, u32[]{:S(2)}, u32[]{:S(2)}) %collective-permute-start.3) | collective-permute-done | bytes 73760 | tf_op jit(solution)/shard_map/ppermute | solution.py:606
  239.7 10.0 %lag_sum.3 = f32[2,528,128]{2,1,0:T(8,128)} custom-call(f32[2,656,128]{2,1,0:T(8,128)} %pad_maximum_fusion.4.x_ref, f32[128,256]{1,0:T(8,128)} %rev.3.taps_ref), custom_call_target="tpu_custom_call" | custom-call | tf_op jit(solution)/shard_map/lag_sum/pallas_call | solution.py:479
  249.8 1.1 slice_bitcast_fusion.5
  251.6 1.4 add_convert_fusion
  253.0 1.7 convolution_convert_fusion.4.refs_0_
  254.7 30.1 %exchange_4.1 = f32[64,1024]{1,0:T(8,128)} custom-call(bf16[512,1024]{1,0:T(8,128)(2,1)} %convolution_convert_fusion.4.refs_0_), custom_call_target="tpu_custom_call" | custom-call | tf_op jit(solution)/shard_map/exchange_4/pallas_call | solution.py:137
  284.8 1.1 multiply_reduce_fusion.1
  285.9 4.8 %convolution_convert_fusion.2.refs_0_ = bf16[64,4096]{1,0:T(8,128)(2,1)} fusion(bf16[64,768]{1,0:T(8,128)(2,1)S(1)} %get-tuple-element.63.refs_2_, bf16[4096,768]{0,1:T(8,128)(2,1)} %bitcast.64), kind=kOutput, calls=%fused_computation.12 | convolution fusion | flops 402915328 | bytes 6914048 | tf_op jit(solution)/shard_map/dot_general | solution.py:784
  291.4 50.0 %exchange_5.1 = (f32[64,256]{1,0:T(8,128)}, f32[64,128]{1,0:T(8,128)}, bf16[8,64,768]{2,1,0:T(8,128)(2,1)}) custom-call(bf16[64,4096]{1,0:T(8,128)(2,1)} %convolution_convert_fusion.2.refs_0_, f32[64,128]{1,0:T(8,128)} %broadcast_in_dim.53.refs_1_, bf16[64,768]{1,0:T(8,128)(2,1)} %copy-done.8), custom_call_target="tpu_custom_call" | custom-call | tf_op jit(solution)/shard_map/exchange_5/pallas_call | solution.py:137
  341.4 1.4 copy.31
  343.0 1.6 fusion.53
  345.2 10.5 %exchange_6.1 = (bf16[8,64,256]{2,1,0:T(8,128)(2,1)}, f32[8,256]{1,0:T(8,128)}) custom-call(bf16[64,256]{1,0:T(8,128)(2,1)} %get-tuple-element.95.refs_0_, f32[8,256]{1,0:T(8,128)} %maximum_maximum_fusion.1.refs_1_), custom_call_target="tpu_custom_call" | custom-call | tf_op jit(solution)/shard_map/exchange_6/pallas_call | solution.py:137
  355.8 1.3 fusion.58
  357.1 1.8 bitcast_convert_fusion
  358.9 2.8 fusion.40
  361.7 1.4 copy.33
  363.1 1.6 copy.34
  (144 shorter events, 19.9 us)
Async XLA Ops:
  7.2 354.5 %reduce-scatter.2.cloned.1.call-start = ((), (), s32[]{:S(2)}) async-start(), calls=%async_computation.1 | async-start | bytes 7077888 | tf_op jit(solution)/shard_map/reduce_scatter | solution.py:740
  8.0 70.1 %collective-permute-start.1 = (s32[144]{0:T(256)S(1)}, s32[144]{0:T(256)S(1)}, u32[]{:S(2)}, u32[]{:S(2)}) collective-permute-start(s32[144]{0:T(256)S(1)} %get-tuple-element.101), channel_id=1, source_target_pairs={{16,0},{32,16},{48,32},{64,48},{80,64},{96,80},{112,96},{17,1},{33... | collective-permute-start | bytes 1736 | tf_op jit(solution)/shard_map/ppermute | solution.py:606
  9.3 68.8 %collective-permute-start = (s32[144]{0:T(256)S(1)}, s32[144]{0:T(256)S(1)}, u32[]{:S(2)}, u32[]{:S(2)}) collective-permute-start(s32[144]{0:T(256)S(1)} %get-tuple-element.100), channel_id=1, source_target_pairs={{0,16},{16,32},{32,48},{48,64},{64,80},{80,96},{96,112},{1,17},{17... | collective-permute-start | bytes 1736 | tf_op jit(solution)/shard_map/ppermute | solution.py:606
  51.7 18.5 %copy-start.31 = (f32[512]{0:T(512)}, f32[512]{0:T(512)S(1)}, u32[]{:S(2)}) copy-start(f32[512]{0:T(512)S(1)} %add_rsqrt_fusion.1) | copy-start | bytes 6148
  51.8 8.8 %copy-start.28 = (f32[7,3,256]{2,0,1:T(8,128)S(1)}, f32[7,3,256]{2,0,1:T(8,128)}, u32[]{:S(2)}) copy-start(f32[7,3,256]{2,0,1:T(8,128)} %param.18) | copy-start | bytes 64516
  51.8 9.0 %copy-start.11 = (bf16[128,256]{1,0:T(8,128)(2,1)S(1)}, bf16[128,256]{1,0:T(8,128)(2,1)}, u32[]{:S(2)}) copy-start(bf16[128,256]{1,0:T(8,128)(2,1)} %param.20) | copy-start | bytes 196612
  60.7 18.6 %copy-start.15 = (f32[768]{0:T(1024)}, f32[768]{0:T(1024)S(1)}, u32[]{:S(2)}) copy-start(f32[768]{0:T(1024)S(1)} %mul.475) | copy-start | bytes 9220
  60.7 18.5 %copy-start.17 = (f32[768]{0:T(1024)}, f32[768]{0:T(1024)S(1)}, u32[]{:S(2)}) copy-start(f32[768]{0:T(1024)S(1)} %mul.472) | copy-start | bytes 9220
  60.7 18.5 %copy-start.19 = (f32[768]{0:T(1024)}, f32[768]{0:T(1024)S(1)}, u32[]{:S(2)}) copy-start(f32[768]{0:T(1024)S(1)} %mul.469) | copy-start | bytes 9220
  60.7 18.5 %copy-start.21 = (f32[768]{0:T(1024)}, f32[768]{0:T(1024)S(1)}, u32[]{:S(2)}) copy-start(f32[768]{0:T(1024)S(1)} %mul.466) | copy-start | bytes 9220
  60.8 18.5 %copy-start.23 = (f32[768]{0:T(1024)}, f32[768]{0:T(1024)S(1)}, u32[]{:S(2)}) copy-start(f32[768]{0:T(1024)S(1)} %mul.463) | copy-start | bytes 9220
  60.8 18.5 %copy-start.25 = (f32[768]{0:T(1024)}, f32[768]{0:T(1024)S(1)}, u32[]{:S(2)}) copy-start(f32[768]{0:T(1024)S(1)} %mul.460) | copy-start | bytes 9220
  61.5 8.7 %copy-start.29 = (f32[7,3,256]{2,0,1:T(8,128)S(1)}, f32[7,3,256]{2,0,1:T(8,128)}, u32[]{:S(2)}) copy-start(f32[7,3,256]{2,0,1:T(8,128)} %param.19) | copy-start | bytes 64516
  70.3 4.0 %copy-start.1 = (bf16[4096,3,256]{0,2,1:T(8,128)(2,1)S(1)}, bf16[4096,3,256]{0,2,1:T(8,128)(2,1)}, u32[]{:S(2)}) copy-start(bf16[4096,3,256]{0,2,1:T(8,128)(2,1)} %copy.27) | copy-start | bytes 18874372
  74.3 3.5 copy-start.4
  74.3 3.6 copy-start.13
  74.3 3.8 %copy-start.10 = (bf16[512,256]{1,0:T(8,128)(2,1)S(1)}, bf16[512,256]{1,0:T(8,128)(2,1)}, u32[]{:S(2)}) copy-start(bf16[512,256]{1,0:T(8,128)(2,1)} %param.13) | copy-start | bytes 786436
  77.8 1.5 copy-start.30
  81.5 1.4 copy-start.2
  125.5 3.5 copy-start
  130.6 7.5 %copy-start.5 = (bf16[528,4096]{1,0:T(8,128)(2,1)}, bf16[528,4096]{1,0:T(8,128)(2,1)S(1)}, u32[]{:S(2)}) copy-start(bf16[528,4096]{1,0:T(8,128)(2,1)S(1)} %fusion.2) | copy-start | bytes 12976132
  138.1 1.3 copy-start.7
  157.6 8.7 %copy-start.6 = (bf16[528,256]{1,0:T(8,128)(2,1)S(1)}, bf16[528,256]{1,0:T(8,128)(2,1)}, u32[]{:S(2)}) copy-start(bf16[528,256]{1,0:T(8,128)(2,1)} %fusion.25.src) | copy-start | bytes 811012
  166.4 7.7 %slice-start = ((s8[4325376]{0:T(1024)(128)(4,1)}), s8[4194304]{0:T(1024)(128)(4,1)S(1)}, s32[]{:S(2)}) async-start(s8[4325376]{0:T(1024)(128)(4,1)} %bitcast.69), calls=%async_computation.2 | async-start | bytes 8388608
  167.5 6.6 %slice-start.1 = ((s8[4325376]{0:T(1024)(128)(4,1)}), s8[131072]{0:T(1024)(128)(4,1)S(1)}, s32[]{:S(2)}) async-start(s8[4325376]{0:T(1024)(128)(4,1)} %bitcast.69), calls=%async_computation.3 | async-start | bytes 262144
  167.5 4.6 %collective-permute-start.2 = (bf16[8,768]{1,0:T(8,128)(2,1)S(1)}, bf16[8,768]{1,0:T(8,128)(2,1)S(1)}, u32[]{:S(2)}, u32[]{:S(2)}) collective-permute-start(bf16[8,768]{1,0:T(8,128)(2,1)S(1)} %slice.421), channel_id=1, source_target_pairs={{16,0},{32,16},{48,32},{64,48},{80,64},{96,80},{112,96},{17,1},{33... | collective-permute-start | bytes 36872 | tf_op jit(solution)/shard_map/ppermute | solution.py:606
  179.6 0.7 copy-start.32
  179.6 0.9 copy-start.12
  179.6 1.5 copy-start.33
  190.5 48.2 %copy-start.3 = (f32[792,768]{1,0:T(8,128)S(1)}, f32[792,768]{1,0:T(8,128)}, u32[]{:S(2)}) copy-start(f32[792,768]{1,0:T(8,128)} %copy-done.2) | copy-start | bytes 7299076
  231.3 7.3 %collective-permute-start.3 = (bf16[144,256]{1,0:T(8,128)(2,1)S(1)}, bf16[144,256]{1,0:T(8,128)(2,1)S(1)}, u32[]{:S(2)}, u32[]{:S(2)}) collective-permute-start(bf16[144,256]{1,0:T(8,128)(2,1)S(1)} %slice.428), channel_id=1, source_target_pairs={{16,0},{32,16},{48,32},{64,48},{80,64},{96,80},{112,96},{17,1},{33... | collective-permute-start | bytes 221192 | tf_op jit(solution)/shard_map/ppermute | solution.py:606
  250.9 0.7 copy-start.16
  250.9 0.7 copy-start.18
  250.9 0.7 copy-start.20
  250.9 0.7 copy-start.22
  250.9 0.7 copy-start.24
  250.9 0.7 copy-start.26
  251.6 1.4 copy-start.9
  285.9 4.9 %copy-start.8 = (bf16[64,768]{1,0:T(8,128)(2,1)}, bf16[64,768]{1,0:T(8,128)(2,1)S(1)}, u32[]{:S(2)}) copy-start(bf16[64,768]{1,0:T(8,128)(2,1)S(1)} %get-tuple-element.63.refs_2_) | copy-start | bytes 294916
  341.4 1.5 copy-start.27
  341.4 1.6 copy-start.14
Sparse Core Ops, SparseCore 0:
  179.7 168.3 reduce-scatter.1

commit v3 on v2

--- a/solution.py
+++ b/solution.py
@@ -1,11 +1,10 @@
-import functools
-
 import jax
 import jax.numpy as jnp
 from jax import lax
 from jax.experimental import pallas as pl
 from jax.experimental.pallas import tpu as pltpu
 from jax.sharding import PartitionSpec as P
+
 
 epsilon = 1e-06
 MESH = pl.DeviceIdType.MESH
@@ -23,6 +22,8 @@
 
     def block(self):
         shape = list(self.array.shape)
+        if self.window == "onward":
+            return tuple(shape[1:])
         if self.window is not None:
             shape[self.window] //= lax.axis_size(self.axis)
         return tuple(shape)
@@ -50,6 +51,8 @@
         def part(k, peer):
             if items[k].window is None:
                 return srcs[k]
+            if items[k].window == "onward":
+                return srcs[k].at[jnp.where(peer > lax.axis_index(items[k].axis), 0, 1)]
             width = blocks[k][items[k].window]
             start = pl.multiple_of(peer * width, width)
             index = [slice(None)] * len(blocks[k])
@@ -141,7 +144,6 @@
         out_specs=[vmem] * count,
         scratch_shapes=scratch,
         compiler_params=pltpu.CompilerParams(collective_id=cid, has_side_effects=True),
-        name=f"exchange_{cid}",
     )(*[it.array for it in items])
 
 
@@ -154,13 +156,17 @@
     return at // 8, lax.rem(at // 2, 4), lax.rem(at, 2)
 
 
-def ring_gather(cid, block):
+def ring_gather(cid, block, tokens=None):
     rows, width = block.shape
     n = lax.axis_size("ch")
     cut = (rows // 2 + 15) // 16 * 16
     halves = ((0, cut), (cut, rows - cut))
 
-    def body(src, out, send_sem, recv_sem, own_sem):
+    def body(*refs):
+        if tokens is None:
+            src, out, send_sem, recv_sem, own_sem = refs
+        else:
+            src, token_in, out, token_out, send_sem, recv_sem, own_sem, token_sem = refs
         x, z, core = spot()
         me = place(x, z, core)
         z_up, z_down, z_far = lax.rem(z + 1, 4), lax.rem(z + 3, 4), lax.rem(z + 2, 4)
@@ -172,7 +178,25 @@
         barrier = pltpu.get_barrier_semaphore()
         for peer in (up, down, over, twin):
             pl.semaphore_signal(barrier, inc=1, device_id={"ch": peer}, device_id_type=MESH)
-        pl.semaphore_wait(barrier, 4)
+        token_copies = []
+        if tokens is None:
+            pl.semaphore_wait(barrier, 4)
+        else:
+            shards = lax.axis_size("seq")
+            at = lax.axis_index("seq")
+            for slot, peer in ((0, lax.rem(at + 1, shards)), (1, lax.rem(at + shards - 1, shards))):
+                pl.semaphore_signal(barrier, inc=1, device_id={"seq": peer}, device_id_type=MESH)
+                token_copies.append(
+                    pltpu.make_async_remote_copy(
+                        src_ref=token_in,
+                        dst_ref=token_out.at[slot],
+                        send_sem=token_sem.at[0, slot],
+                        recv_sem=token_sem.at[1, slot],
+                        device_id={"seq": peer},
+                        device_id_type=MESH,
+                    )
+                )
+            pl.semaphore_wait(barrier, 6)
 
         def window(c, h):
             first, size = halves[h]
@@ -209,6 +233,8 @@
             src, out.at[:, pl.ds(pl.multiple_of(me * width, width), width)], own_sem
         )
         own.start()
+        for copy in token_copies:
+            copy.start()
         arrive(down, 0)
         send(down, 0, up)
         arrive(up, 1)
@@ -243,31 +269,45 @@
         own.wait()
         for copy in sends:
             copy.wait_send()
+        for copy in token_copies:
+            copy.wait()
 
     vmem = pl.BlockSpec(memory_space=pltpu.VMEM)
+    given = [block] if tokens is None else [block, tokens]
+    shapes = [jax.ShapeDtypeStruct((rows, n * width), block.dtype)]
+    scratch = [
+        pltpu.SemaphoreType.DMA((32,)),
+        pltpu.SemaphoreType.DMA((n, 2)),
+        pltpu.SemaphoreType.DMA,
+    ]
+    if tokens is not None:
+        shapes.append(jax.ShapeDtypeStruct((2,) + tokens.shape, tokens.dtype))
+        scratch.append(pltpu.SemaphoreType.DMA((2, 2)))
     return pl.pallas_call(
         body,
-        out_shape=jax.ShapeDtypeStruct((rows, n * width), block.dtype),
-        in_specs=[vmem],
-        out_specs=vmem,
-        scratch_shapes=[
-            pltpu.SemaphoreType.DMA((32,)),
-            pltpu.SemaphoreType.DMA((n, 2)),
-            pltpu.SemaphoreType.DMA,
-        ],
+        out_shape=shapes,
+        in_specs=[vmem] * len(given),
+        out_specs=[vmem] * len(shapes),
+        scratch_shapes=scratch,
         compiler_params=pltpu.CompilerParams(collective_id=cid, has_side_effects=True),
-        name=f"ring_gather_{cid}",
-    )(block)
-
-
-def ring_scatter(cid, partial, row_part):
+    )(*given)
+
+
+def ring_scatter(cid, partial, row_part, weight_part):
+    pieces = 4
+    chip_rows = weight_part.shape[0] // 4
+    piece_rows = chip_rows // pieces
+    side = weight_part.shape[1] // 2
     rows, columns = partial.shape
     n = lax.axis_size("ch")
     width = columns // n
     half = rows // 2
     step_rows = 32
 
-    def body(part, row_in, out, row_out, mate, acc, fwd, blk, cross, mine, row_buf, sems, row_send, row_recv):
+    def body(
+        part, row_in, w_in, out, row_out, w_out, mate, acc, fwd, blk, cross, mine, row_buf, w_one, w_sum, w_two,
+        sems, row_send, row_recv, w_sems
+    ):
         x, z, core = spot()
         me = place(x, z, core)
         z_up, z_down, z_far = lax.rem(z + 1, 4), lax.rem(z + 3, 4), lax.rem(z + 2, 4)
@@ -281,7 +321,62 @@
             return carry
 
         lax.fori_loop(1, n, greet, 0)
-        pl.semaphore_wait(barrier, n - 1)
+        at_seq = lax.axis_index("seq")
+        y, x_low = at_seq // 2, lax.rem(at_seq, 2)
+        onward = [lax.rem(y + 1, 4) * 2 + x_low, lax.rem(y + 3, 4) * 2 + x_low]
+        for peer in onward:
+            pl.semaphore_signal(barrier, inc=1, device_id={"seq": peer}, device_id_type=MESH)
+        pl.semaphore_wait(barrier, n + 1)
+
+        def w_own(chunk, way, p):
+            first = pl.multiple_of(chunk * chip_rows + p * piece_rows, piece_rows)
+            return w_in.at[pl.ds(first, piece_rows), pl.ds(way * side, side)]
+
+        def w_copy(src, dst, step, way, p):
+            return pltpu.make_async_remote_copy(
+                src_ref=src,
+                dst_ref=dst,
+                send_sem=w_sems.at[0, step, way, p],
+                recv_sem=w_sems.at[1, step, way, p],
+                device_id={"seq": onward[way]},
+                device_id_type=MESH,
+            )
+
+        def behind(way, by):
+            return lax.rem(y + (4 - by if way == 0 else by), 4)
+
+        first_step = {}
+        second_step = {}
+        for p in range(pieces):
+            for way in (0, 1):
+                copy = w_copy(w_own(behind(way, 1), way, p), w_one.at[way, p], 0, way, p)
+                copy.start()
+                first_step[way, p] = copy
+
+        def w_add(target, left, right):
+            def chunk(i, carry):
+                index = pl.ds(pl.multiple_of(i * 16, 16), 16)
+                target[index, :] = (left[index, :].astype(f32) + right[index, :].astype(f32)).astype(bf16)
+                return carry
+
+            lax.fori_loop(0, piece_rows // 16, chunk, 0)
+
+        def w_first(p):
+            for way in (0, 1):
+                first_step[way, p].wait_recv()
+                w_add(w_sum.at[way, p], w_one.at[way, p], w_own(behind(way, 2), way, p))
+                copy = w_copy(w_sum.at[way, p], w_two.at[way, p], 1, way, p)
+                copy.start()
+                second_step[way, p] = copy
+
+        def w_second(p):
+            for way in (0, 1):
+                second_step[way, p].wait_recv()
+                w_add(
+                    w_out.at[way, pl.ds(p * piece_rows, piece_rows), :],
+                    w_two.at[way, p],
+                    w_own(behind(way, 3), way, p),
+                )
 
         def columns_of(px, pz, pk):
             return pl.ds(pl.multiple_of(place(px, pz, pk) * width, width), width)
@@ -341,7 +436,6 @@
             firsts[i].wait_recv()
             add(acc.at[i], ((part.at[:, columns_of(px, pz, core)], 0), (mate.at[i], 0)), 0, rows)
 
-        pending = []
         slots = 8
 
         def begin(p):
@@ -371,19 +465,29 @@
             return c, d
 
         pair = begin(0)
+        w_first(0)
         blocks = middle(0, pair)
+        w_first(1)
         pair_own = begin(1)
+        w_first(2)
         blocks_own = middle(1, pair_own)
+        w_first(3)
         for copy in blocks:
             copy.wait_recv()
         add(mine, ((acc.at[3], 0), (blk.at[0, 0], 0), (blk.at[0, 1], 0)), 0, rows)
         crossing = remote(mine, cross, slots + 8, over)
         crossing.start()
+        w_second(0)
+        w_second(1)
         for copy in blocks_own:
             copy.wait_recv()
         crossing.wait_recv()
         add(out, ((acc.at[7], 0), (blk.at[1, 0], 0), (blk.at[1, 1], 0), (cross, 0)), 0, rows)
+        w_second(2)
+        w_second(3)
         for copy in [*firsts, *pair, *blocks, *pair_own, *blocks_own, crossing]:
+            copy.wait_send()
+        for copy in [*first_step.values(), *second_step.values()]:
             copy.wait_send()
 
         def gather_row(step, carry):
@@ -407,9 +511,10 @@
         out_shape=[
             jax.ShapeDtypeStruct((rows, width), f32),
             jax.ShapeDtypeStruct(row_part.shape, f32),
+            jax.ShapeDtypeStruct((2, chip_rows, side), bf16),
         ],
-        in_specs=[vmem] * 2,
-        out_specs=[vmem] * 2,
+        in_specs=[vmem] * 3,
+        out_specs=[vmem] * 3,
         scratch_shapes=[
             pltpu.VMEM((8, rows, width), bf16),
             pltpu.VMEM((8, rows, width), bf16),
@@ -418,13 +523,16 @@
             pltpu.VMEM((rows, width), bf16),
             pltpu.VMEM((rows, width), bf16),
             pltpu.VMEM((n,) + row_part.shape, f32),
+            pltpu.VMEM((2, pieces, piece_rows, side), bf16),
+            pltpu.VMEM((2, pieces, piece_rows, side), bf16),
+            pltpu.VMEM((2, pieces, piece_rows, side), bf16),
             pltpu.SemaphoreType.DMA((2, 17)),
             pltpu.SemaphoreType.DMA((n,)),
             pltpu.SemaphoreType.DMA((n,)),
+            pltpu.SemaphoreType.DMA((2, 2, 2, pieces)),
         ],
         compiler_params=pltpu.CompilerParams(collective_id=cid, has_side_effects=True),
-        name=f"ring_scatter_{cid}",
-    )(partial, row_part)
+    )(partial, row_part, weight_part)
 
 
 def lag_sum(x, taps):
@@ -545,7 +653,7 @@
 
 def mode_apply(ahead, behind, rates, residues, chunks, entering):
     groups, rows, _ = ahead.shape
-    modes, width = rates.shape
+    modes, _ = rates.shape
     length = rows // SUB
     unroll = 2
 
@@ -629,6 +737,28 @@
     return (as_float * scale[:, None] * gain[None, :].astype(f32)).astype(bf16), scale
 
 
+def last_ring_step(ring_sums, weight_part):
+    at = lax.axis_index("seq")
+    y, x_low = at // 2, lax.rem(at, 2)
+    n_seq = lax.axis_size("seq")
+    chip_rows = ring_sums.shape[1]
+    arrived = [
+        lax.ppermute(
+            ring_sums[way], "seq", [(k, (k // 2 + step) % 4 * 2 + k % 2) for k in range(n_seq)]
+        )
+        for way, step in ((0, 1), (1, 3))
+    ]
+    own = lax.dynamic_slice_in_dim(weight_part, y * chip_rows, chip_rows, 0)
+    sums = jnp.concatenate(arrived, axis=1).astype(f32) + own.astype(f32)
+    part = chip_rows // 2
+    theirs = lax.dynamic_slice_in_dim(sums, (1 - x_low) * part, part, 0).astype(bf16)
+    return lax.dynamic_slice_in_dim(sums, x_low * part, part, 0), theirs
+
+
+def cross(theirs):
+    return lax.ppermute(theirs, "seq", [(k, k ^ 1) for k in range(lax.axis_size("seq"))]).astype(f32)
+
+
 def small(vector, lanes=LANES):
     rows = vector.reshape(-1, lanes)
     pad = -rows.shape[0] % SUB
@@ -649,7 +779,7 @@
     decay_rates,
     cotangent,
 ):
-    n_seq, n_ch = lax.axis_size("seq"), lax.axis_size("ch")
+    n_seq = lax.axis_size("seq")
     seq_at = lax.axis_index("seq")
     rows = token_ids.shape[0]
     vocab, width = embedding.shape
@@ -661,19 +791,13 @@
     taps_first = short_first.reshape(-1, wide)
     taps_second = short_second.reshape(-1, wide)
 
-    shifted = token_ids + 1
-    ids = jnp.concatenate(
-        [
-            shift_axis(shifted[rows - HALO :], "seq", 1),
-            shifted,
-            shift_axis(shifted[:HALO], "seq", -1),
-        ]
-    ) - 1
-
     packed = jnp.concatenate(
         [embedding, gain_first[None], gain_second[None], jnp.zeros((14, width), bf16)], axis=0
     )
-    joined = ring_gather(0, packed)
+    joined, around = ring_gather(0, packed, small(token_ids))
+    before = jnp.where(seq_at == 0, -1, around[0].reshape(-1)[rows - HALO : rows])
+    after = jnp.where(seq_at == n_seq - 1, -1, around[1].reshape(-1)[:HALO])
+    ids = jnp.concatenate([before, token_ids, after])
     whole_gain_first, whole_gain_second = joined[vocab], joined[vocab + 1]
     table_normed, table_scale = normalise(joined[:vocab], whole_gain_first)
     table_projected = jnp.dot(table_normed, flat_first, preferred_element_type=f32).astype(bf16)
@@ -696,7 +820,7 @@
     middle_near = (embedded + featured_first[near, :width] * filtered_first).astype(bf16)
     middle = middle_near[LEAD : LEAD + rows]
 
-    whole_rows = ring_gather(1, middle_near)
+    whole_rows = ring_gather(1, middle_near)[0]
     normed_near, scale_near = normalise(whole_rows, whole_gain_second)
     normed_second, scale_second = normed_near[LEAD : LEAD + rows], scale_near[LEAD : LEAD + rows]
     projected_near = jnp.dot(normed_near, flat_second, preferred_element_type=f32).astype(bf16)
@@ -707,9 +831,10 @@
     grad_filtered = (above_second * pick[0]).astype(bf16).astype(f32)
     gated_lanes, grad_lanes = split_lanes(gated_second), split_lanes(grad_filtered)
     chunks, shard_states = mode_close(gated_lanes, grad_lanes, decay_rates)
-    (all_states,) = exchange(2, [Item(shard_states, "seq")])
+    (all_states,) = exchange(2, [Item(shard_states, "seq", window="onward")])
     other = jnp.arange(n_seq, dtype=jnp.int32)
     gaps = jnp.stack([seq_at - 1 - other, other - 1 - seq_at], axis=1)
+    all_states = all_states[:, None]
     weights_of = jnp.where(
         (gaps >= 0)[:, :, None, None],
         jnp.exp(-decay_rates[None, None] * (jnp.maximum(gaps, 0) * rows).astype(f32)[:, :, None, None]),
@@ -735,16 +860,12 @@
     partial_sum = lax.dot_general(
         grad_projected, flat_second, (((1,), (1,)), ((), ())), preferred_element_type=f32
     ).astype(bf16)
-    grad_normed, row_total = ring_scatter(3, partial_sum, small(row_part))
+    weight_part = lax.dot_general(
+        normed_second, grad_projected, (((0,), (0,)), ((), ())), preferred_element_type=f32
+    ).astype(bf16)
+    grad_normed, row_total, ring_sums = ring_scatter(3, partial_sum, small(row_part), weight_part)
+    ours, theirs = last_ring_step(ring_sums, weight_part)
     row_total = row_total.reshape(-1)[:rows]
-    weight_grad_second = lax.psum_scatter(
-        lax.dot_general(
-            normed_second, grad_projected, (((0,), (0,)), ((), ())), preferred_element_type=f32
-        ).astype(bf16),
-        "seq",
-        scatter_dimension=0,
-        tiled=True,
-    ).astype(f32)
     middle_float = middle.astype(f32)
     scale = scale_second[:, None]
     grad_middle = (
@@ -776,7 +897,10 @@
         (((0,), (0,)), ((), ())),
         preferred_element_type=f32,
     ).astype(bf16)
+    by_token, theirs = lax.optimization_barrier((by_token, theirs))
+    crossed = cross(theirs)
     (token_sums,) = exchange(4, [Item(by_token, "seq", window=0, reduce=True)])
+    weight_grad_second = ours + crossed
     token_grad = token_sums[:, :wide].astype(bf16)
     token_above = token_sums[:, wide:]
     own_part = lambda array: lax.dynamic_slice_in_dim(array, seq_at * vocab_part, vocab_part, 0)

time: 373 us -> 345 us (0.925)
  Pallas kernels: 230 us -> 212 us
  between operations: 14.8 us -> 1.34 us
  local copies, waits for them, and re-layouts: 35.4 us -> 43.3 us
  other arithmetic: 40.1 us -> 46.5 us
  waiting for transfers between devices: 8.16 us -> 2.85 us
    pallas_call x4, Pallas kernels: 101 us -> 73.4 us  [exchange(): pl.pallas_call(body, out_shape=shapes, in_specs=[vmem] * count, out_specs...]
    pallas_call x1, Pallas kernels: 38.7 us -> 48.5 us  [ring_scatter(): pl.pallas_call(body, out_shape=[jax.ShapeDtypeStruct((rows, width), f32),...]
    ppermute x4 -> x2, waiting for transfers between devices: 8.14 us -> 0.01 us  [shift_axis(): return lax.ppermute(shard, axis, pairs)]
    ppermute x4 -> x2, starting transfers between devices: 8.56 us -> 2.72 us  [shift_axis(): return lax.ppermute(shard, axis, pairs)]
    add x1 -> x2, other arithmetic: 0.68 us -> 4.63 us  [the longest x1 2.42 us: per_device(): weight_grad_second = ours + crossed]
    dot_general x1, matrix products: 7.49 us -> 3.58 us  [per_device(): jnp.dot(normed_near, flat_second, preferred_element_type=f32).astype(bf16)]
    unnamed x75 -> x81, local copies, waits for them, and re-layouts: 22 us -> 22.7 us
  transfers between devices with their start and end apart: 5 -> 5, of which waited for: 2 -> 2; matrix products, arithmetic and copies ran while one was open for 18% -> 7% of each run, Pallas kernels for 46% -> 9%
where the time goes in v3:
time: 345 us; the launch traced here: 342 us
  Pallas kernels  212 us (61%)
  other arithmetic  46.5 us (13%)
  local copies, waits for them, and re-layouts  43.3 us (13%)
  matrix products  31.2 us (9%)
  starting transfers between devices  4.87 us (1%)
    pallas_call x4, Pallas kernels, exchange(): pl.pallas_call(body, out_shape=shapes, in_specs=[vmem] * count, out_specs...  73.4 us
    pallas_call x2, Pallas kernels, ring_gather(): pl.pallas_call(body, out_shape=shapes, in_specs=[vmem] * len(given), out_...  59.7 us
    pallas_call x1, Pallas kernels, ring_scatter(): pl.pallas_call(body, out_shape=[jax.ShapeDtypeStruct((rows, width), f32),...  48.5 us
    unnamed x81, local copies, waits for them, and re-layouts  22.7 us
    pallas_call x2, Pallas kernels, lag_sum(): pl.pallas_call(body, out_shape=jax.ShapeDtypeStruct((width // LANES, rows...  20 us
    dot_general x1, matrix products, per_device(): lax.dot_general(grad_projected, flat_second, (((1,), (1,)), ((), ())), pr...  7.99 us
    convert_element_type x2, other arithmetic, normalise(): (as_float * scale[:, None] * gain[None, :].astype(f32)).astype(bf16)  7.9 us
  transfers between devices with their start and end apart: 5, of which 2 were waited for; matrix products, arithmetic and copies ran while one was open for 7% of the time, Pallas kernels for 9%

profile of v3, /device:TPU:1, one launch (start us, length us, event | category | flops | bytes accessed | tf_op | source)
XLA Modules:
  0.0 342.3 jit_solution(5968667914918513050)
XLA Ops:
  2.0 1.3 pad.8.refs_1_
  3.3 1.8 maximum_maximum_fusion.refs_0_
  5.1 32.2 %shard_map.163 = (bf16[528,4096]{1,0:T(8,128)(2,1)}, s32[2,8,128]{2,1,0:T(8,128)}) custom-call(bf16[528,256]{1,0:T(8,128)(2,1)} %maximum_maximum_fusion.refs_0_, s32[8,128]{1,0:T(8,128)} %pad.8.refs_1_), custom_call_target="tpu_custom_call" | custom-call | tf_op jit(solution)/shard_map/pallas_call | solution.py:286
  38.2 3.1 fusion.3
  41.4 8.8 %copy.38 = bf16[4096,3,256]{0,2,1:T(8,128)(2,1)} copy(bf16[4096,3,256]{2,0,1:T(8,128)(2,1)} %param.16) | data formatting | bytes 12582912 | tf_op args[4]
  50.4 4.0 %fusion.5 = bf16[512,4096]{1,0:T(8,128)(2,1)S(1)} fusion(f32[4096]{0:T(1024)S(1)} %bitcast.83, f32[512]{0:T(512)S(1)} %add_rsqrt_fusion.1, bf16[528,4096]{1,0:T(8,128)(2,1)} %get-tuple-element.23), kind=kLoop, calls=%fused_computation.9 | loop fusion | flops 8388608 | bytes 8407040 | tf_op jit(solution)/shard_map/convert_element_type | solution.py:737
  54.4 3.5 %convolution_convert_fusion.6 = bf16[512,768]{1,0:T(8,128)(2,1)S(1)} fusion(bf16[512,4096]{1,0:T(8,128)(2,1)S(1)} %fusion.5, bf16[4096,768]{0,1:T(8,128)(2,1)S(1)} %bitcast.74), kind=kOutput, calls=%fused_computation.33 | convolution fusion | flops 3221618688 | bytes 11272192 | tf_op jit(solution)/shard_map/dot_general | solution.py:803
  59.2 2.2 multiply_add_fusion
  61.6 1.3 copy-done.1
  64.5 10.0 %lag_sum.2 = f32[2,528,128]{2,1,0:T(8,128)} custom-call(f32[2,656,128]{2,1,0:T(8,128)} %pad_maximum_fusion.3.x_ref, f32[128,256]{1,0:T(8,128)} %convert_element_type.244.taps_ref), custom_call_target="tpu_custom_call" | custom-call | tf_op jit(solution)/shard_map/lag_sum/pallas_call | solution.py:587
  76.3 1.9 fusion.25.refs_0_
  78.2 27.5 %shard_map.164 = bf16[528,4096]{1,0:T(8,128)(2,1)} custom-call(bf16[528,256]{1,0:T(8,128)(2,1)} %fusion.25.refs_0_), custom_call_target="tpu_custom_call" | custom-call | tf_op jit(solution)/shard_map/pallas_call | solution.py:286
  105.8 3.1 fusion
  108.9 8.7 %copy.39 = bf16[4096,3,256]{0,2,1:T(8,128)(2,1)} copy(bf16[4096,3,256]{2,0,1:T(8,128)(2,1)} %param.17) | data formatting | bytes 12582912 | tf_op args[5]
  117.8 3.9 %fusion.2 = bf16[528,4096]{1,0:T(8,128)(2,1)S(1)} fusion(bf16[528,4096]{1,0:T(8,128)(2,1)} %shard_map.164, f32[4096]{0:T(1024)S(1)} %bitcast.82, f32[528]{0:T(1024)S(1)} %add_rsqrt_fusion), kind=kLoop, calls=%fused_computation.6 | loop fusion | flops 8650752 | bytes 8669248 | tf_op jit(solution)/shard_map/convert_element_type | solution.py:737
  121.9 3.6 %convolution_convert_fusion.5 = bf16[528,768]{1,0:T(8,128)(2,1)S(1)} fusion(bf16[528,4096]{1,0:T(8,128)(2,1)S(1)} %fusion.2, bf16[4096,768]{0,1:T(8,128)(2,1)S(1)} %bitcast.76), kind=kOutput, calls=%fused_computation.32 | convolution fusion | flops 3322294272 | bytes 11427840 | tf_op jit(solution)/shard_map/dot_general | solution.py:826
  125.5 1.3 fusion.12
  129.4 4.0 %mode_close.1 = (f32[2,16,8,256]{3,2,1,0:T(8,128)}, f32[2,16,256]{2,1,0:T(8,128)}) custom-call(f32[2,512,128]{2,1,0:T(8,128)} %pad_maximum_fusion.7.a_ref, f32[2,512,128]{2,1,0:T(8,128)} %pad_maximum_fusion.8.b_ref, f32[16,256]{1,0:T(8,128)} %rate_ref.3), custom_call_target="tpu_custom_call" | custom-call | tf_op jit(solution)/shard_map/mode_close/pallas_call | solution.py:642
  133.4 8.2 %shard_map.165 = f32[8,16,256]{2,1,0:T(8,128)} custom-call(f32[2,16,256]{2,1,0:T(8,128)} %get-tuple-element.25.refs_0_), custom_call_target="tpu_custom_call" | custom-call | tf_op jit(solution)/shard_map/pallas_call | solution.py:140
  141.8 1.6 multiply_reduce_fusion.enter_ref
  143.4 6.6 %mode_apply.1 = (f32[2,512,128]{2,1,0:T(8,128)}, f32[2,512,128]{2,1,0:T(8,128)}) custom-call(f32[2,512,128]{2,1,0:T(8,128)} %pad_maximum_fusion.7.a_ref, f32[2,512,128]{2,1,0:T(8,128)} %pad_maximum_fusion.8.b_ref, f32[16,256]{1,0:T(8,128)} %rate_ref.3, f32[16,256]{1,0:T(8,128)} %res_ref.1, f32[2,16,8,256]{3,2,1,0:T(8,128)} %get-tuple-element.24.chunk_ref, ...), custom_call_target="tpu_custom_call" | custom-call | tf_op jit(solution)/shard_map/mode_apply/pallas_call | solution.py:702
  153.3 1.3 collective-permute-start
  155.7 1.3 fusion.57
  158.1 1.8 fusion.13
  159.8 8.0 %convolution_convert_fusion.1.part = bf16[512,4096]{1,0:T(8,128)(2,1)} fusion(bf16[512,768]{1,0:T(8,128)(2,1)S(1)} %get-tuple-element.81, bf16[4096,768]{0,1:T(8,128)(2,1)} %bitcast.75), kind=kOutput, calls=%fused_computation.11 | convolution fusion | flops 3223322624 | bytes 11272192 | tf_op jit(solution)/shard_map/dot_general | solution.py:860
  167.8 5.4 %convolution_convert_fusion.w_in = bf16[4096,768]{1,0:T(8,128)(2,1)} fusion(bf16[512,768]{1,0:T(8,128)(2,1)S(1)} %get-tuple-element.81, bf16[528,4096]{1,0:T(8,128)(2,1)S(1)} %bitcast.79), kind=kOutput, calls=%fused_computation.10 | convolution fusion | flops 3224371200 | bytes 11272192 | tf_op jit(solution)/shard_map/dot_general | solution.py:863
  173.9 48.5 %shard_map.166 = (f32[512,256]{1,0:T(8,128)}, f32[8,128]{1,0:T(8,128)}, bf16[2,1024,384]{2,1,0:T(8,128)(2,1)}) custom-call(bf16[512,4096]{1,0:T(8,128)(2,1)} %convolution_convert_fusion.1.part, f32[8,128]{1,0:T(8,128)} %pad.9.row_in, bf16[4096,768]{1,0:T(8,128)(2,1)} %convolution_convert_fusion.w_in), custom_call_target="tpu_custom_call" | custom-call | tf_op jit(solution)/shard_map/pallas_call | solution.py:509
  223.0 1.4 fusion.37
  224.4 1.4 collective-permute-start.1
  225.8 2.7 slice_bitcast_fusion.1
  228.5 1.6 collective-permute-start.3
  231.2 10.0 %lag_sum.3 = f32[2,528,128]{2,1,0:T(8,128)} custom-call(f32[2,656,128]{2,1,0:T(8,128)} %pad_maximum_fusion.4.x_ref, f32[128,256]{1,0:T(8,128)} %rev.3.taps_ref), custom_call_target="tpu_custom_call" | custom-call | tf_op jit(solution)/shard_map/lag_sum/pallas_call | solution.py:587
  243.2 1.4 add_convert_fusion
  244.6 1.7 convolution_convert_fusion.4.refs_0_
  247.2 2.0 collective-permute-done.2
  249.2 2.2 convert_add_fusion
  252.4 17.7 %shard_map.167 = f32[64,1024]{1,0:T(8,128)} custom-call(bf16[512,1024]{1,0:T(8,128)(2,1)} %convolution_convert_fusion.4.refs_0_), custom_call_target="tpu_custom_call" | custom-call | tf_op jit(solution)/shard_map/pallas_call | solution.py:140
  271.2 4.8 %convolution_convert_fusion.2.refs_0_ = bf16[64,4096]{1,0:T(8,128)(2,1)} fusion(bf16[64,768]{1,0:T(8,128)(2,1)S(1)} %get-tuple-element.79.refs_2_, bf16[4096,768]{0,1:T(8,128)(2,1)} %bitcast.73), kind=kOutput, calls=%fused_computation.12 | convolution fusion | flops 402915328 | bytes 6914048 | tf_op jit(solution)/shard_map/dot_general | solution.py:908
  276.7 28.3 %shard_map.168 = (f32[64,256]{1,0:T(8,128)}, f32[64,128]{1,0:T(8,128)}, bf16[8,64,768]{2,1,0:T(8,128)(2,1)}) custom-call(bf16[64,4096]{1,0:T(8,128)(2,1)} %convolution_convert_fusion.2.refs_0_, f32[64,128]{1,0:T(8,128)} %broadcast_in_dim.60.refs_1_, bf16[64,768]{1,0:T(8,128)(2,1)} %copy-done.14), custom_call_target="tpu_custom_call" | custom-call | tf_op jit(solution)/shard_map/pallas_call | solution.py:140
  306.4 1.6 fusion.53
  308.7 2.3 copy.43
  311.0 19.2 %shard_map.169 = (bf16[8,64,256]{2,1,0:T(8,128)(2,1)}, f32[8,256]{1,0:T(8,128)}) custom-call(bf16[64,256]{1,0:T(8,128)(2,1)} %get-tuple-element.113.refs_0_, f32[8,256]{1,0:T(8,128)} %maximum_maximum_fusion.1.refs_1_), custom_call_target="tpu_custom_call" | custom-call | tf_op jit(solution)/shard_map/pallas_call | solution.py:140
  330.2 1.3 fusion.58
  331.5 1.8 bitcast_convert_fusion
  333.3 3.1 fusion.40
  336.4 2.4 convert_add_fusion.1
  338.8 1.9 copy.45
  340.7 1.6 copy.46
  (155 shorter events, 25.8 us)
Async XLA Ops:
  41.4 9.0 %copy-start.30 = (f32[512]{0:T(512)}, f32[512]{0:T(512)S(1)}, u32[]{:S(2)}) copy-start(f32[512]{0:T(512)S(1)} %add_rsqrt_fusion.1) | copy-start | bytes 6148
  41.4 8.8 %copy-start.31 = (s32[2,8,128]{2,1,0:T(8,128)S(1)}, s32[2,8,128]{2,1,0:T(8,128)}, u32[]{:S(2)}) copy-start(s32[2,8,128]{2,1,0:T(8,128)} %get-tuple-element.22) | copy-start | bytes 24580
  41.4 8.8 %copy-start.25 = (f32[7,3,256]{2,0,1:T(8,128)S(1)}, f32[7,3,256]{2,0,1:T(8,128)}, u32[]{:S(2)}) copy-start(f32[7,3,256]{2,0,1:T(8,128)} %param.18) | copy-start | bytes 64516
  50.3 8.8 %copy-start.19 = (f32[768]{0:T(1024)}, f32[768]{0:T(1024)S(1)}, u32[]{:S(2)}) copy-start(f32[768]{0:T(1024)S(1)} %mul.477) | copy-start | bytes 9220
  50.4 8.8 %copy-start.21 = (f32[768]{0:T(1024)}, f32[768]{0:T(1024)S(1)}, u32[]{:S(2)}) copy-start(f32[768]{0:T(1024)S(1)} %mul.474) | copy-start | bytes 9220
  50.4 4.0 %copy-start = (bf16[4096,3,256]{0,2,1:T(8,128)(2,1)S(1)}, bf16[4096,3,256]{0,2,1:T(8,128)(2,1)}, u32[]{:S(2)}) copy-start(bf16[4096,3,256]{0,2,1:T(8,128)(2,1)} %copy.38) | copy-start | bytes 18874372
  54.4 3.6 %copy-start.4 = (bf16[512,4096]{1,0:T(8,128)(2,1)}, bf16[512,4096]{1,0:T(8,128)(2,1)S(1)}, u32[]{:S(2)}) copy-start(bf16[512,4096]{1,0:T(8,128)(2,1)S(1)} %fusion.5) | copy-start | bytes 12582916
  54.4 3.6 %copy-start.32 = (s32[512]{0:T(512)S(1)}, s32[512]{0:T(512)}, u32[]{:S(2)}) copy-start(s32[512]{0:T(512)} %param.12) | copy-start | bytes 6148
  54.4 3.7 %copy-start.16 = (bf16[512,256]{1,0:T(8,128)(2,1)S(1)}, bf16[512,256]{1,0:T(8,128)(2,1)}, u32[]{:S(2)}) copy-start(bf16[512,256]{1,0:T(8,128)(2,1)} %param.13) | copy-start | bytes 786436
  57.9 1.3 copy-start.29
  58.1 1.1 copy-start.27
  61.4 1.5 copy-start.1
  61.4 1.5 copy-start.17
  75.5 0.7 copy-start.7
  75.5 0.8 copy-start.9
  108.9 8.9 %copy-start.23 = (f32[528]{0:T(1024)}, f32[528]{0:T(1024)S(1)}, u32[]{:S(2)}) copy-start(f32[528]{0:T(1024)S(1)} %add_rsqrt_fusion) | copy-start | bytes 6340
  108.9 8.7 %copy-start.26 = (f32[7,3,256]{2,0,1:T(8,128)S(1)}, f32[7,3,256]{2,0,1:T(8,128)}, u32[]{:S(2)}) copy-start(f32[7,3,256]{2,0,1:T(8,128)} %param.19) | copy-start | bytes 64516
  117.8 4.1 %copy-start.3 = (bf16[4096,3,256]{0,2,1:T(8,128)(2,1)S(1)}, bf16[4096,3,256]{0,2,1:T(8,128)(2,1)}, u32[]{:S(2)}) copy-start(bf16[4096,3,256]{0,2,1:T(8,128)(2,1)} %copy.39) | copy-start | bytes 18874372
  121.8 3.7 %copy-start.5 = (bf16[528,4096]{1,0:T(8,128)(2,1)}, bf16[528,4096]{1,0:T(8,128)(2,1)S(1)}, u32[]{:S(2)}) copy-start(bf16[528,4096]{1,0:T(8,128)(2,1)S(1)} %fusion.2) | copy-start | bytes 12976132
  125.5 1.3 copy-start.11
  127.0 0.7 copy-start.18
  143.4 8.8 %copy-start.6 = (bf16[528,256]{1,0:T(8,128)(2,1)S(1)}, bf16[528,256]{1,0:T(8,128)(2,1)}, u32[]{:S(2)}) copy-start(bf16[528,256]{1,0:T(8,128)(2,1)} %fusion.25.refs_0_) | copy-start | bytes 811012
  150.0 2.2 copy-start.12
  153.2 1.4 copy-start.24
  153.2 1.5 copy-start.28
  153.2 3.8 %copy-start.35 = (bf16[256]{0:T(256)(128)(2,1)S(1)}, bf16[256]{0:T(256)(128)(2,1)}, u32[]{:S(2)}) copy-start(bf16[256]{0:T(256)(128)(2,1)} %param.15) | copy-start | bytes 1540
  153.2 4.7 %copy-start.36 = (bf16[256]{0:T(256)(128)(2,1)S(1)}, bf16[256]{0:T(256)(128)(2,1)}, u32[]{:S(2)}) copy-start(bf16[256]{0:T(256)(128)(2,1)} %param.14) | copy-start | bytes 1540
  153.3 4.7 %collective-permute-start = (bf16[8,768]{1,0:T(8,128)(2,1)S(1)}, bf16[8,768]{1,0:T(8,128)(2,1)S(1)}, u32[]{:S(2)}, u32[]{:S(2)}) collective-permute-start(bf16[8,768]{1,0:T(8,128)(2,1)S(1)} %slice.437), channel_id=1, source_target_pairs={{16,0},{32,16},{48,32},{64,48},{80,64},{96,80},{112,96},{17,1},{33... | collective-permute-start | bytes 36872 | tf_op jit(solution)/shard_map/ppermute | solution.py:714
  158.1 9.8 %slice-start = ((s8[4325376]{0:T(1024)(128)(4,1)}), s8[4194304]{0:T(1024)(128)(4,1)S(1)}, s32[]{:S(2)}) async-start(s8[4325376]{0:T(1024)(128)(4,1)} %bitcast.78), calls=%async_computation | async-start | bytes 8388608
  159.8 8.0 %slice-start.1 = ((s8[4325376]{0:T(1024)(128)(4,1)}), s8[131072]{0:T(1024)(128)(4,1)S(1)}, s32[]{:S(2)}) async-start(s8[4325376]{0:T(1024)(128)(4,1)} %bitcast.78), calls=%async_computation.1 | async-start | bytes 262144
  173.8 49.2 %copy-start.13 = (bf16[512,256]{1,0:T(8,128)(2,1)S(1)}, bf16[512,256]{1,0:T(8,128)(2,1)}, u32[]{:S(2)}) copy-start(bf16[512,256]{1,0:T(8,128)(2,1)} %param.23) | copy-start | bytes 786436
  224.4 5.8 %copy-start.2 = (f32[792,768]{1,0:T(8,128)S(1)}, f32[792,768]{1,0:T(8,128)}, u32[]{:S(2)}) copy-start(f32[792,768]{1,0:T(8,128)} %copy-done.1) | copy-start | bytes 7299076
  224.4 5.8 %collective-permute-start.1 = (bf16[144,256]{1,0:T(8,128)(2,1)S(1)}, bf16[144,256]{1,0:T(8,128)(2,1)S(1)}, u32[]{:S(2)}, u32[]{:S(2)}) collective-permute-start(bf16[144,256]{1,0:T(8,128)(2,1)S(1)} %slice.445), channel_id=1, source_target_pairs={{16,0},{32,16},{48,32},{64,48},{80,64},{96,80},{112,96},{17,1},{33... | collective-permute-start | bytes 221192 | tf_op jit(solution)/shard_map/ppermute | solution.py:714
  228.5 18.7 %collective-permute-start.3 = (bf16[1024,384]{1,0:T(8,128)(2,1)}, bf16[1024,384]{1,0:T(8,128)(2,1)}, u32[]{:S(2)}, u32[]{:S(2)}) collective-permute-start(bf16[1024,384]{1,0:T(8,128)(2,1)} %get-tuple-element.89), channel_id=1, source_target_pairs={{0,96},{16,112},{32,0},{48,16},{64,32},{80,48},{96,64},{112,80},{1... | collective-permute-start | bytes 2359304 | tf_op jit(solution)/shard_map/ppermute | solution.py:746
  230.1 19.1 %collective-permute-start.2 = (bf16[1024,384]{1,0:T(8,128)(2,1)}, bf16[1024,384]{1,0:T(8,128)(2,1)}, u32[]{:S(2)}, u32[]{:S(2)}) collective-permute-start(bf16[1024,384]{1,0:T(8,128)(2,1)} %get-tuple-element.88), channel_id=1, source_target_pairs={{0,32},{16,48},{32,64},{48,80},{64,96},{80,112},{96,0},{112,16},{1... | collective-permute-start | bytes 2359304 | tf_op jit(solution)/shard_map/ppermute | solution.py:746
  241.2 1.3 copy-start.8
  241.2 1.3 copy-start.10
  242.5 0.7 copy-start.20
  242.5 0.7 copy-start.22
  243.2 1.4 copy-start.15
  271.2 4.9 %copy-start.14 = (bf16[64,768]{1,0:T(8,128)(2,1)}, bf16[64,768]{1,0:T(8,128)(2,1)S(1)}, u32[]{:S(2)}) copy-start(bf16[64,768]{1,0:T(8,128)(2,1)S(1)} %get-tuple-element.79.refs_2_) | copy-start | bytes 294916
  271.2 35.2 %copy-start.33 = (f32[64]{0:T(128)S(1)}, f32[64]{0:T(128)}, u32[]{:S(2)}) copy-start(f32[64]{0:T(128)} %get-tuple-element.76) | copy-start | bytes 772
  271.2 35.2 %copy-start.34 = (f32[64]{0:T(128)S(1)}, f32[64]{0:T(128)}, u32[]{:S(2)}) copy-start(f32[64]{0:T(128)} %get-tuple-element.77) | copy-start | bytes 772
  305.9 30.4 %collective-permute-start.4 = (bf16[512,768]{1,0:T(8,128)(2,1)}, bf16[512,768]{1,0:T(8,128)(2,1)}, u32[]{:S(2)}, u32[]{:S(2)}) collective-permute-start(bf16[512,768]{1,0:T(8,128)(2,1)} %dynamic-slice_convert_fusion), channel_id=1, source_target_pairs={{0,16},{16,0},{32,48},{48,32},{64,80},{80,64},{96,112},{112,96},{1... | collective-permute-start | bytes 2359304 | tf_op jit(solution)/shard_map/ppermute | solution.py:759

commit v4 on v3

--- a/solution.py
+++ b/solution.py
@@ -147,18 +147,21 @@
     )(*[it.array for it in items])
 
 
-def place(x, z, core):
-    return x * 8 + z * 2 + core
-
-
-def spot():
-    at = lax.axis_index("ch")
-    return at // 8, lax.rem(at // 2, 4), lax.rem(at, 2)
-
-
-def ring_gather(cid, block, tokens=None):
+def place(axis, plane, ring, core):
+    return plane * 8 + ring * 2 + core if axis == "ch" else ring * 2 + plane
+
+
+def spot(axis):
+    at = lax.axis_index(axis)
+    if axis == "ch":
+        return at // 8, lax.rem(at // 2, 4), lax.rem(at, 2)
+    return lax.rem(at, 2), at // 2, 0
+
+
+def ring_gather(cid, axis, block, tokens=None):
     rows, width = block.shape
-    n = lax.axis_size("ch")
+    n = lax.axis_size(axis)
+    twins = axis == "ch"
     cut = (rows // 2 + 15) // 16 * 16
     halves = ((0, cut), (cut, rows - cut))
 
@@ -167,20 +170,20 @@
             src, out, send_sem, recv_sem, own_sem = refs
         else:
             src, token_in, out, token_out, send_sem, recv_sem, own_sem, token_sem = refs
-        x, z, core = spot()
-        me = place(x, z, core)
+        x, z, core = spot(axis)
+        me = place(axis, x, z, core)
         z_up, z_down, z_far = lax.rem(z + 1, 4), lax.rem(z + 3, 4), lax.rem(z + 2, 4)
-        up, down, far = place(x, z_up, core), place(x, z_down, core), place(x, z_far, core)
-        over, twin = place(1 - x, z, core), place(x, z, 1 - core)
-        over_up, over_down = place(1 - x, z_up, core), place(1 - x, z_down, core)
-        over_far = place(1 - x, z_far, core)
+        up, down, far = (place(axis, x, to, core) for to in (z_up, z_down, z_far))
+        over, twin = place(axis, 1 - x, z, core), place(axis, x, z, 1 - core)
+        over_up, over_down, over_far = (place(axis, 1 - x, to, core) for to in (z_up, z_down, z_far))
 
         barrier = pltpu.get_barrier_semaphore()
-        for peer in (up, down, over, twin):
-            pl.semaphore_signal(barrier, inc=1, device_id={"ch": peer}, device_id_type=MESH)
+        peers = [up, down, over] + ([twin] if twins else [])
+        for peer in peers:
+            pl.semaphore_signal(barrier, inc=1, device_id={axis: peer}, device_id_type=MESH)
         token_copies = []
         if tokens is None:
-            pl.semaphore_wait(barrier, 4)
+            pl.semaphore_wait(barrier, len(peers))
         else:
             shards = lax.axis_size("seq")
             at = lax.axis_index("seq")
@@ -196,10 +199,12 @@
                         device_id_type=MESH,
                     )
                 )
-            pl.semaphore_wait(barrier, 6)
+            pl.semaphore_wait(barrier, len(peers) + 2)
 
         def window(c, h):
             first, size = halves[h]
+            if not twins:
+                return out.at[c, pl.ds(first, size), :]
             return out.at[pl.ds(first, size), pl.ds(pl.multiple_of(c * width, width), width)]
 
         sends = []
@@ -210,11 +215,15 @@
                 dst_ref=window(c, h),
                 send_sem=send_sem.at[len(sends)],
                 recv_sem=recv_sem.at[c, h],
-                device_id={"ch": to},
+                device_id={axis: to},
                 device_id_type=MESH,
             )
             copy.start()
             sends.append(copy)
+
+        def share(c, h, ref=None):
+            if twins:
+                send(c, h, twin, ref)
 
         def arrive(c, h):
             pltpu.make_async_remote_copy(
@@ -222,16 +231,17 @@
                 dst_ref=window(c, h),
                 send_sem=send_sem.at[0],
                 recv_sem=recv_sem.at[c, h],
-                device_id={"ch": twin},
+                device_id={axis: over},
                 device_id_type=MESH,
             ).wait_recv()
 
         mine = [src.at[pl.ds(first, size), :] for first, size in halves]
-        for h, to in ((0, up), (1, down), (0, over), (1, over), (1, up), (0, down), (0, twin), (1, twin)):
+        for h, to in ((0, up), (1, down), (0, over), (1, over), (1, up), (0, down)):
             send(me, h, to, mine[h])
-        own = pltpu.make_async_copy(
-            src, out.at[:, pl.ds(pl.multiple_of(me * width, width), width)], own_sem
-        )
+        for h in (0, 1):
+            share(me, h, mine[h])
+        here = out.at[:, pl.ds(pl.multiple_of(me * width, width), width)] if twins else out.at[me]
+        own = pltpu.make_async_copy(src, here, own_sem)
         own.start()
         for copy in token_copies:
             copy.start()
@@ -239,33 +249,34 @@
         send(down, 0, up)
         arrive(up, 1)
         send(up, 1, down)
-        send(down, 0, twin)
-        send(up, 1, twin)
+        share(down, 0)
+        share(up, 1)
         for h in (0, 1):
             arrive(over, h)
             send(over, h, up)
             send(over, h, down)
-            send(over, h, twin)
+            share(over, h)
         arrive(down, 1)
-        send(down, 1, twin)
+        share(down, 1)
         arrive(up, 0)
-        send(up, 0, twin)
+        share(up, 0)
         arrive(over_down, 0)
         send(over_down, 0, up)
         arrive(over_up, 1)
         send(over_up, 1, down)
-        for c, h in ((far, 0), (far, 1)):
-            arrive(c, h)
-            send(c, h, twin)
-        send(over_down, 0, twin)
-        send(over_up, 1, twin)
+        for h in (0, 1):
+            arrive(far, h)
+            share(far, h)
+        share(over_down, 0)
+        share(over_up, 1)
         for c, h in ((over_down, 1), (over_up, 0), (over_far, 0), (over_far, 1)):
             arrive(c, h)
-            send(c, h, twin)
-        for px in (0, 1):
-            for pz in range(4):
-                for h in (0, 1):
-                    arrive(place(px, pz, 1 - core), h)
+            share(c, h)
+        if twins:
+            for px in (0, 1):
+                for pz in range(4):
+                    for h in (0, 1):
+                        arrive(place(axis, px, pz, 1 - core), h)
         own.wait()
         for copy in sends:
             copy.wait_send()
@@ -274,7 +285,8 @@
 
     vmem = pl.BlockSpec(memory_space=pltpu.VMEM)
     given = [block] if tokens is None else [block, tokens]
-    shapes = [jax.ShapeDtypeStruct((rows, n * width), block.dtype)]
+    whole = (rows, n * width) if twins else (n, rows, width)
+    shapes = [jax.ShapeDtypeStruct(whole, block.dtype)]
     scratch = [
         pltpu.SemaphoreType.DMA((32,)),
         pltpu.SemaphoreType.DMA((n, 2)),
@@ -293,40 +305,66 @@
     )(*given)
 
 
-def ring_scatter(cid, partial, row_part, weight_part):
-    pieces = 4
-    chip_rows = weight_part.shape[0] // 4
-    piece_rows = chip_rows // pieces
-    side = weight_part.shape[1] // 2
-    rows, columns = partial.shape
-    n = lax.axis_size("ch")
-    width = columns // n
+def ring_scatter(cid, axis, partial, row_part=None, weight_part=None):
+    n = lax.axis_size(axis)
+    twins = axis == "ch"
+    rows, width = (partial.shape[0], partial.shape[1] // n) if twins else (partial.shape[0] // n, partial.shape[1])
     half = rows // 2
     step_rows = 32
-
-    def body(
-        part, row_in, w_in, out, row_out, w_out, mate, acc, fwd, blk, cross, mine, row_buf, w_one, w_sum, w_two,
-        sems, row_send, row_recv, w_sems
-    ):
-        x, z, core = spot()
-        me = place(x, z, core)
+    has_rows, has_weights = row_part is not None, weight_part is not None
+    pieces = 4
+    if has_weights:
+        chip_rows = weight_part.shape[0] // 4
+        piece_rows = chip_rows // pieces
+        side = weight_part.shape[1] // 2
+
+    def body(*refs):
+        refs = list(refs)
+        part = refs.pop(0)
+        row_in = refs.pop(0) if has_rows else None
+        w_in = refs.pop(0) if has_weights else None
+        out = refs.pop(0)
+        row_out = refs.pop(0) if has_rows else None
+        w_out = refs.pop(0) if has_weights else None
+        acc, fwd, blk, cross, mine, sems = refs[:6]
+        refs = refs[6:]
+        mate = refs.pop(0) if twins else None
+        if has_rows:
+            row_buf, row_send, row_recv = refs[:3]
+            refs = refs[3:]
+        if has_weights:
+            w_one, w_sum, w_two, w_sems = refs
+        x, z, core = spot(axis)
+        me = place(axis, x, z, core)
         z_up, z_down, z_far = lax.rem(z + 1, 4), lax.rem(z + 3, 4), lax.rem(z + 2, 4)
-        up, down = place(x, z_up, core), place(x, z_down, core)
-        over, twin = place(1 - x, z, core), place(x, z, 1 - core)
+        up, down = place(axis, x, z_up, core), place(axis, x, z_down, core)
+        over, twin = place(axis, 1 - x, z, core), place(axis, x, z, 1 - core)
         barrier = pltpu.get_barrier_semaphore()
-
-        def greet(step, carry):
-            peer = lax.rem(me + step, n)
-            pl.semaphore_signal(barrier, inc=1, device_id={"ch": peer}, device_id_type=MESH)
-            return carry
-
-        lax.fori_loop(1, n, greet, 0)
-        at_seq = lax.axis_index("seq")
-        y, x_low = at_seq // 2, lax.rem(at_seq, 2)
-        onward = [lax.rem(y + 1, 4) * 2 + x_low, lax.rem(y + 3, 4) * 2 + x_low]
-        for peer in onward:
-            pl.semaphore_signal(barrier, inc=1, device_id={"seq": peer}, device_id_type=MESH)
-        pl.semaphore_wait(barrier, n + 1)
+        if has_rows:
+
+            def greet(step, carry):
+                peer = lax.rem(me + step, n)
+                pl.semaphore_signal(barrier, inc=1, device_id={axis: peer}, device_id_type=MESH)
+                return carry
+
+            lax.fori_loop(1, n, greet, 0)
+            greeted = n - 1
+        else:
+            peers = [up, down, over] + ([twin] if twins else [])
+            for peer in peers:
+                pl.semaphore_signal(barrier, inc=1, device_id={axis: peer}, device_id_type=MESH)
+            greeted = len(peers)
+        if has_weights:
+            at_seq = lax.axis_index("seq")
+            y, x_low = at_seq // 2, lax.rem(at_seq, 2)
+            onward = [lax.rem(y + 1, 4) * 2 + x_low, lax.rem(y + 3, 4) * 2 + x_low]
+            for peer in onward:
+                pl.semaphore_signal(barrier, inc=1, device_id={"seq": peer}, device_id_type=MESH)
+            greeted += 2
+        pl.semaphore_wait(barrier, greeted)
+
+        first_step = {}
+        second_step = {}
 
         def w_own(chunk, way, p):
             first = pl.multiple_of(chunk * chip_rows + p * piece_rows, piece_rows)
@@ -345,14 +383,6 @@
         def behind(way, by):
             return lax.rem(y + (4 - by if way == 0 else by), 4)
 
-        first_step = {}
-        second_step = {}
-        for p in range(pieces):
-            for way in (0, 1):
-                copy = w_copy(w_own(behind(way, 1), way, p), w_one.at[way, p], 0, way, p)
-                copy.start()
-                first_step[way, p] = copy
-
         def w_add(target, left, right):
             def chunk(i, carry):
                 index = pl.ds(pl.multiple_of(i * 16, 16), 16)
@@ -362,7 +392,7 @@
             lax.fori_loop(0, piece_rows // 16, chunk, 0)
 
         def w_first(p):
-            for way in (0, 1):
+            for way in (0, 1) if has_weights else ():
                 first_step[way, p].wait_recv()
                 w_add(w_sum.at[way, p], w_one.at[way, p], w_own(behind(way, 2), way, p))
                 copy = w_copy(w_sum.at[way, p], w_two.at[way, p], 1, way, p)
@@ -370,7 +400,7 @@
                 second_step[way, p] = copy
 
         def w_second(p):
-            for way in (0, 1):
+            for way in (0, 1) if has_weights else ():
                 second_step[way, p].wait_recv()
                 w_add(
                     w_out.at[way, pl.ds(p * piece_rows, piece_rows), :],
@@ -378,8 +408,17 @@
                     w_own(behind(way, 3), way, p),
                 )
 
-        def columns_of(px, pz, pk):
-            return pl.ds(pl.multiple_of(place(px, pz, pk) * width, width), width)
+        for p in range(pieces) if has_weights else ():
+            for way in (0, 1):
+                copy = w_copy(w_own(behind(way, 1), way, p), w_one.at[way, p], 0, way, p)
+                copy.start()
+                first_step[way, p] = copy
+
+        def own_block(px, pz, pk):
+            at = place(axis, px, pz, pk)
+            if twins:
+                return part.at[:, pl.ds(pl.multiple_of(at * width, width), width)]
+            return part.at[pl.ds(pl.multiple_of(at * rows, rows), rows), :]
 
         order = []
         for px in (1 - x, x):
@@ -392,13 +431,13 @@
                 dst_ref=dst,
                 send_sem=sems.at[0, k],
                 recv_sem=sems.at[1, k],
-                device_id={"ch": to},
+                device_id={axis: to},
                 device_id_type=MESH,
             )
 
         firsts = []
-        for i, (px, pz) in enumerate(order):
-            copy = remote(part.at[:, columns_of(px, pz, 1 - core)], mate.at[i], i, twin)
+        for i, (px, pz) in enumerate(order) if twins else ():
+            copy = remote(own_block(px, pz, 1 - core), mate.at[i], i, twin)
             copy.start()
             firsts.append(copy)
 
@@ -408,7 +447,7 @@
                 dst_ref=row_buf.at[me],
                 send_sem=row_send.at[slot],
                 recv_sem=row_recv.at[me],
-                device_id={"ch": peer},
+                device_id={axis: peer},
                 device_id_type=MESH,
             )
 
@@ -416,7 +455,8 @@
             row_copy(lax.rem(me + step, n), step).start()
             return carry
 
-        lax.fori_loop(1, n, push_row, 0)
+        if has_rows:
+            lax.fori_loop(1, n, push_row, 0)
 
         def add(target, sources, first, size):
             def chunk(i, carry):
@@ -433,8 +473,11 @@
 
         def meet(i):
             px, pz = order[i]
-            firsts[i].wait_recv()
-            add(acc.at[i], ((part.at[:, columns_of(px, pz, core)], 0), (mate.at[i], 0)), 0, rows)
+            sources = ((own_block(px, pz, core), 0),)
+            if twins:
+                firsts[i].wait_recv()
+                sources += ((mate.at[i], 0),)
+            add(acc.at[i], sources, 0, rows)
 
         slots = 8
 
@@ -498,41 +541,48 @@
                 dst_ref=row_buf.at[peer],
                 send_sem=row_send.at[step],
                 recv_sem=row_recv.at[peer],
-                device_id={"ch": peer},
+                device_id={axis: peer},
                 device_id_type=MESH,
             ).wait_recv()
             return carry + row_buf[peer]
 
-        row_out[...] = lax.fori_loop(1, n, gather_row, row_in[...])
+        if has_rows:
+            row_out[...] = lax.fori_loop(1, n, gather_row, row_in[...])
 
     vmem = pl.BlockSpec(memory_space=pltpu.VMEM)
+    given = [partial]
+    shapes = [jax.ShapeDtypeStruct((rows, width), f32)]
+    scratch = [
+        pltpu.VMEM((8, rows, width), bf16),
+        pltpu.VMEM((2, 2, half, width), bf16),
+        pltpu.VMEM((2, 2, rows, width), bf16),
+        pltpu.VMEM((rows, width), bf16),
+        pltpu.VMEM((rows, width), bf16),
+        pltpu.SemaphoreType.DMA((2, 17)),
+    ]
+    if twins:
+        scratch.append(pltpu.VMEM((8, rows, width), bf16))
+    if has_rows:
+        given.append(row_part)
+        shapes.append(jax.ShapeDtypeStruct(row_part.shape, f32))
+        scratch += [
+            pltpu.VMEM((n,) + row_part.shape, f32),
+            pltpu.SemaphoreType.DMA((n,)),
+            pltpu.SemaphoreType.DMA((n,)),
+        ]
+    if has_weights:
+        given.append(weight_part)
+        shapes.append(jax.ShapeDtypeStruct((2, chip_rows, side), bf16))
+        scratch += [pltpu.VMEM((2, pieces, piece_rows, side), bf16)] * 3
+        scratch.append(pltpu.SemaphoreType.DMA((2, 2, 2, pieces)))
     return pl.pallas_call(
         body,
-        out_shape=[
-            jax.ShapeDtypeStruct((rows, width), f32),
-            jax.ShapeDtypeStruct(row_part.shape, f32),
-            jax.ShapeDtypeStruct((2, chip_rows, side), bf16),
-        ],
-        in_specs=[vmem] * 3,
-        out_specs=[vmem] * 3,
-        scratch_shapes=[
-            pltpu.VMEM((8, rows, width), bf16),
-            pltpu.VMEM((8, rows, width), bf16),
-            pltpu.VMEM((2, 2, half, width), bf16),
-            pltpu.VMEM((2, 2, rows, width), bf16),
-            pltpu.VMEM((rows, width), bf16),
-            pltpu.VMEM((rows, width), bf16),
-            pltpu.VMEM((n,) + row_part.shape, f32),
-            pltpu.VMEM((2, pieces, piece_rows, side), bf16),
-            pltpu.VMEM((2, pieces, piece_rows, side), bf16),
-            pltpu.VMEM((2, pieces, piece_rows, side), bf16),
-            pltpu.SemaphoreType.DMA((2, 17)),
-            pltpu.SemaphoreType.DMA((n,)),
-            pltpu.SemaphoreType.DMA((n,)),
-            pltpu.SemaphoreType.DMA((2, 2, 2, pieces)),
-        ],
+        out_shape=shapes,
+        in_specs=[vmem] * len(given),
+        out_specs=[vmem] * len(shapes),
+        scratch_shapes=scratch,
         compiler_params=pltpu.CompilerParams(collective_id=cid, has_side_effects=True),
-    )(partial, row_part, weight_part)
+    )(*given)
 
 
 def lag_sum(x, taps):
@@ -759,8 +809,8 @@
     return lax.ppermute(theirs, "seq", [(k, k ^ 1) for k in range(lax.axis_size("seq"))]).astype(f32)
 
 
-def small(vector, lanes=LANES):
-    rows = vector.reshape(-1, lanes)
+def small(vector):
+    rows = vector.reshape(-1, LANES)
     pad = -rows.shape[0] % SUB
     return jnp.pad(rows, ((0, pad), (0, 0)))
 
@@ -794,7 +844,7 @@
     packed = jnp.concatenate(
         [embedding, gain_first[None], gain_second[None], jnp.zeros((14, width), bf16)], axis=0
     )
-    joined, around = ring_gather(0, packed, small(token_ids))
+    joined, around = ring_gather(0, "ch", packed, small(token_ids))
     before = jnp.where(seq_at == 0, -1, around[0].reshape(-1)[rows - HALO : rows])
     after = jnp.where(seq_at == n_seq - 1, -1, around[1].reshape(-1)[:HALO])
     ids = jnp.concatenate([before, token_ids, after])
@@ -820,7 +870,7 @@
     middle_near = (embedded + featured_first[near, :width] * filtered_first).astype(bf16)
     middle = middle_near[LEAD : LEAD + rows]
 
-    whole_rows = ring_gather(1, middle_near)[0]
+    whole_rows = ring_gather(1, "ch", middle_near)[0]
     normed_near, scale_near = normalise(whole_rows, whole_gain_second)
     normed_second, scale_second = normed_near[LEAD : LEAD + rows], scale_near[LEAD : LEAD + rows]
     projected_near = jnp.dot(normed_near, flat_second, preferred_element_type=f32).astype(bf16)
@@ -863,7 +913,7 @@
     weight_part = lax.dot_general(
         normed_second, grad_projected, (((0,), (0,)), ((), ())), preferred_element_type=f32
     ).astype(bf16)
-    grad_normed, row_total, ring_sums = ring_scatter(3, partial_sum, small(row_part), weight_part)
+    grad_normed, row_total, ring_sums = ring_scatter(3, "ch", partial_sum, small(row_part), weight_part)
     ours, theirs = last_ring_step(ring_sums, weight_part)
     row_total = row_total.reshape(-1)[:rows]
     middle_float = middle.astype(f32)
@@ -899,7 +949,7 @@
     ).astype(bf16)
     by_token, theirs = lax.optimization_barrier((by_token, theirs))
     crossed = cross(theirs)
-    (token_sums,) = exchange(4, [Item(by_token, "seq", window=0, reduce=True)])
+    (token_sums,) = ring_scatter(4, "seq", by_token)
     weight_grad_second = ours + crossed
     token_grad = token_sums[:, :wide].astype(bf16)
     token_above = token_sums[:, wide:]
@@ -908,38 +958,43 @@
     token_partial = lax.dot_general(
         token_grad, flat_first, (((1,), (1,)), ((), ())), preferred_element_type=f32
     ).astype(bf16)
-    spread = jnp.broadcast_to(token_part[:, None], (vocab_part, LANES))
-    token_normed, token_total, token_grads = exchange(
-        5,
-        [
-            Item(token_partial, "ch", window=1, reduce=True),
-            Item(spread, "ch", reduce=True),
-            Item(token_grad, "seq"),
-        ],
-    )
+    token_normed, token_total = ring_scatter(5, "ch", token_partial, small(jnp.pad(token_part, (0, -vocab_part % LANES))))
+    token_total = token_total.reshape(-1)[:vocab_part, None]
     table_float = own_part(embedding).astype(f32)
     scale = own_part(table_scale)[:, None]
     grad_table = (
         token_above
         + scale * token_normed * gain_first.astype(f32)
-        - table_float * (scale * scale) * token_total[:, :1] / features
+        - table_float * (scale * scale) * token_total / features
     )
     gain_part_first = jnp.sum(token_normed * table_float * scale, axis=0)
-    gain_parts = jnp.concatenate(
-        [gain_part_first[None], gain_part_second[None], jnp.zeros((6, width), f32)], axis=0
-    )
-    table_parts, gain_total = exchange(
-        6, [Item(grad_table.astype(bf16), "seq"), Item(gain_parts, "seq", reduce=True)]
-    )
+    highs = [part.astype(bf16) for part in (gain_part_first, gain_part_second)]
+    lows = [
+        (part - high.astype(f32)).astype(bf16)
+        for part, high in zip((gain_part_first, gain_part_second), highs)
+    ]
+    gain_row = jnp.concatenate([highs[0], lows[0], highs[1], lows[1]])
+    closing = jnp.concatenate(
+        [
+            jnp.concatenate([token_grad, grad_table.astype(bf16)], axis=1),
+            gain_row[None],
+            jnp.zeros((15, wide + width), bf16),
+        ],
+        axis=0,
+    )
+    (closed,) = ring_gather(6, "seq", closing)
+    token_grads = closed[:, :vocab_part, :wide].reshape(vocab, wide)
+    table_parts = closed[:, :vocab_part, wide:].reshape(vocab, width)
+    gain_total = jnp.sum(closed[:, vocab_part].astype(f32).reshape(n_seq, 2, 2, width), axis=(0, 2))
     weight_grad_first = lax.dot_general(
         lax.dynamic_slice_in_dim(table_normed, seq_at * (features // n_seq), features // n_seq, 1),
-        token_grads.reshape(vocab, wide),
+        token_grads,
         (((0,), (0,)), ((), ())),
         preferred_element_type=f32,
     )
     return (
         output,
-        table_parts.reshape(vocab, width).astype(f32),
+        table_parts.astype(f32),
         gain_total[0],
         gain_total[1],
         weight_grad_first.reshape(-1, 3, width),

time: 345 us -> 339 us (0.983)
  Pallas kernels: 212 us -> 199 us
  waiting for transfers between devices: 2.85 us -> 9.65 us
    pallas_call x4 -> x1, Pallas kernels: 73.4 us -> 8.19 us  [exchange(): pl.pallas_call(body, out_shape=shapes, in_specs=[vmem] * count, out_specs...]
    pallas_call x1 -> x3, Pallas kernels: 48.5 us -> 83.4 us  [ring_scatter(): pl.pallas_call(body, out_shape=shapes, in_specs=[vmem] * len(given), out_...]
    pallas_call x2 -> x3, Pallas kernels: 59.7 us -> 76.4 us  [ring_gather(): pl.pallas_call(body, out_shape=shapes, in_specs=[vmem] * len(given), out_...]
    ppermute x1, waiting for transfers between devices: 0.01 us -> 6.92 us  [cross(): lax.ppermute(theirs, 'seq', [(k, k ^ 1) for k in range(lax.axis_size('seq...]
    unnamed x81 -> x91, local copies, waits for them, and re-layouts: 22.7 us -> 23.6 us
  transfers between devices with their start and end apart: 5 -> 5, of which waited for: 2 -> 3; matrix products, arithmetic and copies ran while one was open for 7% -> 6% of each run, Pallas kernels for 9% -> 3%
where the time goes in v4:
time: 339 us; the launch traced here: 334 us
  Pallas kernels  199 us (59%)
  other arithmetic  45.7 us (13%)
  local copies, waits for them, and re-layouts  43 us (13%)
  matrix products  31 us (9%)
  waiting for transfers between devices  9.65 us (3%)
  starting transfers between devices  4.56 us (1%)
    pallas_call x3, Pallas kernels, ring_scatter(): pl.pallas_call(body, out_shape=shapes, in_specs=[vmem] * len(given), out_...  83.4 us
    pallas_call x3, Pallas kernels, ring_gather(): pl.pallas_call(body, out_shape=shapes, in_specs=[vmem] * len(given), out_...  76.4 us
    unnamed x91, local copies, waits for them, and re-layouts  23.6 us
    pallas_call x2, Pallas kernels, lag_sum(): pl.pallas_call(body, out_shape=jax.ShapeDtypeStruct((width // LANES, rows...  20 us
    pallas_call x1, Pallas kernels, exchange(): pl.pallas_call(body, out_shape=shapes, in_specs=[vmem] * count, out_specs...  8.19 us
    convert_element_type x2, other arithmetic, normalise(): (as_float * scale[:, None] * gain[None, :].astype(f32)).astype(bf16)  7.9 us
    dot_general x1, matrix products, per_device(): lax.dot_general(grad_projected, flat_second, (((1,), (1,)), ((), ())), pr...  7.89 us
    ppermute x1, waiting for transfers between devices, cross(): lax.ppermute(theirs, 'seq', [(k, k ^ 1) for k in range(lax.axis_size('seq...  6.92 us
  transfers between devices with their start and end apart: 5, of which 3 were waited for; matrix products, arithmetic and copies ran while one was open for 6% of the time, Pallas kernels for 3%

profile of v4, /device:TPU:1, one launch (start us, length us, event | category | flops | bytes accessed | tf_op | source)
XLA Modules:
  0.0 334.1 jit_solution(9280797310859775003)
XLA Ops:
  2.0 1.3 pad.16.refs_1_
  3.3 1.8 maximum_maximum_fusion.refs_0_
  5.1 32.2 %shard_map.163 = (bf16[528,4096]{1,0:T(8,128)(2,1)}, s32[2,8,128]{2,1,0:T(8,128)}) custom-call(bf16[528,256]{1,0:T(8,128)(2,1)} %maximum_maximum_fusion.refs_0_, s32[8,128]{1,0:T(8,128)} %pad.16.refs_1_), custom_call_target="tpu_custom_call" | custom-call | tf_op jit(solution)/shard_map/pallas_call | solution.py:298
  38.3 3.1 fusion.3
  41.4 8.7 %copy.38 = bf16[4096,3,256]{0,2,1:T(8,128)(2,1)} copy(bf16[4096,3,256]{2,0,1:T(8,128)(2,1)} %param.16) | data formatting | bytes 12582912 | tf_op args[4]
  50.4 4.0 %fusion.5 = bf16[512,4096]{1,0:T(8,128)(2,1)S(1)} fusion(f32[4096]{0:T(1024)S(1)} %bitcast.84, f32[512]{0:T(512)S(1)} %add_rsqrt_fusion.1, bf16[528,4096]{1,0:T(8,128)(2,1)} %get-tuple-element.20), kind=kLoop, calls=%fused_computation.9 | loop fusion | flops 8388608 | bytes 8407040 | tf_op jit(solution)/shard_map/convert_element_type | solution.py:787
  54.4 3.5 %convolution_convert_fusion.6 = bf16[512,768]{1,0:T(8,128)(2,1)S(1)} fusion(bf16[512,4096]{1,0:T(8,128)(2,1)S(1)} %fusion.5, bf16[4096,768]{0,1:T(8,128)(2,1)S(1)} %bitcast.75), kind=kOutput, calls=%fused_computation.33 | convolution fusion | flops 3221618688 | bytes 11272192 | tf_op jit(solution)/shard_map/dot_general | solution.py:853
  59.2 2.2 multiply_add_fusion
  61.6 1.3 copy-done.1
  64.4 10.0 %lag_sum.2 = f32[2,528,128]{2,1,0:T(8,128)} custom-call(f32[2,656,128]{2,1,0:T(8,128)} %pad_maximum_fusion.3.x_ref, f32[128,256]{1,0:T(8,128)} %convert_element_type.271.taps_ref), custom_call_target="tpu_custom_call" | custom-call | tf_op jit(solution)/shard_map/lag_sum/pallas_call | solution.py:637
  75.5 2.1 fusion.25.refs_0_
  77.6 27.6 %shard_map.164 = bf16[528,4096]{1,0:T(8,128)(2,1)} custom-call(bf16[528,256]{1,0:T(8,128)(2,1)} %fusion.25.refs_0_), custom_call_target="tpu_custom_call" | custom-call | tf_op jit(solution)/shard_map/pallas_call | solution.py:298
  105.2 3.1 fusion
  108.4 8.7 %copy.39 = bf16[4096,3,256]{0,2,1:T(8,128)(2,1)} copy(bf16[4096,3,256]{2,0,1:T(8,128)(2,1)} %param.17) | data formatting | bytes 12582912 | tf_op args[5]
  117.2 3.9 %fusion.2 = bf16[528,4096]{1,0:T(8,128)(2,1)S(1)} fusion(bf16[528,4096]{1,0:T(8,128)(2,1)} %shard_map.164, f32[4096]{0:T(1024)S(1)} %bitcast.83, f32[528]{0:T(1024)S(1)} %add_rsqrt_fusion), kind=kLoop, calls=%fused_computation.6 | loop fusion | flops 8650752 | bytes 8669248 | tf_op jit(solution)/shard_map/convert_element_type | solution.py:787
  121.3 3.6 %convolution_convert_fusion.5 = bf16[528,768]{1,0:T(8,128)(2,1)S(1)} fusion(bf16[528,4096]{1,0:T(8,128)(2,1)S(1)} %fusion.2, bf16[4096,768]{0,1:T(8,128)(2,1)S(1)} %bitcast.77), kind=kOutput, calls=%fused_computation.32 | convolution fusion | flops 3322294272 | bytes 11427840 | tf_op jit(solution)/shard_map/dot_general | solution.py:876
  124.9 1.3 fusion.12
  128.8 4.0 %mode_close.1 = (f32[2,16,8,256]{3,2,1,0:T(8,128)}, f32[2,16,256]{2,1,0:T(8,128)}) custom-call(f32[2,512,128]{2,1,0:T(8,128)} %pad_maximum_fusion.7.a_ref, f32[2,512,128]{2,1,0:T(8,128)} %pad_maximum_fusion.8.b_ref, f32[16,256]{1,0:T(8,128)} %rate_ref.3), custom_call_target="tpu_custom_call" | custom-call | tf_op jit(solution)/shard_map/mode_close/pallas_call | solution.py:692
  132.8 8.2 %shard_map.165 = f32[8,16,256]{2,1,0:T(8,128)} custom-call(f32[2,16,256]{2,1,0:T(8,128)} %get-tuple-element.22.refs_0_), custom_call_target="tpu_custom_call" | custom-call | tf_op jit(solution)/shard_map/pallas_call | solution.py:140
  141.1 1.6 multiply_reduce_fusion.enter_ref
  142.8 6.6 %mode_apply.1 = (f32[2,512,128]{2,1,0:T(8,128)}, f32[2,512,128]{2,1,0:T(8,128)}) custom-call(f32[2,512,128]{2,1,0:T(8,128)} %pad_maximum_fusion.7.a_ref, f32[2,512,128]{2,1,0:T(8,128)} %pad_maximum_fusion.8.b_ref, f32[16,256]{1,0:T(8,128)} %rate_ref.3, f32[16,256]{1,0:T(8,128)} %res_ref.1, f32[2,16,8,256]{3,2,1,0:T(8,128)} %get-tuple-element.21.chunk_ref, ...), custom_call_target="tpu_custom_call" | custom-call | tf_op jit(solution)/shard_map/mode_apply/pallas_call | solution.py:752
  152.7 1.3 collective-permute-start
  155.1 1.3 fusion.57
  158.6 1.8 fusion.13
  160.4 7.9 %convolution_convert_fusion.1.refs_0_ = bf16[512,4096]{1,0:T(8,128)(2,1)} fusion(bf16[512,768]{1,0:T(8,128)(2,1)S(1)} %get-tuple-element.79, bf16[4096,768]{0,1:T(8,128)(2,1)} %bitcast.76), kind=kOutput, calls=%fused_computation.11 | convolution fusion | flops 3223322624 | bytes 11272192 | tf_op jit(solution)/shard_map/dot_general | solution.py:910
  168.3 5.4 %convolution_convert_fusion.refs_2_ = bf16[4096,768]{1,0:T(8,128)(2,1)} fusion(bf16[512,768]{1,0:T(8,128)(2,1)S(1)} %get-tuple-element.79, bf16[528,4096]{1,0:T(8,128)(2,1)S(1)} %bitcast.80), kind=kOutput, calls=%fused_computation.10 | convolution fusion | flops 3224371200 | bytes 11272192 | tf_op jit(solution)/shard_map/dot_general | solution.py:913
  174.3 48.5 %shard_map.166 = (f32[512,256]{1,0:T(8,128)}, f32[8,128]{1,0:T(8,128)}, bf16[2,1024,384]{2,1,0:T(8,128)(2,1)}) custom-call(bf16[512,4096]{1,0:T(8,128)(2,1)} %convolution_convert_fusion.1.refs_0_, f32[8,128]{1,0:T(8,128)} %pad.17.refs_1_, bf16[4096,768]{1,0:T(8,128)(2,1)} %convolution_convert_fusion.refs_2_), custom_call_target="tpu_custom_call" | custom-call | tf_op jit(solution)/shard_map/pallas_call | solution.py:578
  223.5 1.4 fusion.35
  224.9 1.4 collective-permute-start.1
  226.3 2.7 slice_bitcast_fusion.1
  229.0 1.6 collective-permute-start.3
  231.8 10.0 %lag_sum.3 = f32[2,528,128]{2,1,0:T(8,128)} custom-call(f32[2,656,128]{2,1,0:T(8,128)} %pad_maximum_fusion.4.x_ref, f32[128,256]{1,0:T(8,128)} %rev.3.taps_ref), custom_call_target="tpu_custom_call" | custom-call | tf_op jit(solution)/shard_map/lag_sum/pallas_call | solution.py:637
  241.8 1.1 slice_bitcast_fusion.7
  243.8 1.4 add_convert_fusion
  245.2 1.7 convolution_convert_fusion.4.refs_0_
  247.7 2.0 collective-permute-done.2
  249.6 2.2 convert_add_fusion
  251.9 1.7 copy-done.3
  253.7 14.5 %shard_map.167 = f32[64,1024]{1,0:T(8,128)} custom-call(bf16[512,1024]{1,0:T(8,128)(2,1)} %convolution_convert_fusion.4.refs_0_), custom_call_target="tpu_custom_call" | custom-call | tf_op jit(solution)/shard_map/pallas_call | solution.py:578
  269.4 4.8 %convolution_convert_fusion.2.refs_0_ = bf16[64,4096]{1,0:T(8,128)(2,1)} fusion(bf16[64,768]{1,0:T(8,128)(2,1)S(1)} %get-tuple-element.75, bf16[4096,768]{0,1:T(8,128)(2,1)} %bitcast.74), kind=kOutput, calls=%fused_computation.12 | convolution fusion | flops 402915328 | bytes 6914048 | tf_op jit(solution)/shard_map/dot_general | solution.py:958
  274.7 20.4 %shard_map.168 = (f32[64,256]{1,0:T(8,128)}, f32[8,128]{1,0:T(8,128)}) custom-call(bf16[64,4096]{1,0:T(8,128)(2,1)} %convolution_convert_fusion.2.refs_0_, f32[8,128]{1,0:T(8,128)} %pad.19.refs_1_), custom_call_target="tpu_custom_call" | custom-call | tf_op jit(solution)/shard_map/pallas_call | solution.py:578
  297.6 16.7 %shard_map.169 = bf16[8,80,1024]{2,1,0:T(8,128)(2,1)} custom-call(bf16[80,1024]{1,0:T(8,128)(2,1)} %maximum_maximum_fusion.1.refs_0_), custom_call_target="tpu_custom_call" | custom-call | tf_op jit(solution)/shard_map/pallas_call | solution.py:298
  316.3 1.2 slice.417
  319.2 3.1 fusion.40
  322.3 6.9 %collective-permute-done.4 = bf16[512,768]{1,0:T(8,128)(2,1)S(1)} collective-permute-done((bf16[512,768]{1,0:T(8,128)(2,1)S(1)}, bf16[512,768]{1,0:T(8,128)(2,1)S(1)}, u32[]{:S(2)}, u32[]{:S(2)}) %collective-permute-start.4) | collective-permute-done | bytes 786464 | tf_op jit(solution)/shard_map/ppermute | solution.py:809
  329.3 1.3 convert_add_fusion.1
  330.6 1.9 copy.45
  332.5 1.6 copy.46
  (175 shorter events, 28.2 us)
Async XLA Ops:
  41.4 8.9 %copy-start.33 = (f32[512]{0:T(512)}, f32[512]{0:T(512)S(1)}, u32[]{:S(2)}) copy-start(f32[512]{0:T(512)S(1)} %add_rsqrt_fusion.1) | copy-start | bytes 6148
  41.4 8.7 %copy-start.34 = (s32[2,8,128]{2,1,0:T(8,128)S(1)}, s32[2,8,128]{2,1,0:T(8,128)}, u32[]{:S(2)}) copy-start(s32[2,8,128]{2,1,0:T(8,128)} %get-tuple-element.19) | copy-start | bytes 24580
  41.4 8.7 %copy-start.28 = (f32[7,3,256]{2,0,1:T(8,128)S(1)}, f32[7,3,256]{2,0,1:T(8,128)}, u32[]{:S(2)}) copy-start(f32[7,3,256]{2,0,1:T(8,128)} %param.18) | copy-start | bytes 64516
  50.3 8.8 %copy-start.22 = (f32[768]{0:T(1024)}, f32[768]{0:T(1024)S(1)}, u32[]{:S(2)}) copy-start(f32[768]{0:T(1024)S(1)} %mul.475) | copy-start | bytes 9220
  50.3 8.8 %copy-start.24 = (f32[768]{0:T(1024)}, f32[768]{0:T(1024)S(1)}, u32[]{:S(2)}) copy-start(f32[768]{0:T(1024)S(1)} %mul.472) | copy-start | bytes 9220
  50.4 4.0 %copy-start = (bf16[4096,3,256]{0,2,1:T(8,128)(2,1)S(1)}, bf16[4096,3,256]{0,2,1:T(8,128)(2,1)}, u32[]{:S(2)}) copy-start(bf16[4096,3,256]{0,2,1:T(8,128)(2,1)} %copy.38) | copy-start | bytes 18874372
  54.3 3.5 %copy-start.6 = (bf16[512,4096]{1,0:T(8,128)(2,1)}, bf16[512,4096]{1,0:T(8,128)(2,1)S(1)}, u32[]{:S(2)}) copy-start(bf16[512,4096]{1,0:T(8,128)(2,1)S(1)} %fusion.5) | copy-start | bytes 12582916
  54.4 3.6 %copy-start.35 = (s32[512]{0:T(512)S(1)}, s32[512]{0:T(512)}, u32[]{:S(2)}) copy-start(s32[512]{0:T(512)} %param.12) | copy-start | bytes 6148
  54.4 3.7 %copy-start.17 = (bf16[512,256]{1,0:T(8,128)(2,1)S(1)}, bf16[512,256]{1,0:T(8,128)(2,1)}, u32[]{:S(2)}) copy-start(bf16[512,256]{1,0:T(8,128)(2,1)} %param.13) | copy-start | bytes 786436
  57.9 1.3 copy-start.32
  58.1 1.1 copy-start.30
  61.4 1.5 copy-start.1
  61.4 1.5 copy-start.20
  75.5 29.6 %copy-start.9 = (f32[528,128]{1,0:T(8,128)}, f32[528,128]{1,0:T(8,128)S(1)}, u32[]{:S(2)}) copy-start(f32[528,128]{1,0:T(8,128)S(1)} %get-tuple-element.99) | copy-start | bytes 811012
  75.5 29.6 %copy-start.11 = (f32[528,128]{1,0:T(8,128)}, f32[528,128]{1,0:T(8,128)S(1)}, u32[]{:S(2)}) copy-start(f32[528,128]{1,0:T(8,128)S(1)} %get-tuple-element.100) | copy-start | bytes 811012
  108.3 8.9 %copy-start.26 = (f32[528]{0:T(1024)}, f32[528]{0:T(1024)S(1)}, u32[]{:S(2)}) copy-start(f32[528]{0:T(1024)S(1)} %add_rsqrt_fusion) | copy-start | bytes 6340
  108.3 8.7 %copy-start.29 = (f32[7,3,256]{2,0,1:T(8,128)S(1)}, f32[7,3,256]{2,0,1:T(8,128)}, u32[]{:S(2)}) copy-start(f32[7,3,256]{2,0,1:T(8,128)} %param.19) | copy-start | bytes 64516
  117.2 4.1 %copy-start.5 = (bf16[4096,3,256]{0,2,1:T(8,128)(2,1)S(1)}, bf16[4096,3,256]{0,2,1:T(8,128)(2,1)}, u32[]{:S(2)}) copy-start(bf16[4096,3,256]{0,2,1:T(8,128)(2,1)} %copy.39) | copy-start | bytes 18874372
  121.2 3.7 %copy-start.7 = (bf16[528,4096]{1,0:T(8,128)(2,1)}, bf16[528,4096]{1,0:T(8,128)(2,1)S(1)}, u32[]{:S(2)}) copy-start(bf16[528,4096]{1,0:T(8,128)(2,1)S(1)} %fusion.2) | copy-start | bytes 12976132
  124.9 1.3 copy-start.13
  126.4 0.7 copy-start.21
  142.8 8.8 %copy-start.8 = (bf16[528,256]{1,0:T(8,128)(2,1)S(1)}, bf16[528,256]{1,0:T(8,128)(2,1)}, u32[]{:S(2)}) copy-start(bf16[528,256]{1,0:T(8,128)(2,1)} %fusion.25.refs_0_) | copy-start | bytes 811012
  149.4 2.2 copy-start.14
  152.6 1.4 copy-start.27
  152.6 1.5 copy-start.31
  152.6 3.8 %copy-start.40 = (bf16[256]{0:T(256)(128)(2,1)S(1)}, bf16[256]{0:T(256)(128)(2,1)}, u32[]{:S(2)}) copy-start(bf16[256]{0:T(256)(128)(2,1)} %param.15) | copy-start | bytes 1540
  152.6 4.7 %copy-start.41 = (bf16[256]{0:T(256)(128)(2,1)S(1)}, bf16[256]{0:T(256)(128)(2,1)}, u32[]{:S(2)}) copy-start(bf16[256]{0:T(256)(128)(2,1)} %param.14) | copy-start | bytes 1540
  152.7 5.9 %collective-permute-start = (bf16[8,768]{1,0:T(8,128)(2,1)S(1)}, bf16[8,768]{1,0:T(8,128)(2,1)S(1)}, u32[]{:S(2)}, u32[]{:S(2)}) collective-permute-start(bf16[8,768]{1,0:T(8,128)(2,1)S(1)} %slice.449), channel_id=1, source_target_pairs={{16,0},{32,16},{48,32},{64,48},{80,64},{96,80},{112,96},{17,1},{33... | collective-permute-start | bytes 36872 | tf_op jit(solution)/shard_map/ppermute | solution.py:764
  158.6 9.7 %slice-start = ((s8[4325376]{0:T(1024)(128)(4,1)}), s8[4194304]{0:T(1024)(128)(4,1)S(1)}, s32[]{:S(2)}) async-start(s8[4325376]{0:T(1024)(128)(4,1)} %bitcast.79), calls=%async_computation | async-start | bytes 8388608
  160.4 7.9 %slice-start.1 = ((s8[4325376]{0:T(1024)(128)(4,1)}), s8[131072]{0:T(1024)(128)(4,1)S(1)}, s32[]{:S(2)}) async-start(s8[4325376]{0:T(1024)(128)(4,1)} %bitcast.79), calls=%async_computation.1 | async-start | bytes 262144
  174.3 49.2 %copy-start.15 = (bf16[512,256]{1,0:T(8,128)(2,1)S(1)}, bf16[512,256]{1,0:T(8,128)(2,1)}, u32[]{:S(2)}) copy-start(bf16[512,256]{1,0:T(8,128)(2,1)} %param.23) | copy-start | bytes 786436
  224.9 5.9 %copy-start.2 = (f32[792,768]{1,0:T(8,128)S(1)}, f32[792,768]{1,0:T(8,128)}, u32[]{:S(2)}) copy-start(f32[792,768]{1,0:T(8,128)} %copy-done.1) | copy-start | bytes 7299076
  224.9 5.9 %collective-permute-start.1 = (bf16[144,256]{1,0:T(8,128)(2,1)S(1)}, bf16[144,256]{1,0:T(8,128)(2,1)S(1)}, u32[]{:S(2)}, u32[]{:S(2)}) collective-permute-start(bf16[144,256]{1,0:T(8,128)(2,1)S(1)} %slice.457), channel_id=1, source_target_pairs={{16,0},{32,16},{48,32},{64,48},{80,64},{96,80},{112,96},{17,1},{33... | collective-permute-start | bytes 221192 | tf_op jit(solution)/shard_map/ppermute | solution.py:764
  229.0 18.7 %collective-permute-start.3 = (bf16[1024,384]{1,0:T(8,128)(2,1)}, bf16[1024,384]{1,0:T(8,128)(2,1)}, u32[]{:S(2)}, u32[]{:S(2)}) collective-permute-start(bf16[1024,384]{1,0:T(8,128)(2,1)} %get-tuple-element.87), channel_id=1, source_target_pairs={{0,96},{16,112},{32,0},{48,16},{64,32},{80,48},{96,64},{112,80},{1... | collective-permute-start | bytes 2359304 | tf_op jit(solution)/shard_map/ppermute | solution.py:796
  230.6 19.1 %collective-permute-start.2 = (bf16[1024,384]{1,0:T(8,128)(2,1)}, bf16[1024,384]{1,0:T(8,128)(2,1)}, u32[]{:S(2)}, u32[]{:S(2)}) collective-permute-start(bf16[1024,384]{1,0:T(8,128)(2,1)} %get-tuple-element.86), channel_id=1, source_target_pairs={{0,32},{16,48},{32,64},{48,80},{64,96},{80,112},{96,0},{112,16},{1... | collective-permute-start | bytes 2359304 | tf_op jit(solution)/shard_map/ppermute | solution.py:796
  230.8 1.0 copy-start.18
  241.8 1.3 copy-start.10
  241.8 1.3 copy-start.12
  241.8 1.3 copy-start.19
  243.1 0.7 copy-start.25
  243.8 1.4 copy-start.16
  251.9 1.7 copy-start.3
  269.3 26.5 %copy-start.36 = (f32[64]{0:T(128)S(1)}, f32[64]{0:T(128)}, u32[]{:S(2)}) copy-start(f32[64]{0:T(128)} %get-tuple-element.70) | copy-start | bytes 772
  269.3 26.5 %copy-start.37 = (f32[64]{0:T(128)S(1)}, f32[64]{0:T(128)}, u32[]{:S(2)}) copy-start(f32[64]{0:T(128)} %get-tuple-element.71) | copy-start | bytes 772
  269.3 26.5 %copy-start.38 = (f32[256]{0:T(256)S(1)}, f32[256]{0:T(256)}, u32[]{:S(2)}) copy-start(f32[256]{0:T(256)} %convert_element_type.323) | copy-start | bytes 3076
  269.3 27.5 %copy-start.39 = (bf16[80]{0:T(256)(128)(2,1)S(1)}, bf16[80]{0:T(256)(128)(2,1)}, u32[]{:S(2)}) copy-start(bf16[80]{0:T(256)(128)(2,1)} %pad.23.clone) | copy-start | bytes 484
  314.3 15.0 %collective-permute-start.4 = (bf16[512,768]{1,0:T(8,128)(2,1)S(1)}, bf16[512,768]{1,0:T(8,128)(2,1)S(1)}, u32[]{:S(2)}, u32[]{:S(2)}) collective-permute-start(bf16[512,768]{1,0:T(8,128)(2,1)S(1)} %dynamic-slice_convert_fusion), channel_id=1, source_target_pairs={{0,16},{16,0},{32,48},{48,32},{64,80},{80,64},{96,112},{112,96},{1... | collective-permute-start | bytes 2359304 | tf_op jit(solution)/shard_map/ppermute | solution.py:809
  318.4 10.9 %copy-start.4 = (f32[1024,768]{1,0:T(8,128)S(1)}, f32[1024,768]{1,0:T(8,128)}, u32[]{:S(2)}) copy-start(f32[1024,768]{1,0:T(8,128)} %copy-done.3) | copy-start | bytes 9437188
  (1 other events, 0.7 us)
